TPU v7x, 32 devices: a whole 2x2x4 slice. The times are simulated.
32 devices in a mesh: ctx: 8 (over z, x), exp: 4 (over y, core).
Axes of the slice: x: 2, y: 2, z: 4, core: 2. Of those that a mesh axis runs over, the one named last changes fastest.
Arguments:
- q_spikes: bfloat16 [4096, 4096], P('ctx', 'exp'), may hold values from -1 to 1, as said below
- k_spikes: bfloat16 [4096, 4096], P('ctx', 'exp'), may hold values from -1 to 1, as said below
- v_spikes: bfloat16 [4096, 4096], P('ctx', 'exp'), may hold values from -1 to 1, as said below
- log_decay: float32 [4096, 32], P('ctx', 'exp'), may hold values from -1 to 0, as said below
- norm_gain: float32 [4096], P('exp'), may hold values from 0.1 to 1.9
- out_weight: bfloat16 [4096, 4096], P('exp'), may hold values from -0.09375 to 0.09375
- residual: bfloat16 [4096, 4096], P(('ctx', 'exp')), may hold values from -6 to 6
Outputs:
- mixed: bfloat16 [4096, 4096], P(('ctx', 'exp'))
Inputs may be any that keep to these rules, and one draw needn't show every extreme that they name: `q_spikes`: every entry is -1, 0 or 1. `k_spikes`: every entry is -1, 0 or 1. `v_spikes`: every entry is -1, 0 or 1. `log_decay`: every entry is negative.
All inputs are finite; a program needn't handle non-finite values.
Results may differ from a plain program's by a relative error of at most 0.015.
Values may be sent and summed in bfloat16 or wider, within the bound.
No kernel may reach another device: no remote copies, remote signals or barrier semaphores. Data moves between devices by JAX's collectives and lax.ppermute only.
A program may use at most 64 MiB of HBM per device.

v0:
```python
import functools

import jax
import jax.numpy as jnp
from jax import lax
from jax.experimental import pallas as pl
from jax.experimental.pallas import tpu as pltpu
from jax.sharding import PartitionSpec as P


F32 = jnp.float32
BF16 = jnp.bfloat16
PARAMS = pltpu.CompilerParams(vmem_limit_bytes=16 << 20)
PACKED = pltpu.CompilerParams(vmem_limit_bytes=16 << 20)
VMEM = pl.BlockSpec(memory_space=pltpu.VMEM)
SMEM = pl.BlockSpec(memory_space=pltpu.SMEM)
ANY = pl.BlockSpec(memory_space=pl.ANY)


def held(shape, kind):
    return pltpu.VMEM(shape, kind)


def near(x):
    return pltpu.with_memory_space_constraint(x, pltpu.VMEM)


def outside(x):
    return pltpu.with_memory_space_constraint(x, pltpu.HBM)


def tile_of(size, want):
    while size % want:
        want //= 2
    return want


def pad_rows(count):
    return -(-count // 8) * 8


def running_sum(logd):
    heads, rows = logd.shape
    tile = tile_of(rows, 128)
    count = rows // tile
    tiles = jnp.concatenate([logd[:, i * tile : (i + 1) * tile] for i in range(count)], axis=0)
    one = tiles.astype(BF16).astype(F32)
    two = (tiles - one).astype(BF16).astype(F32)
    three = tiles - one - two
    parts = jnp.concatenate([one, two, three], axis=0).astype(BF16)
    upper = (
        lax.broadcasted_iota(jnp.int32, (tile, tile), 0)
        <= lax.broadcasted_iota(jnp.int32, (tile, tile), 1)
    ).astype(F32)
    sums = jnp.dot(parts, upper.astype(BF16), preferred_element_type=F32)
    size = count * heads
    sums = sums[:size] + sums[size : 2 * size] + sums[2 * size :]
    done, carry = [], None
    for i in range(count):
        part = sums[i * heads : (i + 1) * heads]
        if carry is not None:
            part = part + carry
        carry = part[:, tile - 1 : tile]
        done.append(part)
    return jnp.concatenate(done, axis=1)


def copies_of(source, target, sems, first=0):
    count = sems.shape[0]
    size = target.shape[0] // count
    return [
        pltpu.make_async_copy(
            source.at[pl.ds(i * size, size), pl.ds(first, target.shape[1])],
            target.at[pl.ds(i * size, size), :],
            sems.at[i],
        )
        for i in range(count)
    ]


def pay_shape(count, width, kind):
    return held((count * width + 2 * pad_rows(count), width), kind)


def part_of(place_ref, size, away):
    return (place_ref[0] & (size - 1)) ^ away


def put_states(part, count, width, key, value, weight_ref, cum_ref, pay_ref):
    rows = cum_ref.shape[1]
    turned = [key[:, j * width : (j + 1) * width].T for j in range(count)]
    decays = []
    for j in range(count):
        head = pl.ds(part * count + j, 1)
        keyed = turned[j] * weight_ref[head, :].astype(BF16)
        state = jnp.dot(keyed, value[:, j * width : (j + 1) * width], preferred_element_type=F32)
        pay_ref[j * width : (j + 1) * width, :] = state.astype(pay_ref.dtype)
        total = cum_ref[head, :][:, rows - 1 : rows]
        decays.append(jnp.broadcast_to(jnp.exp(total), (1, width)))
    put_decays(pay_ref, decays, count, width)


def put_sums(logd_ref, cum_ref, weight_ref):
    cum = running_sum(logd_ref[...])
    cum_ref[...] = cum
    weight_ref[...] = jnp.exp(cum[:, cum.shape[1] - 1 :] - cum)


def early_kernel(size, count, width, place_ref, logd_in, key_in, value_in, *refs):
    pay_refs = refs[: size - 1]
    key_ref, value_ref, logd_ref, cum_ref, weight_ref, logd_sem, sems = refs[size - 1 :]
    cols = count * width
    logd = pltpu.make_async_copy(logd_in, logd_ref, logd_sem)
    logd.start()
    copies = []
    for away in range(1, size):
        part = part_of(place_ref, size, away)
        first = pl.multiple_of(part * cols, cols)
        here = pl.ds((away - 1) * cols, cols)
        copies.append(
            copies_of(key_in, key_ref.at[:, here], sems.at[0, away - 1], first)
            + copies_of(value_in, value_ref.at[:, here], sems.at[1, away - 1], first)
        )
        for copy in copies[-1]:
            copy.start()
    logd.wait()
    put_sums(logd_ref, cum_ref, weight_ref)
    for away in range(1, size):
        for copy in copies[away - 1]:
            copy.wait()
        here = slice((away - 1) * cols, away * cols)
        put_states(
            part_of(place_ref, size, away), count, width, key_ref[:, here], value_ref[:, here],
            weight_ref, cum_ref, pay_refs[away - 1],
        )


def early_states(place, logd, key, value, size, count, width):
    heads, rows = logd.shape
    cols = (size - 1) * count * width
    *pays, key, value = pl.pallas_call(
        functools.partial(early_kernel, size, count, width),
        in_specs=[SMEM] + [ANY] * 3,
        out_specs=[VMEM] * (size + 1),
        out_shape=[pay_shape(count, width, BF16)] * (size - 1) + [held((rows, cols), BF16)] * 2,
        scratch_shapes=[pltpu.VMEM((heads, rows), F32)] * 3
        + [pltpu.SemaphoreType.DMA, pltpu.SemaphoreType.DMA((2, size - 1, 4))],
        compiler_params=PACKED,
        name="early_states",
    )(place, outside(logd), outside(key), outside(value))
    return pays, key, value


def load_kernel(size, count, width, place_ref, logd_in, key_in, value_in, query_in, hold_ref, *refs):
    pay_ref, key_ref, value_ref, query_ref, cum_ref, logd_ref, weight_ref, logd_sem, sems = refs
    cols = count * width
    logd = pltpu.make_async_copy(logd_in, logd_ref, logd_sem)
    logd.start()
    first = pl.multiple_of(part_of(place_ref, size, 0) * cols, cols)
    copies = copies_of(key_in, key_ref, sems.at[0], first)
    copies += copies_of(value_in, value_ref, sems.at[1], first)
    last = []
    for away in range(size):
        start = pl.multiple_of(part_of(place_ref, size, away) * cols, cols)
        target = query_ref.at[:, pl.ds(away * cols, cols)]
        last += copies_of(query_in, target, sems.at[2 + away], start)
    for copy in copies + last:
        copy.start()
    logd.wait()
    put_sums(logd_ref, cum_ref, weight_ref)
    for copy in copies:
        copy.wait()
    put_states(
        part_of(place_ref, size, 0), count, width, key_ref[...], value_ref[...], weight_ref, cum_ref, pay_ref
    )
    for copy in last:
        copy.wait()


def load(place, logd, key, value, query, hold, size, count, width):
    heads, rows = logd.shape
    return pl.pallas_call(
        functools.partial(load_kernel, size, count, width),
        in_specs=[SMEM] + [ANY] * 5,
        out_specs=[VMEM] * 5,
        out_shape=[
            pay_shape(count, width, F32),
            held((rows, count * width), BF16),
            held((rows, count * width), BF16),
            held(query.shape, BF16),
            held((heads, rows), F32),
        ],
        scratch_shapes=[pltpu.VMEM((heads, rows), F32)] * 2
        + [pltpu.SemaphoreType.DMA, pltpu.SemaphoreType.DMA((2 + size, 4))],
        compiler_params=PACKED,
        name="load",
    )(place, outside(logd), outside(key), outside(value), outside(query), hold)


def decay_row(pay, j, count, width):
    at = count * width + j
    pad = pad_rows(count)
    return pay[at : at + 1, :].astype(F32) + pay[at + pad : at + pad + 1, :].astype(F32)


def put_decays(ref, rows, count, width):
    pad = pad_rows(count)
    blank = [jnp.zeros((1, width), F32)] * (pad - count)
    if ref.dtype == BF16:
        highs = [row.astype(BF16).astype(F32) for row in rows]
        lows = [row - high for row, high in zip(rows, highs)]
    else:
        highs, lows = rows, [jnp.zeros_like(row) for row in rows]
    tail = jnp.concatenate(highs + blank + lows + blank, axis=0)
    ref[count * width :, :] = tail.astype(ref.dtype)


def picked(values, index):
    found = values[0]
    for i in range(1, len(values)):
        found = jnp.where(index == i, values[i], found)
    return found


def gather_kernel(size, count, width, place_ref, *refs):
    in_refs, pay_ref, window_ref, past_refs = refs[:size], refs[size], refs[size + 1], refs[size + 2 :]
    decays = [[] for _ in range(size)]
    for j in range(count):
        rows = slice(j * width, (j + 1) * width)
        found = [ref[rows, :].astype(F32) for ref in in_refs]
        found_decays = [decay_row(ref, j, count, width) for ref in in_refs]
        total, total_decay = None, None
        for b in range(size):
            index = part_of(place_ref, size, b)
            state, decay = picked(found, index), picked(found_decays, index)
            if b:
                past_refs[b - 1][rows, :] = total
                decays[b - 1].append(total_decay)
                total, total_decay = total * decay + state, total_decay * decay
            else:
                total, total_decay = state, decay
        window_ref[rows, :] = total
        pay_ref[rows, :] = total.astype(pay_ref.dtype)
        decays[-1].append(total_decay)
    for ref, rows in zip(past_refs, decays):
        put_decays(ref, rows, count, width)
    put_decays(window_ref, decays[-1], count, width)
    put_decays(pay_ref, decays[-1], count, width)


def gather(place, own, met, size, count, width):
    shape = own.shape
    pay, window, *past = pl.pallas_call(
        functools.partial(gather_kernel, size, count, width),
        in_specs=[SMEM] + [VMEM] * size,
        out_specs=[VMEM] * (size + 1),
        out_shape=[held(shape, BF16)] + [held(shape, F32)] * size,
        compiler_params=PARAMS,
        name="gather",
    )(place, near(own), *map(near, met))
    return pay, window, past


def widen_kernel(count, width, bit, opening, keep, place_ref, got_ref, window_ref, before_ref, pay_ref, past_ref, *refs):
    is_later = (place_ref[0] & bit) != 0
    decays, pasts = [], []
    for j in range(count):
        rows = slice(j * width, (j + 1) * width)
        got, window = got_ref[rows, :].astype(F32), window_ref[rows, :]
        got_decay = decay_row(got_ref, j, count, width)
        window_decay = decay_row(window_ref, j, count, width)
        wide = jnp.where(is_later, got, window) * jnp.where(
            is_later, window_decay, got_decay
        ) + jnp.where(is_later, window, got)
        pay_ref[rows, :] = wide.astype(pay_ref.dtype)
        if keep:
            refs[0][rows, :] = wide
        decays.append(got_decay * window_decay)
        if opening:
            past_ref[rows, :] = jnp.where(is_later, got, jnp.zeros_like(got))
            pasts.append(jnp.where(is_later, got_decay, jnp.ones_like(got_decay)))
        else:
            before = before_ref[rows, :]
            before_decay = decay_row(before_ref, j, count, width)
            past_ref[rows, :] = jnp.where(is_later, got * before_decay + before, before)
            pasts.append(jnp.where(is_later, got_decay * before_decay, before_decay))
    put_decays(pay_ref, decays, count, width)
    if keep:
        put_decays(refs[0], decays, count, width)
    put_decays(past_ref, pasts, count, width)


def widen(place, got, window, before, count, width, bit, keep):
    shape = got.shape
    opening = before is None
    before = window if before is None else before
    done = pl.pallas_call(
        functools.partial(widen_kernel, count, width, bit, opening, keep),
        in_specs=[SMEM, VMEM, VMEM, VMEM],
        out_specs=[VMEM] * (2 + keep),
        out_shape=[held(shape, BF16), held(shape, F32)] + [held(shape, F32)] * keep,
        compiler_params=PARAMS,
        name="widen",
    )(place, near(got), near(window), near(before))
    return done if keep else (*done, None)


def enter_kernel(size, count, width, bit, opening, place_ref, got_ref, before_ref, *refs):
    past_refs, out_refs = refs[: size - 1], refs[size - 1 :]
    is_later = (place_ref[0] & bit) != 0
    for j in range(count):
        rows = slice(j * width, (j + 1) * width)
        before = jnp.zeros((width, width), F32)
        if bit:
            got = got_ref[rows, :].astype(F32)
            if not opening:
                before = before_ref[rows, :]
                got = got * decay_row(before_ref, j, count, width) + before
            before = jnp.where(is_later, got, before)
        entering = [before] + [
            before * decay_row(ref, j, count, width) + ref[rows, :] for ref in past_refs
        ]
        for away in range(size):
            index = part_of(place_ref, size, away)
            out_refs[away][rows, :] = picked(entering, index).astype(BF16)


def enter(place, got, before, past, size, count, width, bit):
    opening = before is None
    got = past[0] if got is None else got
    before = past[0] if opening else before
    return pl.pallas_call(
        functools.partial(enter_kernel, size, count, width, bit, opening),
        in_specs=[SMEM] + [VMEM] * (size + 1),
        out_specs=[VMEM] * size,
        out_shape=[held((count * width, width), BF16)] * size,
        compiler_params=PARAMS,
        name="enter",
    )(place, near(got), near(before), *map(near, past))


def local_kernel(size, count, width, away, place_ref, cum_ref, q_ref, k_ref, v_ref, out_ref, decayed_ref):
    from_q, from_kv = away * count, max(away - 1, 0) * count
    sums = [
        cum_ref[pl.ds(part_of(place_ref, size, away) * count + j, 1), :] for j in range(count)
    ]
    rows = cum_ref.shape[1]
    tile = tile_of(rows, 2 * width)
    causal = lax.broadcasted_iota(jnp.int32, (tile, tile), 0) >= lax.broadcasted_iota(
        jnp.int32, (tile, tile), 1
    )

    def downward(row):
        turned = jnp.broadcast_to(row, (width, tile)).T
        return jnp.concatenate([turned] * (tile // width), axis=1)

    def columns(start, j):
        return slice((start + j) * width, (start + j + 1) * width)

    def scores(j, i):
        return lax.dot_general(
            q_ref[i * tile : (i + 1) * tile, columns(from_q, j)],
            k_ref[: (i + 1) * tile, columns(from_kv, j)],
            (((1,), (1,)), ((), ())),
            preferred_element_type=F32,
        )

    def weighted(j, i, found):
        cum = sums[j]
        here = slice(i * tile, (i + 1) * tile)
        across = cum[:, here]
        down = downward(across)
        weight = jnp.exp(jnp.where(causal, down - across, -jnp.inf))
        near_part = (found[:, i * tile :] * weight).astype(BF16)
        if i == 0:
            return near_part, None, None, jnp.exp(down)
        edge = cum[:, i * tile - 1 : i * tile]
        since = jnp.exp(down - edge)
        far_part = (found[:, : i * tile] * jnp.exp(edge - cum[:, : i * tile])).astype(BF16)
        return near_part, far_part, since, since * jnp.exp(edge)

    def finish(j, i, near_part, far_part, since, decay):
        cols = slice(j * width, (j + 1) * width)
        from_cols = columns(from_kv, j)
        here = slice(i * tile, (i + 1) * tile)
        out = jnp.dot(near_part, v_ref[here, from_cols], preferred_element_type=F32)
        if far_part is not None:
            out = out + since[:, :width] * jnp.dot(
                far_part, v_ref[: i * tile, from_cols], preferred_element_type=F32
            )
        out_ref[here, cols] = out
        decayed_ref[here, cols] = (
            q_ref[here, columns(from_q, j)].astype(F32) * decay[:, :width]
        ).astype(BF16)

    units = [(j, i) for i in range(rows // tile) for j in range(count)]
    found, held_parts = {}, {}
    for step in range(len(units) + 3):
        if step < len(units):
            found[step] = scores(*units[step])
        if 0 <= step - 2 < len(units):
            held_parts[step - 2] = weighted(*units[step - 2], found.pop(step - 2))
        if 0 <= step - 3:
            finish(*units[step - 3], *held_parts.pop(step - 3))


def local(place, cum, query, key, value, size, count, width, away):
    rows = cum.shape[1]
    cols = count * width
    return pl.pallas_call(
        functools.partial(local_kernel, size, count, width, away),
        in_specs=[SMEM] + [VMEM] * 4,
        out_specs=[VMEM, VMEM],
        out_shape=[held((rows, cols), F32), held((rows, cols), BF16)],
        compiler_params=PARAMS,
        name="local",
    )(place, near(cum), near(query), near(key), near(value))


def norm_kernel(size, count, width, chips, block, away, group, place_ref, chip_ref, core_ref, gain_ref, *refs):
    members = len(group)
    inside_refs, query_refs = refs[:members], refs[members : 2 * members]
    state_refs, out_ref = refs[2 * members : -1], refs[-1]
    ones = jnp.full((width, width), 1.0 / width, F32).astype(BF16)
    units = [(at, j) for at in range(members) for j in range(count)]

    def rows_of(ref, j):
        src = slice(j * width, (j + 1) * width)
        found = []
        for i in range(chips):
            spot = 2 * lax.rem(chip_ref[0] + i, chips)
            spot = spot + (1 - core_ref[0] if away else core_ref[0])
            found.append(ref[pl.ds(pl.multiple_of(spot * block, block), block), src])
        return jnp.concatenate(found, axis=0)

    def carry(at, j):
        state = state_refs[at][j * width : (j + 1) * width, :]
        return jnp.dot(rows_of(query_refs[at], j), state, preferred_element_type=F32)

    def square(at, j, carried):
        attended = rows_of(inside_refs[at], j) + carried
        return attended, jnp.dot(
            (attended * attended).astype(BF16), ones, preferred_element_type=F32
        )

    def finish_head(at, j, attended, mean):
        gain = gain_ref[pl.ds(part_of(place_ref, size, group[at]) * count + j, 1), :]
        col = (at * count + j) * width
        out_ref[:, col : col + width] = (
            attended * lax.rsqrt(mean + 1e-06) * gain
        ).astype(out_ref.dtype)

    first, second = {}, {}
    for step in range(len(units) + 2):
        if step < len(units):
            first[step] = carry(*units[step])
        if 0 <= step - 1 < len(units):
            second[step - 1] = square(*units[step - 1], first.pop(step - 1))
        if 0 <= step - 2:
            finish_head(*units[step - 2], *second.pop(step - 2))


def norm(group, scalars, gain, insides, queries, entering, size, count, width, chips, block, away):
    cols = len(group) * count * width
    parts = [a[i] for a in (insides, queries, entering) for i in group]
    return pl.pallas_call(
        functools.partial(norm_kernel, size, count, width, chips, block, away, group),
        in_specs=[SMEM] * 3 + [VMEM] * (1 + len(parts)),
        out_specs=VMEM,
        out_shape=held((chips * block, cols), BF16),
        compiler_params=PARAMS,
        name="norm_away" if away else "norm_home",
    )(*scalars, gain, *map(near, parts))


def project_kernel(block, first, tile, size, place_ref, *refs):
    own_ref, away_ref = refs[-2:]
    sides = [(refs[0], refs[1], refs[4]), (refs[2], refs[3], refs[5])]
    cols = refs[1].shape[1]
    for i in range(own_ref.shape[1] // tile):
        here = slice(i * tile, (i + 1) * tile)
        span = slice(first + i * tile, first + (i + 1) * tile)
        total = None
        for one_ref, two_ref, weight_ref in sides:
            for away in range(size):
                last = away == size - 1
                normed = two_ref[...] if last else one_ref[:, away * cols : (away + 1) * cols]
                start = pl.multiple_of(part_of(place_ref, size, away) * cols, cols)
                part = jnp.dot(
                    normed, weight_ref[pl.ds(start, cols), span], preferred_element_type=F32
                )
                total = part if total is None else total + part
        own_ref[:, here] = total[:block]
        away_ref[:, here] = total[block:].astype(away_ref.dtype)


def project(place, home, other, first_weight, second_weight, hold, block, first, count, tile, size):
    rows = home[0].shape[0]
    tile = tile_of(count, tile)
    return pl.pallas_call(
        functools.partial(project_kernel, block, first, tile, size),
        in_specs=[SMEM] + [VMEM] * 6 + [ANY],
        out_specs=[VMEM, VMEM],
        out_shape=[held((block, count), F32), held((rows - block, count), BF16)],
        compiler_params=PARAMS,
        name="project",
    )(place, *map(near, [*home, *other, first_weight, second_weight]), hold)


def finish_kernel(first, pieces, own_ref, residual_ref, *refs):
    part_refs, (out_ref, total_ref, sems) = refs[:pieces], refs[-3:]
    count = own_ref.shape[1]
    total = own_ref[...] + residual_ref[:, first : first + count].astype(F32)
    for ref in part_refs:
        total = total + ref[...].astype(F32)
    total_ref[...] = total.astype(BF16)
    rows = total_ref.shape[0] // sems.shape[0]
    copies = []
    for i in range(sems.shape[0]):
        here = pl.ds(i * rows, rows)
        copies.append(
            pltpu.make_async_copy(
                total_ref.at[here, :], out_ref.at[here, pl.ds(first, count)], sems.at[i]
            )
        )
    for copy in copies:
        copy.start()
    for copy in copies:
        copy.wait()


def finish(out, own, residual, parts, first):
    block, total = residual.shape
    earlier = [] if out is None else [outside(out)]
    return pl.pallas_call(
        functools.partial(finish_kernel, first, len(parts)),
        in_specs=[VMEM] * (2 + len(parts)) + [ANY] * len(earlier),
        out_specs=ANY,
        out_shape=pltpu.HBM((block, total), BF16),
        scratch_shapes=[
            pltpu.VMEM((block, own.shape[1]), BF16),
            pltpu.SemaphoreType.DMA((tile_of(block // 16, 4),)),
        ],
        input_output_aliases={2 + len(parts): 0} if earlier else {},
        compiler_params=PARAMS,
        name="finish",
    )(near(own), near(residual), *map(near, parts), *earlier)


def shards(blocks, group, q_spikes, k_spikes, v_spikes, log_decay, norm_gain, out_weight, residual):
    rows, heads = log_decay.shape
    width = q_spikes.shape[1] // heads
    size = 4 if heads % 4 == 0 and blocks % 4 == 0 else 2
    count = heads // size
    chips = group // 2
    block = rows // group
    place = lax.axis_index("ctx").astype(jnp.int32)
    member = lax.axis_index("exp").astype(jnp.int32)
    place, chip, core = lax.optimization_barrier(
        tuple(a.reshape(1) for a in (place, member >> 1, member & 1))
    )
    cores = [(i, i ^ 1) for i in range(group)]

    def swap(x, bit):
        return lax.ppermute(x, "ctx", [(i, i ^ bit) for i in range(blocks)])

    logd = log_decay.T
    if heads % 8:
        logd = jnp.pad(logd, ((0, pad_rows(heads) - heads), (0, 0)))
    sent, keys, values = early_states(place, logd, k_spikes, v_spikes, size, count, width)
    met = [swap(a, i + 1) for i, a in enumerate(sent)]
    kept, key, value, query, cum = load(
        place, logd, k_spikes, v_spikes, q_spikes, sent[0], size, count, width
    )
    kept, weight = lax.optimization_barrier((kept, out_weight))
    far_weight = lax.ppermute(outside(weight), "exp", cores)
    total = out_weight.shape[1]
    tile = tile_of(total, 512)

    pay, window, past = gather(place, kept, met, size, count, width)
    _, own_weight = lax.optimization_barrier((pay, out_weight))
    before, got, level, bit = None, None, 0, size
    while bit < blocks:
        got = swap(pay, bit)
        if 2 * bit < blocks:
            pay, before, window = widen(
                place, got, window, before, count, width, bit, int(4 * bit < blocks)
            )
        bit, level = 2 * bit, level + 1
    own, *theirs = enter(place, got, before, past, size, count, width, bit // 2 if level else 0)
    entering = [own] + [swap(a, i + 1) for i, a in enumerate(theirs)]

    insides, queries = [], []
    for away in range(size):
        inside, decayed = local(
            place, cum, query, keys if away else key, values if away else value,
            size, count, width, away,
        )
        insides.append(inside)
        queries.append(decayed)

    gain = norm_gain.reshape(heads, width)
    home, other = [], []
    for which in (range(size - 1), range(size - 1, size)):
        args = (
            tuple(which), (place, chip, core), gain, insides, queries, entering,
            size, count, width, chips, block,
        )
        away = norm(*args, True)
        other.append(lax.ppermute(away, "exp", cores))
        home.append(norm(*args, False))

    sizes = [tile, tile]
    while total - sum(sizes) > 2 * tile:
        sizes.append(2 * tile)
    rest = total - sum(sizes)
    sizes += [rest - tile // 2, tile // 2] if rest > tile // 2 else [rest]
    out, at, hold = None, 0, home[1]
    sums = []
    for span in sizes:
        own, pieces = project(place, home, other, own_weight, far_weight, hold, block, at, span, tile, size)
        hold = pieces
        got = []
        for d in range(1, chips):
            piece = pieces[(d - 1) * block : d * block]
            perm = [(i, 2 * ((i // 2 + d) % chips) + i % 2) for i in range(group)]
            got.append(lax.ppermute(piece, "exp", perm))
        sums.append((own, got, at))
        at += span
    for own, got, at in sums:
        out = finish(out, own, residual, got, at)
    return out


def solution(mesh):
    in_specs = (
        P("ctx", "exp"),
        P("ctx", "exp"),
        P("ctx", "exp"),
        P("ctx", "exp"),
        P("exp"),
        P("exp", None),
        P(("ctx", "exp"), None),
    )
    out_specs = P(("ctx", "exp"), None)

    def body(*args):
        return shards(mesh.shape["ctx"], mesh.shape["exp"], *args)

    return jax.shard_map(
        body, mesh=mesh, in_specs=in_specs, out_specs=out_specs, check_vma=False
    )
```

profile of v0, /device:TPU:0, one launch (start us, length us, event | category | flops | bytes accessed | tf_op | source)
XLA Modules:
  0.0 66.1 jit_solution(13300296524598622929)
XLA Ops:
  0.0 2.8 %early_states.1 = (bf16[272,128]{1,0:T(8,128)(2,1)S(1)}, bf16[272,128]{1,0:T(8,128)(2,1)S(1)}, bf16[272,128]{1,0:T(8,128)(2,1)S(1)}, bf16[512,768]{1,0:T(8,128)(2,1)S(1)}, bf16[512,768]{1,0:T(8,128)(2,1)S(1)}) custom-call(s32[1]{0:T(128)} %bitcast.place_ref, f32[8,512]{1,0:T(8,128)} %bitcast.11, bf16[512,1024]{1,0:T(8,128)(2,1)} %key_in.3, ...), custom_call_target="tpu_custom_call" | custom-call | tf_op jit(solution)/shard_map/early_states/pallas_call | solution.py:141
  2.8 2.2 %load.1 = (f32[272,128]{1,0:T(8,128)S(1)}, bf16[512,256]{1,0:T(8,128)(2,1)S(1)}, bf16[512,256]{1,0:T(8,128)(2,1)S(1)}, bf16[512,1024]{1,0:T(8,128)(2,1)S(1)}, f32[8,512]{1,0:T(8,128)S(1)}) custom-call(s32[1]{0:T(128)} %bitcast.place_ref, f32[8,512]{1,0:T(8,128)} %bitcast.12, bf16[512,1024]{1,0:T(8,128)(2,1)} %key_in.3, bf16[512,1024]{1,0:T(8,128)(2,1)} %value_in.3, ...), custom_call_target="tpu_custom_call" | custom-call | tf_op jit(solution)/shard_map/load/pallas_call | solution.py:182
  5.1 0.6 collective-permute-start.9
  5.6 2.6 %collective-permute-start.1 = (bf16[272,128]{1,0:T(8,128)(2,1)S(1)}, bf16[272,128]{1,0:T(8,128)(2,1)S(1)}, u32[]{:S(2)}, u32[]{:S(2)}) collective-permute-start(bf16[272,128]{1,0:T(8,128)(2,1)S(1)} %get-tuple-element.67), channel_id=1, source_target_pairs={{0,8},{4,12},{8,0},{12,4},{16,24},{20,28},{24,16},{28,20},{1,9},{5... | collective-permute-start | bytes 208904 | tf_op jit(solution)/shard_map/ppermute | solution.py:565
  8.3 1.4 %collective-permute-start.2 = (bf16[272,128]{1,0:T(8,128)(2,1)S(1)}, bf16[272,128]{1,0:T(8,128)(2,1)S(1)}, u32[]{:S(2)}, u32[]{:S(2)}) collective-permute-start(bf16[272,128]{1,0:T(8,128)(2,1)S(1)} %get-tuple-element.68), channel_id=1, source_target_pairs={{0,12},{4,8},{8,4},{12,0},{16,28},{20,24},{24,20},{28,16},{1,13},{... | collective-permute-start | bytes 208904 | tf_op jit(solution)/shard_map/ppermute | solution.py:565
  9.6 0.2 collective-permute-start
  9.8 1.2 %collective-permute-done.1.refs_2_ = bf16[272,128]{1,0:T(8,128)(2,1)S(1)} collective-permute-done((bf16[272,128]{1,0:T(8,128)(2,1)S(1)}, bf16[272,128]{1,0:T(8,128)(2,1)S(1)}, u32[]{:S(2)}, u32[]{:S(2)}) %collective-permute-start.1) | collective-permute-done | bytes 69664 | tf_op jit(solution)/shard_map/ppermute | solution.py:565
  11.0 2.7 %collective-permute-done.2.refs_3_ = bf16[272,128]{1,0:T(8,128)(2,1)S(1)} collective-permute-done((bf16[272,128]{1,0:T(8,128)(2,1)S(1)}, bf16[272,128]{1,0:T(8,128)(2,1)S(1)}, u32[]{:S(2)}, u32[]{:S(2)}) %collective-permute-start.2) | collective-permute-done | bytes 69664 | tf_op jit(solution)/shard_map/ppermute | solution.py:565
  13.7 1.3 %collective-permute-done.refs_1_ = bf16[272,128]{1,0:T(8,128)(2,1)S(1)} collective-permute-done((bf16[272,128]{1,0:T(8,128)(2,1)S(1)}, bf16[272,128]{1,0:T(8,128)(2,1)S(1)}, u32[]{:S(2)}, u32[]{:S(2)}) %collective-permute-start) | collective-permute-done | bytes 69664 | tf_op jit(solution)/shard_map/ppermute | solution.py:565
  15.0 0.8 %gather.1 = (bf16[272,128]{1,0:T(8,128)(2,1)S(1)}, f32[272,128]{1,0:T(8,128)}, f32[272,128]{1,0:T(8,128)S(1)}, f32[272,128]{1,0:T(8,128)S(1)}, f32[272,128]{1,0:T(8,128)S(1)}) custom-call(s32[1]{0:T(128)} %bitcast.place_ref, f32[272,128]{1,0:T(8,128)S(1)} %get-tuple-element.66.refs_0_, bf16[272,128]{1,0:T(8,128)(2,1)S(1)} %collective-permute-done.refs_1_, ...), custom_call_target="tpu_custom_call" | custom-call | tf_op jit(solution)/shard_map/gather/pallas_call | solution.py:253
  15.8 2.6 %collective-permute-start.3 = (bf16[272,128]{1,0:T(8,128)(2,1)S(1)}, bf16[272,128]{1,0:T(8,128)(2,1)S(1)}, u32[]{:S(2)}, u32[]{:S(2)}) collective-permute-start(bf16[272,128]{1,0:T(8,128)(2,1)S(1)} %get-tuple-element.69), channel_id=1, source_target_pairs={{0,16},{4,20},{8,24},{12,28},{16,0},{20,4},{24,8},{28,12},{1,17},{... | collective-permute-start | bytes 208904 | tf_op jit(solution)/shard_map/ppermute | solution.py:565
  18.3 3.8 %collective-permute-done.3.got_ref = bf16[272,128]{1,0:T(8,128)(2,1)S(1)} collective-permute-done((bf16[272,128]{1,0:T(8,128)(2,1)S(1)}, bf16[272,128]{1,0:T(8,128)(2,1)S(1)}, u32[]{:S(2)}, u32[]{:S(2)}) %collective-permute-start.3) | collective-permute-done | bytes 69664 | tf_op jit(solution)/shard_map/ppermute | solution.py:565
  22.1 0.1 enter.1
  22.2 0.7 %collective-permute-start.4 = (bf16[256,128]{1,0:T(8,128)(2,1)S(1)}, bf16[256,128]{1,0:T(8,128)(2,1)S(1)}, u32[]{:S(2)}, u32[]{:S(2)}) collective-permute-start(bf16[256,128]{1,0:T(8,128)(2,1)S(1)} %get-tuple-element.74), channel_id=1, source_target_pairs={{0,4},{4,0},{8,12},{12,8},{16,20},{20,16},{24,28},{28,24},{1,5},{5... | collective-permute-start | bytes 196616 | tf_op jit(solution)/shard_map/ppermute | solution.py:565
  22.9 0.2 collective-permute-start.5
  23.2 0.6 local.6
  23.8 0.6 local.5
  24.5 0.6 local.4
  25.1 1.5 %collective-permute-done.4.refs_7_ = bf16[256,128]{1,0:T(8,128)(2,1)S(1)} collective-permute-done((bf16[256,128]{1,0:T(8,128)(2,1)S(1)}, bf16[256,128]{1,0:T(8,128)(2,1)S(1)}, u32[]{:S(2)}, u32[]{:S(2)}) %collective-permute-start.4) | collective-permute-done | bytes 65568 | tf_op jit(solution)/shard_map/ppermute | solution.py:565
  26.6 0.6 collective-permute-done.5.refs_8_
  27.2 0.4 norm_away.2
  27.7 1.4 %collective-permute-start.6 = (bf16[256,128]{1,0:T(8,128)(2,1)S(1)}, bf16[256,128]{1,0:T(8,128)(2,1)S(1)}, u32[]{:S(2)}, u32[]{:S(2)}) collective-permute-start(bf16[256,128]{1,0:T(8,128)(2,1)S(1)} %get-tuple-element.78), channel_id=1, source_target_pairs={{0,12},{4,8},{8,4},{12,0},{16,28},{20,24},{24,20},{28,16},{1,13},{... | collective-permute-start | bytes 196616 | tf_op jit(solution)/shard_map/ppermute | solution.py:565
  29.1 0.6 local.7
  29.8 3.4 %collective-permute-done.6.refs_2_ = bf16[256,128]{1,0:T(8,128)(2,1)S(1)} collective-permute-done((bf16[256,128]{1,0:T(8,128)(2,1)S(1)}, bf16[256,128]{1,0:T(8,128)(2,1)S(1)}, u32[]{:S(2)}, u32[]{:S(2)}) %collective-permute-start.6) | collective-permute-done | bytes 65568 | tf_op jit(solution)/shard_map/ppermute | solution.py:565
  33.1 0.3 norm_away.3
  33.6 0.3 norm_home.3.refs_1_.refs_6_
  33.9 0.5 norm_home.2.refs_0_
  34.4 0.5 collective-permute-done.8.refs_3_
  34.9 0.7 %project.6 = (f32[128,512]{1,0:T(8,128)S(1)}, bf16[128,512]{1,0:T(8,128)(2,1)S(1)}) custom-call(s32[1]{0:T(128)} %bitcast.place_ref, bf16[256,768]{1,0:T(8,128)(2,1)S(1)} %norm_home.2.refs_0_, bf16[256,256]{1,0:T(8,128)(2,1)S(1)} %norm_home.3.refs_1_.refs_6_, bf16[256,768]{1,0:T(8,128)(2,1)S(1)} %collective-permute-done.7.refs_2_, ...), custom_call_target="tpu_custom_call" | custom-call | tf_op jit(solution)/shard_map/project/pallas_call | solution.py:500
  35.6 0.7 %project.7 = (f32[128,512]{1,0:T(8,128)S(1)}, bf16[128,512]{1,0:T(8,128)(2,1)S(1)}) custom-call(s32[1]{0:T(128)} %bitcast.place_ref, bf16[256,768]{1,0:T(8,128)(2,1)S(1)} %norm_home.2.refs_0_, bf16[256,256]{1,0:T(8,128)(2,1)S(1)} %norm_home.3.refs_1_.refs_6_, bf16[256,768]{1,0:T(8,128)(2,1)S(1)} %collective-permute-done.7.refs_2_, ...), custom_call_target="tpu_custom_call" | custom-call | tf_op jit(solution)/shard_map/project/pallas_call | solution.py:500
  36.4 1.3 %project.8 = (f32[128,1024]{1,0:T(8,128)S(1)}, bf16[128,1024]{1,0:T(8,128)(2,1)S(1)}) custom-call(s32[1]{0:T(128)} %bitcast.place_ref, bf16[256,768]{1,0:T(8,128)(2,1)S(1)} %norm_home.2.refs_0_, bf16[256,256]{1,0:T(8,128)(2,1)S(1)} %norm_home.3.refs_1_.refs_6_, bf16[256,768]{1,0:T(8,128)(2,1)S(1)} %collective-permute-done.7.refs_2_, ...), custom_call_target="tpu_custom_call" | custom-call | tf_op jit(solution)/shard_map/project/pallas_call | solution.py:500
  37.7 1.6 %collective-permute-start.13 = (bf16[128,1024]{1,0:T(8,128)(2,1)S(1)}, bf16[128,1024]{1,0:T(8,128)(2,1)S(1)}, u32[]{:S(2)}, u32[]{:S(2)}) collective-permute-start(bf16[128,1024]{1,0:T(8,128)(2,1)S(1)} %get-tuple-element.83.refs_6_), channel_id=1, source_target_pairs={{0,2},{1,3},{2,0},{3,1},{4,6},{5,7},{6,4},{7,5},{8,10},{9,11},{10,... | collective-permute-start | bytes 786440 | tf_op jit(solution)/shard_map/ppermute | solution.py:627
  39.2 1.3 %project.9 = (f32[128,1024]{1,0:T(8,128)S(1)}, bf16[128,1024]{1,0:T(8,128)(2,1)S(1)}) custom-call(s32[1]{0:T(128)} %bitcast.place_ref, bf16[256,768]{1,0:T(8,128)(2,1)S(1)} %norm_home.2.refs_0_, bf16[256,256]{1,0:T(8,128)(2,1)S(1)} %norm_home.3.refs_1_.refs_6_, bf16[256,768]{1,0:T(8,128)(2,1)S(1)} %collective-permute-done.7.refs_2_, ...), custom_call_target="tpu_custom_call" | custom-call | tf_op jit(solution)/shard_map/project/pallas_call | solution.py:500
  40.5 0.6 collective-permute-start.12
  41.1 1.0 %project.10 = (f32[128,768]{1,0:T(8,128)S(1)}, bf16[128,768]{1,0:T(8,128)(2,1)S(1)}) custom-call(s32[1]{0:T(128)} %bitcast.place_ref, bf16[256,768]{1,0:T(8,128)(2,1)S(1)} %norm_home.2.refs_0_, bf16[256,256]{1,0:T(8,128)(2,1)S(1)} %norm_home.3.refs_1_.refs_6_, bf16[256,768]{1,0:T(8,128)(2,1)S(1)} %collective-permute-done.7.refs_2_, ...), custom_call_target="tpu_custom_call" | custom-call | tf_op jit(solution)/shard_map/project/pallas_call | solution.py:500
  42.1 1.6 %collective-permute-start.11 = (bf16[128,768]{1,0:T(8,128)(2,1)S(1)}, bf16[128,768]{1,0:T(8,128)(2,1)S(1)}, u32[]{:S(2)}, u32[]{:S(2)}) collective-permute-start(bf16[128,768]{1,0:T(8,128)(2,1)S(1)} %get-tuple-element.85.refs_6_), channel_id=1, source_target_pairs={{0,2},{1,3},{2,0},{3,1},{4,6},{5,7},{6,4},{7,5},{8,10},{9,11},{10,... | collective-permute-start | bytes 589832 | tf_op jit(solution)/shard_map/ppermute | solution.py:627
  43.7 0.5 collective-permute-start.15
  44.2 1.5 %collective-permute-start.14 = (bf16[128,512]{1,0:T(8,128)(2,1)S(1)}, bf16[128,512]{1,0:T(8,128)(2,1)S(1)}, u32[]{:S(2)}, u32[]{:S(2)}) collective-permute-start(bf16[128,512]{1,0:T(8,128)(2,1)S(1)} %get-tuple-element.82.refs_6_), channel_id=1, source_target_pairs={{0,2},{1,3},{2,0},{3,1},{4,6},{5,7},{6,4},{7,5},{8,10},{9,11},{10,... | collective-permute-start | bytes 393224 | tf_op jit(solution)/shard_map/ppermute | solution.py:627
  45.7 0.5 project.11
  46.2 13.4 %collective-permute-done.15.refs_0_ = bf16[128,512]{1,0:T(8,128)(2,1)S(1)} collective-permute-done((bf16[128,512]{1,0:T(8,128)(2,1)S(1)}, bf16[128,512]{1,0:T(8,128)(2,1)S(1)}, u32[]{:S(2)}, u32[]{:S(2)}) %collective-permute-start.15) | collective-permute-done | bytes 131104 | tf_op jit(solution)/shard_map/ppermute | solution.py:627
  59.5 1.5 %collective-permute-start.10 = (bf16[128,256]{1,0:T(8,128)(2,1)S(1)}, bf16[128,256]{1,0:T(8,128)(2,1)S(1)}, u32[]{:S(2)}, u32[]{:S(2)}) collective-permute-start(bf16[128,256]{1,0:T(8,128)(2,1)S(1)} %get-tuple-element.87), channel_id=1, source_target_pairs={{0,2},{1,3},{2,0},{3,1},{4,6},{5,7},{6,4},{7,5},{8,10},{9,11},{10,... | collective-permute-start | bytes 196616 | tf_op jit(solution)/shard_map/ppermute | solution.py:627
  61.1 0.7 %finish.6.refs_1_ = bf16[128,4096]{1,0:T(8,128)(2,1)} custom-call(f32[128,512]{1,0:T(8,128)S(1)} %get-tuple-element.92.own_ref, bf16[128,4096]{1,0:T(8,128)(2,1)S(1)} %copy-done, bf16[128,512]{1,0:T(8,128)(2,1)S(1)} %collective-permute-done.15.refs_0_), custom_call_target="tpu_custom_call" | custom-call | tf_op jit(solution)/shard_map/finish/pallas_call | solution.py:535
  61.8 0.5 collective-permute-done.14.refs_0_
  62.2 0.7 %finish.7.refs_1_ = bf16[128,4096]{1,0:T(8,128)(2,1)} custom-call(f32[128,512]{1,0:T(8,128)S(1)} %get-tuple-element.91.own_ref, bf16[128,4096]{1,0:T(8,128)(2,1)S(1)} %copy-done, bf16[128,512]{1,0:T(8,128)(2,1)S(1)} %collective-permute-done.14.refs_0_, bf16[128,4096]{1,0:T(8,128)(2,1)} %finish.6.refs_1_), custom_call_target="tpu_custom_call", output_to_operand_aliasing={{}: (3, {})} | custom-call | tf_op jit(solution)/shard_map/finish/pallas_call | solution.py:535
  63.0 0.8 %finish.8.refs_1_ = bf16[128,4096]{1,0:T(8,128)(2,1)} custom-call(f32[128,1024]{1,0:T(8,128)S(1)} %get-tuple-element.90.own_ref, bf16[128,4096]{1,0:T(8,128)(2,1)S(1)} %copy-done, bf16[128,1024]{1,0:T(8,128)(2,1)S(1)} %collective-permute-done.13.refs_0_, bf16[128,4096]{1,0:T(8,128)(2,1)} %finish.7.refs_1_), custom_call_target="tpu_custom_call", output_to_operand_aliasing={{}: (3, {})} | custom-call | tf_op jit(solution)/shard_map/finish/pallas_call | solution.py:535
  63.8 0.8 %finish.9.refs_1_ = bf16[128,4096]{1,0:T(8,128)(2,1)} custom-call(f32[128,1024]{1,0:T(8,128)S(1)} %get-tuple-element.89.own_ref, bf16[128,4096]{1,0:T(8,128)(2,1)S(1)} %copy-done, bf16[128,1024]{1,0:T(8,128)(2,1)S(1)} %collective-permute-done.12.refs_0_, bf16[128,4096]{1,0:T(8,128)(2,1)} %finish.8.refs_1_), custom_call_target="tpu_custom_call", output_to_operand_aliasing={{}: (3, {})} | custom-call | tf_op jit(solution)/shard_map/finish/pallas_call | solution.py:535
  64.7 0.8 %finish.10.refs_1_ = bf16[128,4096]{1,0:T(8,128)(2,1)} custom-call(f32[128,768]{1,0:T(8,128)S(1)} %get-tuple-element.88.own_ref, bf16[128,4096]{1,0:T(8,128)(2,1)S(1)} %copy-done, bf16[128,768]{1,0:T(8,128)(2,1)S(1)} %collective-permute-done.11.refs_0_, bf16[128,4096]{1,0:T(8,128)(2,1)} %finish.9.refs_1_), custom_call_target="tpu_custom_call", output_to_operand_aliasing={{}: (3, {})} | custom-call | tf_op jit(solution)/shard_map/finish/pallas_call | solution.py:535
  65.4 0.7 %finish.11 = bf16[128,4096]{1,0:T(8,128)(2,1)} custom-call(f32[128,256]{1,0:T(8,128)S(1)} %get-tuple-element.86.own_ref, bf16[128,4096]{1,0:T(8,128)(2,1)S(1)} %copy-done, bf16[128,256]{1,0:T(8,128)(2,1)S(1)} %collective-permute-done.10.refs_0_, bf16[128,4096]{1,0:T(8,128)(2,1)} %finish.10.refs_1_), custom_call_target="tpu_custom_call", output_to_operand_aliasing={{}: (3, {})} | custom-call | tf_op jit(solution)/shard_map/finish/pallas_call | solution.py:535
  (17 shorter events, 0.2 us)
Async XLA Ops:
  0.0 27.2 %copy-start.1 = (f32[1024]{0:T(1024)S(1)}, f32[1024]{0:T(1024)}, u32[]{:S(2)}) copy-start(f32[1024]{0:T(1024)} %param.11) | copy-start | bytes 12292
  5.1 29.8 %collective-permute-start.9 = (bf16[1024,4096]{1,0:T(8,128)(2,1)}, bf16[1024,4096]{1,0:T(8,128)(2,1)S(1)}, u32[]{:S(2)}, u32[]{:S(2)}) collective-permute-start(bf16[1024,4096]{1,0:T(8,128)(2,1)} %refs_4_.5), channel_id=1, source_target_pairs={{0,1},{1,0},{2,3},{3,2},{4,5},{5,4},{6,7},{7,6},{8,9},{9,8},{10,11... | collective-permute-start | bytes 25165832 | tf_op jit(solution)/shard_map/ppermute | solution.py:576
  5.6 5.4 %collective-permute-start.1 = (bf16[272,128]{1,0:T(8,128)(2,1)S(1)}, bf16[272,128]{1,0:T(8,128)(2,1)S(1)}, u32[]{:S(2)}, u32[]{:S(2)}) collective-permute-start(bf16[272,128]{1,0:T(8,128)(2,1)S(1)} %get-tuple-element.67), channel_id=1, source_target_pairs={{0,8},{4,12},{8,0},{12,4},{16,24},{20,28},{24,16},{28,20},{1,9},{5... | collective-permute-start | bytes 208904 | tf_op jit(solution)/shard_map/ppermute | solution.py:565
  8.3 5.5 %collective-permute-start.2 = (bf16[272,128]{1,0:T(8,128)(2,1)S(1)}, bf16[272,128]{1,0:T(8,128)(2,1)S(1)}, u32[]{:S(2)}, u32[]{:S(2)}) collective-permute-start(bf16[272,128]{1,0:T(8,128)(2,1)S(1)} %get-tuple-element.68), channel_id=1, source_target_pairs={{0,12},{4,8},{8,4},{12,0},{16,28},{20,24},{24,20},{28,16},{1,13},{... | collective-permute-start | bytes 208904 | tf_op jit(solution)/shard_map/ppermute | solution.py:565
  9.6 5.3 %collective-permute-start = (bf16[272,128]{1,0:T(8,128)(2,1)S(1)}, bf16[272,128]{1,0:T(8,128)(2,1)S(1)}, u32[]{:S(2)}, u32[]{:S(2)}) collective-permute-start(bf16[272,128]{1,0:T(8,128)(2,1)S(1)} %get-tuple-element.52.hold_ref), channel_id=1, source_target_pairs={{0,4},{4,0},{8,12},{12,8},{16,20},{20,16},{24,28},{28,24},{1,5},{5... | collective-permute-start | bytes 208904 | tf_op jit(solution)/shard_map/ppermute | solution.py:565
  15.8 6.4 %collective-permute-start.3 = (bf16[272,128]{1,0:T(8,128)(2,1)S(1)}, bf16[272,128]{1,0:T(8,128)(2,1)S(1)}, u32[]{:S(2)}, u32[]{:S(2)}) collective-permute-start(bf16[272,128]{1,0:T(8,128)(2,1)S(1)} %get-tuple-element.69), channel_id=1, source_target_pairs={{0,16},{4,20},{8,24},{12,28},{16,0},{20,4},{24,8},{28,12},{1,17},{... | collective-permute-start | bytes 208904 | tf_op jit(solution)/shard_map/ppermute | solution.py:565
  22.2 4.3 %collective-permute-start.4 = (bf16[256,128]{1,0:T(8,128)(2,1)S(1)}, bf16[256,128]{1,0:T(8,128)(2,1)S(1)}, u32[]{:S(2)}, u32[]{:S(2)}) collective-permute-start(bf16[256,128]{1,0:T(8,128)(2,1)S(1)} %get-tuple-element.74), channel_id=1, source_target_pairs={{0,4},{4,0},{8,12},{12,8},{16,20},{20,16},{24,28},{28,24},{1,5},{5... | collective-permute-start | bytes 196616 | tf_op jit(solution)/shard_map/ppermute | solution.py:565
  22.9 4.3 %collective-permute-start.5 = (bf16[256,128]{1,0:T(8,128)(2,1)S(1)}, bf16[256,128]{1,0:T(8,128)(2,1)S(1)}, u32[]{:S(2)}, u32[]{:S(2)}) collective-permute-start(bf16[256,128]{1,0:T(8,128)(2,1)S(1)} %get-tuple-element.75), channel_id=1, source_target_pairs={{0,8},{4,12},{8,0},{12,4},{16,24},{20,28},{24,16},{28,20},{1,9},{5... | collective-permute-start | bytes 196616 | tf_op jit(solution)/shard_map/ppermute | solution.py:565
  23.2 11.7 %slice-start = ((s8[8388608]{0:T(1024)(128)(4,1)}), s8[4194304]{0:T(1024)(128)(4,1)S(1)}, s32[]{:S(2)}) async-start(s8[8388608]{0:T(1024)(128)(4,1)} %bitcast.5), calls=%async_computation | async-start | bytes 8388608
  27.2 7.7 %slice-start.1 = ((s8[8388608]{0:T(1024)(128)(4,1)}), s8[4194304]{0:T(1024)(128)(4,1)S(1)}, s32[]{:S(2)}) async-start(s8[8388608]{0:T(1024)(128)(4,1)} %bitcast.5), calls=%async_computation.1 | async-start | bytes 8388608
  27.7 7.2 %collective-permute-start.7 = (bf16[256,768]{1,0:T(8,128)(2,1)S(1)}, bf16[256,768]{1,0:T(8,128)(2,1)S(1)}, u32[]{:S(2)}, u32[]{:S(2)}) collective-permute-start(bf16[256,768]{1,0:T(8,128)(2,1)S(1)} %norm_away.2), channel_id=1, source_target_pairs={{0,1},{1,0},{2,3},{3,2},{4,5},{5,4},{6,7},{7,6},{8,9},{9,8},{10,11... | collective-permute-start | bytes 1179656 | tf_op jit(solution)/shard_map/ppermute | solution.py:610
  27.7 5.4 %collective-permute-start.6 = (bf16[256,128]{1,0:T(8,128)(2,1)S(1)}, bf16[256,128]{1,0:T(8,128)(2,1)S(1)}, u32[]{:S(2)}, u32[]{:S(2)}) collective-permute-start(bf16[256,128]{1,0:T(8,128)(2,1)S(1)} %get-tuple-element.78), channel_id=1, source_target_pairs={{0,12},{4,8},{8,4},{12,0},{16,28},{20,24},{24,20},{28,16},{1,13},{... | collective-permute-start | bytes 196616 | tf_op jit(solution)/shard_map/ppermute | solution.py:565
  33.5 1.4 %collective-permute-start.8 = (bf16[256,256]{1,0:T(8,128)(2,1)S(1)}, bf16[256,256]{1,0:T(8,128)(2,1)S(1)}, u32[]{:S(2)}, u32[]{:S(2)}) collective-permute-start(bf16[256,256]{1,0:T(8,128)(2,1)S(1)} %norm_away.3), channel_id=1, source_target_pairs={{0,1},{1,0},{2,3},{3,2},{4,5},{5,4},{6,7},{7,6},{8,9},{9,8},{10,11... | collective-permute-start | bytes 393224 | tf_op jit(solution)/shard_map/ppermute | solution.py:610
  37.7 25.3 %collective-permute-start.13 = (bf16[128,1024]{1,0:T(8,128)(2,1)S(1)}, bf16[128,1024]{1,0:T(8,128)(2,1)S(1)}, u32[]{:S(2)}, u32[]{:S(2)}) collective-permute-start(bf16[128,1024]{1,0:T(8,128)(2,1)S(1)} %get-tuple-element.83.refs_6_), channel_id=1, source_target_pairs={{0,2},{1,3},{2,0},{3,1},{4,6},{5,7},{6,4},{7,5},{8,10},{9,11},{10,... | collective-permute-start | bytes 786440 | tf_op jit(solution)/shard_map/ppermute | solution.py:627
  40.5 23.3 %collective-permute-start.12 = (bf16[128,1024]{1,0:T(8,128)(2,1)S(1)}, bf16[128,1024]{1,0:T(8,128)(2,1)S(1)}, u32[]{:S(2)}, u32[]{:S(2)}) collective-permute-start(bf16[128,1024]{1,0:T(8,128)(2,1)S(1)} %get-tuple-element.84.refs_6_), channel_id=1, source_target_pairs={{0,2},{1,3},{2,0},{3,1},{4,6},{5,7},{6,4},{7,5},{8,10},{9,11},{10,... | collective-permute-start | bytes 786440 | tf_op jit(solution)/shard_map/ppermute | solution.py:627
  42.1 18.9 %copy-start = (bf16[128,4096]{1,0:T(8,128)(2,1)S(1)}, bf16[128,4096]{1,0:T(8,128)(2,1)}, u32[]{:S(2)}) copy-start(bf16[128,4096]{1,0:T(8,128)(2,1)} %residual_ref.11) | copy-start | bytes 3145732
  42.1 22.5 %collective-permute-start.11 = (bf16[128,768]{1,0:T(8,128)(2,1)S(1)}, bf16[128,768]{1,0:T(8,128)(2,1)S(1)}, u32[]{:S(2)}, u32[]{:S(2)}) collective-permute-start(bf16[128,768]{1,0:T(8,128)(2,1)S(1)} %get-tuple-element.85.refs_6_), channel_id=1, source_target_pairs={{0,2},{1,3},{2,0},{3,1},{4,6},{5,7},{6,4},{7,5},{8,10},{9,11},{10,... | collective-permute-start | bytes 589832 | tf_op jit(solution)/shard_map/ppermute | solution.py:627
  43.7 15.9 %collective-permute-start.15 = (bf16[128,512]{1,0:T(8,128)(2,1)S(1)}, bf16[128,512]{1,0:T(8,128)(2,1)S(1)}, u32[]{:S(2)}, u32[]{:S(2)}) collective-permute-start(bf16[128,512]{1,0:T(8,128)(2,1)S(1)} %get-tuple-element.81.refs_6_), channel_id=1, source_target_pairs={{0,2},{1,3},{2,0},{3,1},{4,6},{5,7},{6,4},{7,5},{8,10},{9,11},{10,... | collective-permute-start | bytes 393224 | tf_op jit(solution)/shard_map/ppermute | solution.py:627
  44.2 18.0 %collective-permute-start.14 = (bf16[128,512]{1,0:T(8,128)(2,1)S(1)}, bf16[128,512]{1,0:T(8,128)(2,1)S(1)}, u32[]{:S(2)}, u32[]{:S(2)}) collective-permute-start(bf16[128,512]{1,0:T(8,128)(2,1)S(1)} %get-tuple-element.82.refs_6_), channel_id=1, source_target_pairs={{0,2},{1,3},{2,0},{3,1},{4,6},{5,7},{6,4},{7,5},{8,10},{9,11},{10,... | collective-permute-start | bytes 393224 | tf_op jit(solution)/shard_map/ppermute | solution.py:627
  59.5 5.9 %collective-permute-start.10 = (bf16[128,256]{1,0:T(8,128)(2,1)S(1)}, bf16[128,256]{1,0:T(8,128)(2,1)S(1)}, u32[]{:S(2)}, u32[]{:S(2)}) collective-permute-start(bf16[128,256]{1,0:T(8,128)(2,1)S(1)} %get-tuple-element.87), channel_id=1, source_target_pairs={{0,2},{1,3},{2,0},{3,1},{4,6},{5,7},{6,4},{7,5},{8,10},{9,11},{10,... | collective-permute-start | bytes 196616 | tf_op jit(solution)/shard_map/ppermute | solution.py:627
where the time goes:
time: 66.4 us; the launch traced here: 66.1 us
  waiting for transfers between devices  28.8 us (43%)
  Pallas kernels  20 us (30%)
  starting transfers between devices  17 us (26%)
    ppermute x7, waiting for transfers between devices, swap(): return lax.ppermute(x, 'ctx', [(i, i ^ bit) for i in range(blocks)])  14.5 us
    ppermute x6, waiting for transfers between devices, shards(): got.append(lax.ppermute(piece, 'exp', perm))  13.8 us
    ppermute x7, starting transfers between devices, swap(): return lax.ppermute(x, 'ctx', [(i, i ^ bit) for i in range(blocks)])  9.07 us
    ppermute x6, starting transfers between devices, shards(): got.append(lax.ppermute(piece, 'exp', perm))  7.26 us
    pallas_call x6, Pallas kernels, project(): pl.pallas_call(functools.partial(project_kernel, block, first, tile, size...  5.45 us
    pallas_call x6, Pallas kernels, finish(): pl.pallas_call(functools.partial(finish_kernel, first, len(parts)), in_sp...  4.54 us
    pallas_call x1, Pallas kernels, early_states(): pl.pallas_call(functools.partial(early_kernel, size, count, width), in_sp...  2.81 us
    pallas_call x4, Pallas kernels, local(): pl.pallas_call(functools.partial(local_kernel, size, count, width, away),...  2.53 us
  transfers between devices with their start and end apart: 16, of which 10 were waited for; matrix products, arithmetic and copies ran while one was open for 0% of the time, Pallas kernels for 17%

commit v1 on v0

--- a/solution.py
+++ b/solution.py
@@ -106,29 +106,23 @@
     weight_ref[...] = jnp.exp(cum[:, cum.shape[1] - 1 :] - cum)
 
 
+def part_columns(place_ref, size, away, cols):
+    return pl.ds(pl.multiple_of(part_of(place_ref, size, away) * cols, cols), cols)
+
+
 def early_kernel(size, count, width, place_ref, logd_in, key_in, value_in, *refs):
     pay_refs = refs[: size - 1]
     key_ref, value_ref, logd_ref, cum_ref, weight_ref, logd_sem, sems = refs[size - 1 :]
-    cols = count * width
-    logd = pltpu.make_async_copy(logd_in, logd_ref, logd_sem)
-    logd.start()
-    copies = []
+    copies = [pltpu.make_async_copy(logd_in, logd_ref, logd_sem)]
+    copies += copies_of(key_in, key_ref, sems.at[0]) + copies_of(value_in, value_ref, sems.at[1])
+    for copy in copies:
+        copy.start()
+    copies[0].wait()
+    put_sums(logd_ref, cum_ref, weight_ref)
+    for copy in copies[1:]:
+        copy.wait()
     for away in range(1, size):
-        part = part_of(place_ref, size, away)
-        first = pl.multiple_of(part * cols, cols)
-        here = pl.ds((away - 1) * cols, cols)
-        copies.append(
-            copies_of(key_in, key_ref.at[:, here], sems.at[0, away - 1], first)
-            + copies_of(value_in, value_ref.at[:, here], sems.at[1, away - 1], first)
-        )
-        for copy in copies[-1]:
-            copy.start()
-    logd.wait()
-    put_sums(logd_ref, cum_ref, weight_ref)
-    for away in range(1, size):
-        for copy in copies[away - 1]:
-            copy.wait()
-        here = slice((away - 1) * cols, away * cols)
+        here = part_columns(place_ref, size, away, count * width)
         put_states(
             part_of(place_ref, size, away), count, width, key_ref[:, here], value_ref[:, here],
             weight_ref, cum_ref, pay_refs[away - 1],
@@ -137,43 +131,34 @@
 
 def early_states(place, logd, key, value, size, count, width):
     heads, rows = logd.shape
-    cols = (size - 1) * count * width
     *pays, key, value = pl.pallas_call(
         functools.partial(early_kernel, size, count, width),
         in_specs=[SMEM] + [ANY] * 3,
         out_specs=[VMEM] * (size + 1),
-        out_shape=[pay_shape(count, width, BF16)] * (size - 1) + [held((rows, cols), BF16)] * 2,
+        out_shape=[pay_shape(count, width, BF16)] * (size - 1) + [held(key.shape, BF16)] * 2,
         scratch_shapes=[pltpu.VMEM((heads, rows), F32)] * 3
-        + [pltpu.SemaphoreType.DMA, pltpu.SemaphoreType.DMA((2, size - 1, 4))],
+        + [pltpu.SemaphoreType.DMA, pltpu.SemaphoreType.DMA((2, 2))],
         compiler_params=PACKED,
         name="early_states",
     )(place, outside(logd), outside(key), outside(value))
     return pays, key, value
 
 
-def load_kernel(size, count, width, place_ref, logd_in, key_in, value_in, query_in, hold_ref, *refs):
-    pay_ref, key_ref, value_ref, query_ref, cum_ref, logd_ref, weight_ref, logd_sem, sems = refs
-    cols = count * width
+def load_kernel(size, count, width, place_ref, logd_in, query_in, key_ref, value_ref, hold_ref, *refs):
+    pay_ref, query_ref, cum_ref, logd_ref, weight_ref, logd_sem, sems = refs
     logd = pltpu.make_async_copy(logd_in, logd_ref, logd_sem)
     logd.start()
-    first = pl.multiple_of(part_of(place_ref, size, 0) * cols, cols)
-    copies = copies_of(key_in, key_ref, sems.at[0], first)
-    copies += copies_of(value_in, value_ref, sems.at[1], first)
-    last = []
-    for away in range(size):
-        start = pl.multiple_of(part_of(place_ref, size, away) * cols, cols)
-        target = query_ref.at[:, pl.ds(away * cols, cols)]
-        last += copies_of(query_in, target, sems.at[2 + away], start)
-    for copy in copies + last:
+    copies = copies_of(query_in, query_ref, sems)
+    for copy in copies:
         copy.start()
     logd.wait()
     put_sums(logd_ref, cum_ref, weight_ref)
+    here = part_columns(place_ref, size, 0, count * width)
+    put_states(
+        part_of(place_ref, size, 0), count, width, key_ref[:, here], value_ref[:, here],
+        weight_ref, cum_ref, pay_ref,
+    )
     for copy in copies:
-        copy.wait()
-    put_states(
-        part_of(place_ref, size, 0), count, width, key_ref[...], value_ref[...], weight_ref, cum_ref, pay_ref
-    )
-    for copy in last:
         copy.wait()
 
 
@@ -181,20 +166,18 @@
     heads, rows = logd.shape
     return pl.pallas_call(
         functools.partial(load_kernel, size, count, width),
-        in_specs=[SMEM] + [ANY] * 5,
-        out_specs=[VMEM] * 5,
+        in_specs=[SMEM, ANY, ANY, VMEM, VMEM, ANY],
+        out_specs=[VMEM] * 3,
         out_shape=[
             pay_shape(count, width, F32),
-            held((rows, count * width), BF16),
-            held((rows, count * width), BF16),
             held(query.shape, BF16),
             held((heads, rows), F32),
         ],
         scratch_shapes=[pltpu.VMEM((heads, rows), F32)] * 2
-        + [pltpu.SemaphoreType.DMA, pltpu.SemaphoreType.DMA((2 + size, 4))],
+        + [pltpu.SemaphoreType.DMA, pltpu.SemaphoreType.DMA((2,))],
         compiler_params=PACKED,
         name="load",
-    )(place, outside(logd), outside(key), outside(value), outside(query), hold)
+    )(place, outside(logd), outside(query), near(key), near(value), hold)
 
 
 def decay_row(pay, j, count, width):
@@ -223,7 +206,8 @@
 
 
 def gather_kernel(size, count, width, place_ref, *refs):
-    in_refs, pay_ref, window_ref, past_refs = refs[:size], refs[size], refs[size + 1], refs[size + 2 :]
+    in_refs, pay_ref, past_refs = refs[:size], refs[size], refs[size + 1 : 2 * size]
+    window_refs = refs[2 * size :]
     decays = [[] for _ in range(size)]
     for j in range(count):
         rows = slice(j * width, (j + 1) * width)
@@ -239,26 +223,26 @@
                 total, total_decay = total * decay + state, total_decay * decay
             else:
                 total, total_decay = state, decay
-        window_ref[rows, :] = total
-        pay_ref[rows, :] = total.astype(pay_ref.dtype)
+        for ref in (pay_ref, *window_refs):
+            ref[rows, :] = total.astype(ref.dtype)
         decays[-1].append(total_decay)
     for ref, rows in zip(past_refs, decays):
         put_decays(ref, rows, count, width)
-    put_decays(window_ref, decays[-1], count, width)
-    put_decays(pay_ref, decays[-1], count, width)
-
-
-def gather(place, own, met, size, count, width):
+    for ref in (pay_ref, *window_refs):
+        put_decays(ref, decays[-1], count, width)
+
+
+def gather(place, own, met, size, count, width, keep):
     shape = own.shape
-    pay, window, *past = pl.pallas_call(
+    pay, *past = pl.pallas_call(
         functools.partial(gather_kernel, size, count, width),
         in_specs=[SMEM] + [VMEM] * size,
-        out_specs=[VMEM] * (size + 1),
-        out_shape=[held(shape, BF16)] + [held(shape, F32)] * size,
+        out_specs=[VMEM] * (size + keep),
+        out_shape=[held(shape, BF16)] + [held(shape, F32)] * (size - 1 + keep),
         compiler_params=PARAMS,
         name="gather",
     )(place, near(own), *map(near, met))
-    return pay, window, past
+    return pay, past[: size - 1], past[-1]
 
 
 def widen_kernel(count, width, bit, opening, keep, place_ref, got_ref, window_ref, before_ref, pay_ref, past_ref, *refs):
@@ -340,10 +324,8 @@
 
 
 def local_kernel(size, count, width, away, place_ref, cum_ref, q_ref, k_ref, v_ref, out_ref, decayed_ref):
-    from_q, from_kv = away * count, max(away - 1, 0) * count
-    sums = [
-        cum_ref[pl.ds(part_of(place_ref, size, away) * count + j, 1), :] for j in range(count)
-    ]
+    part = part_of(place_ref, size, away)
+    sums = [cum_ref[pl.ds(part * count + j, 1), :] for j in range(count)]
     rows = cum_ref.shape[1]
     tile = tile_of(rows, 2 * width)
     causal = lax.broadcasted_iota(jnp.int32, (tile, tile), 0) >= lax.broadcasted_iota(
@@ -354,13 +336,13 @@
         turned = jnp.broadcast_to(row, (width, tile)).T
         return jnp.concatenate([turned] * (tile // width), axis=1)
 
-    def columns(start, j):
-        return slice((start + j) * width, (start + j + 1) * width)
+    def columns(j):
+        return pl.ds(pl.multiple_of((part * count + j) * width, width), width)
 
     def scores(j, i):
         return lax.dot_general(
-            q_ref[i * tile : (i + 1) * tile, columns(from_q, j)],
-            k_ref[: (i + 1) * tile, columns(from_kv, j)],
+            q_ref[i * tile : (i + 1) * tile, columns(j)],
+            k_ref[: (i + 1) * tile, columns(j)],
             (((1,), (1,)), ((), ())),
             preferred_element_type=F32,
         )
@@ -381,7 +363,7 @@
 
     def finish(j, i, near_part, far_part, since, decay):
         cols = slice(j * width, (j + 1) * width)
-        from_cols = columns(from_kv, j)
+        from_cols = columns(j)
         here = slice(i * tile, (i + 1) * tile)
         out = jnp.dot(near_part, v_ref[here, from_cols], preferred_element_type=F32)
         if far_part is not None:
@@ -390,7 +372,7 @@
             )
         out_ref[here, cols] = out
         decayed_ref[here, cols] = (
-            q_ref[here, columns(from_q, j)].astype(F32) * decay[:, :width]
+            q_ref[here, columns(j)].astype(F32) * decay[:, :width]
         ).astype(BF16)
 
     units = [(j, i) for i in range(rows // tile) for j in range(count)]
@@ -567,17 +549,15 @@
     logd = log_decay.T
     if heads % 8:
         logd = jnp.pad(logd, ((0, pad_rows(heads) - heads), (0, 0)))
-    sent, keys, values = early_states(place, logd, k_spikes, v_spikes, size, count, width)
+    sent, key, value = early_states(place, logd, k_spikes, v_spikes, size, count, width)
     met = [swap(a, i + 1) for i, a in enumerate(sent)]
-    kept, key, value, query, cum = load(
-        place, logd, k_spikes, v_spikes, q_spikes, sent[0], size, count, width
-    )
+    kept, query, cum = load(place, logd, key, value, q_spikes, sent[0], size, count, width)
     kept, weight = lax.optimization_barrier((kept, out_weight))
     far_weight = lax.ppermute(outside(weight), "exp", cores)
     total = out_weight.shape[1]
     tile = tile_of(total, 512)
 
-    pay, window, past = gather(place, kept, met, size, count, width)
+    pay, past, window = gather(place, kept, met, size, count, width, int(2 * size < blocks))
     _, own_weight = lax.optimization_barrier((pay, out_weight))
     before, got, level, bit = None, None, 0, size
     while bit < blocks:
@@ -592,10 +572,7 @@
 
     insides, queries = [], []
     for away in range(size):
-        inside, decayed = local(
-            place, cum, query, keys if away else key, values if away else value,
-            size, count, width, away,
-        )
+        inside, decayed = local(place, cum, query, key, value, size, count, width, away)
         insides.append(inside)
         queries.append(decayed)
 

time: 66.4 us -> 64.4 us (0.970)
  Pallas kernels: 20 us -> 18.4 us
    pallas_call x1, Pallas kernels: 2.24 us -> 1.57 us  [load(): pl.pallas_call(functools.partial(load_kernel, size, count, width), in_spe...]
  transfers between devices with their start and end apart: 16 -> 16, of which waited for: 10 -> 10; matrix products, arithmetic and copies ran while one was open for 0% -> 0% of each run, Pallas kernels for 17% -> 18%
where the time goes in v1:
time: 64.4 us; the launch traced here: 64.2 us
  waiting for transfers between devices  28.4 us (44%)
  Pallas kernels  18.4 us (29%)
  starting transfers between devices  17.1 us (27%)
    ppermute x7, waiting for transfers between devices, swap(): return lax.ppermute(x, 'ctx', [(i, i ^ bit) for i in range(blocks)])  14.1 us
    ppermute x6, waiting for transfers between devices, shards(): got.append(lax.ppermute(piece, 'exp', perm))  13.8 us
    ppermute x7, starting transfers between devices, swap(): return lax.ppermute(x, 'ctx', [(i, i ^ bit) for i in range(blocks)])  9.13 us
    ppermute x6, starting transfers between devices, shards(): got.append(lax.ppermute(piece, 'exp', perm))  7.29 us
    pallas_call x6, Pallas kernels, project(): pl.pallas_call(functools.partial(project_kernel, block, first, tile, size...  5.44 us
    pallas_call x6, Pallas kernels, finish(): pl.pallas_call(functools.partial(finish_kernel, first, len(parts)), in_sp...  4.52 us
    pallas_call x4, Pallas kernels, local(): pl.pallas_call(functools.partial(local_kernel, size, count, width, away),...  2.91 us
    pallas_call x1, Pallas kernels, early_states(): pl.pallas_call(functools.partial(early_kernel, size, count, width), in_sp...  2.18 us
  transfers between devices with their start and end apart: 16, of which 10 were waited for; matrix products, arithmetic and copies ran while one was open for 0% of the time, Pallas kernels for 18%

profile of v1, /device:TPU:0, one launch (start us, length us, event | category | flops | bytes accessed | tf_op | source)
XLA Modules:
  0.0 64.2 jit_solution(5808298926783846454)
XLA Ops:
  0.0 2.2 %early_states.1 = (bf16[272,128]{1,0:T(8,128)(2,1)S(1)}, bf16[272,128]{1,0:T(8,128)(2,1)S(1)}, bf16[272,128]{1,0:T(8,128)(2,1)S(1)}, bf16[512,1024]{1,0:T(8,128)(2,1)S(1)}, bf16[512,1024]{1,0:T(8,128)(2,1)S(1)}) custom-call(s32[1]{0:T(128)} %bitcast.place_ref, f32[8,512]{1,0:T(8,128)} %bitcast.11, bf16[512,1024]{1,0:T(8,128)(2,1)} %key_in.1, ...), custom_call_target="tpu_custom_call" | custom-call | tf_op jit(solution)/shard_map/early_states/pallas_call | solution.py:134
  2.2 1.6 %load.1 = (f32[272,128]{1,0:T(8,128)S(1)}, bf16[512,1024]{1,0:T(8,128)(2,1)S(1)}, f32[8,512]{1,0:T(8,128)S(1)}) custom-call(s32[1]{0:T(128)} %bitcast.place_ref, f32[8,512]{1,0:T(8,128)} %bitcast.12, bf16[512,1024]{1,0:T(8,128)(2,1)} %query_in.1, bf16[512,1024]{1,0:T(8,128)(2,1)S(1)} %get-tuple-element.50.key_ref.k_ref, ...), custom_call_target="tpu_custom_call" | custom-call | tf_op jit(solution)/shard_map/load/pallas_call | solution.py:167
  3.8 0.6 collective-permute-start.9
  4.3 2.6 %collective-permute-start.1 = (bf16[272,128]{1,0:T(8,128)(2,1)S(1)}, bf16[272,128]{1,0:T(8,128)(2,1)S(1)}, u32[]{:S(2)}, u32[]{:S(2)}) collective-permute-start(bf16[272,128]{1,0:T(8,128)(2,1)S(1)} %get-tuple-element.63), channel_id=1, source_target_pairs={{0,8},{4,12},{8,0},{12,4},{16,24},{20,28},{24,16},{28,20},{1,9},{5... | collective-permute-start | bytes 208904 | tf_op jit(solution)/shard_map/ppermute | solution.py:547
  7.0 1.4 %collective-permute-start.2 = (bf16[272,128]{1,0:T(8,128)(2,1)S(1)}, bf16[272,128]{1,0:T(8,128)(2,1)S(1)}, u32[]{:S(2)}, u32[]{:S(2)}) collective-permute-start(bf16[272,128]{1,0:T(8,128)(2,1)S(1)} %get-tuple-element.64), channel_id=1, source_target_pairs={{0,12},{4,8},{8,4},{12,0},{16,28},{20,24},{24,20},{28,16},{1,13},{... | collective-permute-start | bytes 208904 | tf_op jit(solution)/shard_map/ppermute | solution.py:547
  8.3 0.2 collective-permute-start
  8.5 1.2 %collective-permute-done.1.refs_2_ = bf16[272,128]{1,0:T(8,128)(2,1)S(1)} collective-permute-done((bf16[272,128]{1,0:T(8,128)(2,1)S(1)}, bf16[272,128]{1,0:T(8,128)(2,1)S(1)}, u32[]{:S(2)}, u32[]{:S(2)}) %collective-permute-start.1) | collective-permute-done | bytes 69664 | tf_op jit(solution)/shard_map/ppermute | solution.py:547
  9.7 2.7 %collective-permute-done.2.refs_3_ = bf16[272,128]{1,0:T(8,128)(2,1)S(1)} collective-permute-done((bf16[272,128]{1,0:T(8,128)(2,1)S(1)}, bf16[272,128]{1,0:T(8,128)(2,1)S(1)}, u32[]{:S(2)}, u32[]{:S(2)}) %collective-permute-start.2) | collective-permute-done | bytes 69664 | tf_op jit(solution)/shard_map/ppermute | solution.py:547
  12.4 1.3 %collective-permute-done.refs_1_ = bf16[272,128]{1,0:T(8,128)(2,1)S(1)} collective-permute-done((bf16[272,128]{1,0:T(8,128)(2,1)S(1)}, bf16[272,128]{1,0:T(8,128)(2,1)S(1)}, u32[]{:S(2)}, u32[]{:S(2)}) %collective-permute-start) | collective-permute-done | bytes 69664 | tf_op jit(solution)/shard_map/ppermute | solution.py:547
  13.7 0.1 gather.1
  13.8 2.7 %collective-permute-start.3 = (bf16[272,128]{1,0:T(8,128)(2,1)S(1)}, bf16[272,128]{1,0:T(8,128)(2,1)S(1)}, u32[]{:S(2)}, u32[]{:S(2)}) collective-permute-start(bf16[272,128]{1,0:T(8,128)(2,1)S(1)} %get-tuple-element.65), channel_id=1, source_target_pairs={{0,16},{4,20},{8,24},{12,28},{16,0},{20,4},{24,8},{28,12},{1,17},{... | collective-permute-start | bytes 208904 | tf_op jit(solution)/shard_map/ppermute | solution.py:547
  16.5 3.8 %collective-permute-done.3.got_ref = bf16[272,128]{1,0:T(8,128)(2,1)S(1)} collective-permute-done((bf16[272,128]{1,0:T(8,128)(2,1)S(1)}, bf16[272,128]{1,0:T(8,128)(2,1)S(1)}, u32[]{:S(2)}, u32[]{:S(2)}) %collective-permute-start.3) | collective-permute-done | bytes 69664 | tf_op jit(solution)/shard_map/ppermute | solution.py:547
  20.2 0.1 enter.1
  20.4 0.7 %collective-permute-start.4 = (bf16[256,128]{1,0:T(8,128)(2,1)S(1)}, bf16[256,128]{1,0:T(8,128)(2,1)S(1)}, u32[]{:S(2)}, u32[]{:S(2)}) collective-permute-start(bf16[256,128]{1,0:T(8,128)(2,1)S(1)} %get-tuple-element.70), channel_id=1, source_target_pairs={{0,4},{4,0},{8,12},{12,8},{16,20},{20,16},{24,28},{28,24},{1,5},{5... | collective-permute-start | bytes 196616 | tf_op jit(solution)/shard_map/ppermute | solution.py:547
  21.1 0.2 collective-permute-start.5
  21.3 0.7 %local.6 = (f32[512,256]{1,0:T(8,128)S(1)}, bf16[512,256]{1,0:T(8,128)(2,1)S(1)}) custom-call(s32[1]{0:T(128)} %bitcast.place_ref, f32[8,512]{1,0:T(8,128)S(1)} %get-tuple-element.53.cum_ref, bf16[512,1024]{1,0:T(8,128)(2,1)S(1)} %get-tuple-element.54.q_ref, bf16[512,1024]{1,0:T(8,128)(2,1)S(1)} %get-tuple-element.50.key_ref.k_ref, ...), custom_call_target="tpu_custom_call" | custom-call | tf_op jit(solution)/shard_map/local/pallas_call | solution.py:392
  22.0 0.7 %local.5 = (f32[512,256]{1,0:T(8,128)S(1)}, bf16[512,256]{1,0:T(8,128)(2,1)S(1)}) custom-call(s32[1]{0:T(128)} %bitcast.place_ref, f32[8,512]{1,0:T(8,128)S(1)} %get-tuple-element.53.cum_ref, bf16[512,1024]{1,0:T(8,128)(2,1)S(1)} %get-tuple-element.54.q_ref, bf16[512,1024]{1,0:T(8,128)(2,1)S(1)} %get-tuple-element.50.key_ref.k_ref, ...), custom_call_target="tpu_custom_call" | custom-call | tf_op jit(solution)/shard_map/local/pallas_call | solution.py:392
  22.8 0.7 %local.4 = (f32[512,256]{1,0:T(8,128)S(1)}, bf16[512,256]{1,0:T(8,128)(2,1)S(1)}) custom-call(s32[1]{0:T(128)} %bitcast.place_ref, f32[8,512]{1,0:T(8,128)S(1)} %get-tuple-element.53.cum_ref, bf16[512,1024]{1,0:T(8,128)(2,1)S(1)} %get-tuple-element.54.q_ref, bf16[512,1024]{1,0:T(8,128)(2,1)S(1)} %get-tuple-element.50.key_ref.k_ref, ...), custom_call_target="tpu_custom_call" | custom-call | tf_op jit(solution)/shard_map/local/pallas_call | solution.py:392
  23.5 1.2 %collective-permute-done.4.refs_7_ = bf16[256,128]{1,0:T(8,128)(2,1)S(1)} collective-permute-done((bf16[256,128]{1,0:T(8,128)(2,1)S(1)}, bf16[256,128]{1,0:T(8,128)(2,1)S(1)}, u32[]{:S(2)}, u32[]{:S(2)}) %collective-permute-start.4) | collective-permute-done | bytes 65568 | tf_op jit(solution)/shard_map/ppermute | solution.py:547
  24.7 0.6 collective-permute-done.5.refs_8_
  25.3 0.5 norm_away.2
  25.9 1.4 %collective-permute-start.6 = (bf16[256,128]{1,0:T(8,128)(2,1)S(1)}, bf16[256,128]{1,0:T(8,128)(2,1)S(1)}, u32[]{:S(2)}, u32[]{:S(2)}) collective-permute-start(bf16[256,128]{1,0:T(8,128)(2,1)S(1)} %get-tuple-element.74), channel_id=1, source_target_pairs={{0,12},{4,8},{8,4},{12,0},{16,28},{20,24},{24,20},{28,16},{1,13},{... | collective-permute-start | bytes 196616 | tf_op jit(solution)/shard_map/ppermute | solution.py:547
  27.2 0.7 %local.7 = (f32[512,256]{1,0:T(8,128)S(1)}, bf16[512,256]{1,0:T(8,128)(2,1)S(1)}) custom-call(s32[1]{0:T(128)} %bitcast.place_ref, f32[8,512]{1,0:T(8,128)S(1)} %get-tuple-element.53.cum_ref, bf16[512,1024]{1,0:T(8,128)(2,1)S(1)} %get-tuple-element.54.q_ref, bf16[512,1024]{1,0:T(8,128)(2,1)S(1)} %get-tuple-element.50.key_ref.k_ref, ...), custom_call_target="tpu_custom_call" | custom-call | tf_op jit(solution)/shard_map/local/pallas_call | solution.py:392
  28.0 3.3 %collective-permute-done.6.refs_2_ = bf16[256,128]{1,0:T(8,128)(2,1)S(1)} collective-permute-done((bf16[256,128]{1,0:T(8,128)(2,1)S(1)}, bf16[256,128]{1,0:T(8,128)(2,1)S(1)}, u32[]{:S(2)}, u32[]{:S(2)}) %collective-permute-start.6) | collective-permute-done | bytes 65568 | tf_op jit(solution)/shard_map/ppermute | solution.py:547
  31.3 0.3 norm_away.3
  31.7 0.3 norm_home.3.refs_1_.refs_6_
  32.0 0.5 norm_home.2.refs_0_
  32.5 0.5 collective-permute-done.8.refs_3_
  33.0 0.7 %project.6 = (f32[128,512]{1,0:T(8,128)S(1)}, bf16[128,512]{1,0:T(8,128)(2,1)S(1)}) custom-call(s32[1]{0:T(128)} %bitcast.place_ref, bf16[256,768]{1,0:T(8,128)(2,1)S(1)} %norm_home.2.refs_0_, bf16[256,256]{1,0:T(8,128)(2,1)S(1)} %norm_home.3.refs_1_.refs_6_, bf16[256,768]{1,0:T(8,128)(2,1)S(1)} %collective-permute-done.7.refs_2_, ...), custom_call_target="tpu_custom_call" | custom-call | tf_op jit(solution)/shard_map/project/pallas_call | solution.py:482
  33.8 0.7 %project.7 = (f32[128,512]{1,0:T(8,128)S(1)}, bf16[128,512]{1,0:T(8,128)(2,1)S(1)}) custom-call(s32[1]{0:T(128)} %bitcast.place_ref, bf16[256,768]{1,0:T(8,128)(2,1)S(1)} %norm_home.2.refs_0_, bf16[256,256]{1,0:T(8,128)(2,1)S(1)} %norm_home.3.refs_1_.refs_6_, bf16[256,768]{1,0:T(8,128)(2,1)S(1)} %collective-permute-done.7.refs_2_, ...), custom_call_target="tpu_custom_call" | custom-call | tf_op jit(solution)/shard_map/project/pallas_call | solution.py:482
  34.5 1.3 %project.8 = (f32[128,1024]{1,0:T(8,128)S(1)}, bf16[128,1024]{1,0:T(8,128)(2,1)S(1)}) custom-call(s32[1]{0:T(128)} %bitcast.place_ref, bf16[256,768]{1,0:T(8,128)(2,1)S(1)} %norm_home.2.refs_0_, bf16[256,256]{1,0:T(8,128)(2,1)S(1)} %norm_home.3.refs_1_.refs_6_, bf16[256,768]{1,0:T(8,128)(2,1)S(1)} %collective-permute-done.7.refs_2_, ...), custom_call_target="tpu_custom_call" | custom-call | tf_op jit(solution)/shard_map/project/pallas_call | solution.py:482
  35.8 1.6 %collective-permute-start.13 = (bf16[128,1024]{1,0:T(8,128)(2,1)S(1)}, bf16[128,1024]{1,0:T(8,128)(2,1)S(1)}, u32[]{:S(2)}, u32[]{:S(2)}) collective-permute-start(bf16[128,1024]{1,0:T(8,128)(2,1)S(1)} %get-tuple-element.79.refs_6_), channel_id=1, source_target_pairs={{0,2},{1,3},{2,0},{3,1},{4,6},{5,7},{6,4},{7,5},{8,10},{9,11},{10,... | collective-permute-start | bytes 786440 | tf_op jit(solution)/shard_map/ppermute | solution.py:604
  37.4 1.3 %project.9 = (f32[128,1024]{1,0:T(8,128)S(1)}, bf16[128,1024]{1,0:T(8,128)(2,1)S(1)}) custom-call(s32[1]{0:T(128)} %bitcast.place_ref, bf16[256,768]{1,0:T(8,128)(2,1)S(1)} %norm_home.2.refs_0_, bf16[256,256]{1,0:T(8,128)(2,1)S(1)} %norm_home.3.refs_1_.refs_6_, bf16[256,768]{1,0:T(8,128)(2,1)S(1)} %collective-permute-done.7.refs_2_, ...), custom_call_target="tpu_custom_call" | custom-call | tf_op jit(solution)/shard_map/project/pallas_call | solution.py:482
  38.6 0.6 collective-permute-start.12
  39.2 1.0 %project.10 = (f32[128,768]{1,0:T(8,128)S(1)}, bf16[128,768]{1,0:T(8,128)(2,1)S(1)}) custom-call(s32[1]{0:T(128)} %bitcast.place_ref, bf16[256,768]{1,0:T(8,128)(2,1)S(1)} %norm_home.2.refs_0_, bf16[256,256]{1,0:T(8,128)(2,1)S(1)} %norm_home.3.refs_1_.refs_6_, bf16[256,768]{1,0:T(8,128)(2,1)S(1)} %collective-permute-done.7.refs_2_, ...), custom_call_target="tpu_custom_call" | custom-call | tf_op jit(solution)/shard_map/project/pallas_call | solution.py:482
  40.2 1.6 %collective-permute-start.11 = (bf16[128,768]{1,0:T(8,128)(2,1)S(1)}, bf16[128,768]{1,0:T(8,128)(2,1)S(1)}, u32[]{:S(2)}, u32[]{:S(2)}) collective-permute-start(bf16[128,768]{1,0:T(8,128)(2,1)S(1)} %get-tuple-element.81.refs_6_), channel_id=1, source_target_pairs={{0,2},{1,3},{2,0},{3,1},{4,6},{5,7},{6,4},{7,5},{8,10},{9,11},{10,... | collective-permute-start | bytes 589832 | tf_op jit(solution)/shard_map/ppermute | solution.py:604
  41.8 0.5 collective-permute-start.15
  42.3 1.5 %collective-permute-start.14 = (bf16[128,512]{1,0:T(8,128)(2,1)S(1)}, bf16[128,512]{1,0:T(8,128)(2,1)S(1)}, u32[]{:S(2)}, u32[]{:S(2)}) collective-permute-start(bf16[128,512]{1,0:T(8,128)(2,1)S(1)} %get-tuple-element.78.refs_6_), channel_id=1, source_target_pairs={{0,2},{1,3},{2,0},{3,1},{4,6},{5,7},{6,4},{7,5},{8,10},{9,11},{10,... | collective-permute-start | bytes 393224 | tf_op jit(solution)/shard_map/ppermute | solution.py:604
  43.9 0.5 project.11
  44.3 13.4 %collective-permute-done.15.refs_0_ = bf16[128,512]{1,0:T(8,128)(2,1)S(1)} collective-permute-done((bf16[128,512]{1,0:T(8,128)(2,1)S(1)}, bf16[128,512]{1,0:T(8,128)(2,1)S(1)}, u32[]{:S(2)}, u32[]{:S(2)}) %collective-permute-start.15) | collective-permute-done | bytes 131104 | tf_op jit(solution)/shard_map/ppermute | solution.py:604
  57.7 1.5 %collective-permute-start.10 = (bf16[128,256]{1,0:T(8,128)(2,1)S(1)}, bf16[128,256]{1,0:T(8,128)(2,1)S(1)}, u32[]{:S(2)}, u32[]{:S(2)}) collective-permute-start(bf16[128,256]{1,0:T(8,128)(2,1)S(1)} %get-tuple-element.83), channel_id=1, source_target_pairs={{0,2},{1,3},{2,0},{3,1},{4,6},{5,7},{6,4},{7,5},{8,10},{9,11},{10,... | collective-permute-start | bytes 196616 | tf_op jit(solution)/shard_map/ppermute | solution.py:604
  59.2 0.7 %finish.6.refs_1_ = bf16[128,4096]{1,0:T(8,128)(2,1)} custom-call(f32[128,512]{1,0:T(8,128)S(1)} %get-tuple-element.88.own_ref, bf16[128,4096]{1,0:T(8,128)(2,1)S(1)} %copy-done, bf16[128,512]{1,0:T(8,128)(2,1)S(1)} %collective-permute-done.15.refs_0_), custom_call_target="tpu_custom_call" | custom-call | tf_op jit(solution)/shard_map/finish/pallas_call | solution.py:517
  59.9 0.4 collective-permute-done.14.refs_0_
  60.4 0.7 %finish.7.refs_1_ = bf16[128,4096]{1,0:T(8,128)(2,1)} custom-call(f32[128,512]{1,0:T(8,128)S(1)} %get-tuple-element.87.own_ref, bf16[128,4096]{1,0:T(8,128)(2,1)S(1)} %copy-done, bf16[128,512]{1,0:T(8,128)(2,1)S(1)} %collective-permute-done.14.refs_0_, bf16[128,4096]{1,0:T(8,128)(2,1)} %finish.6.refs_1_), custom_call_target="tpu_custom_call", output_to_operand_aliasing={{}: (3, {})} | custom-call | tf_op jit(solution)/shard_map/finish/pallas_call | solution.py:517
  61.1 0.8 %finish.8.refs_1_ = bf16[128,4096]{1,0:T(8,128)(2,1)} custom-call(f32[128,1024]{1,0:T(8,128)S(1)} %get-tuple-element.86.own_ref, bf16[128,4096]{1,0:T(8,128)(2,1)S(1)} %copy-done, bf16[128,1024]{1,0:T(8,128)(2,1)S(1)} %collective-permute-done.13.refs_0_, bf16[128,4096]{1,0:T(8,128)(2,1)} %finish.7.refs_1_), custom_call_target="tpu_custom_call", output_to_operand_aliasing={{}: (3, {})} | custom-call | tf_op jit(solution)/shard_map/finish/pallas_call | solution.py:517
  61.9 0.8 %finish.9.refs_1_ = bf16[128,4096]{1,0:T(8,128)(2,1)} custom-call(f32[128,1024]{1,0:T(8,128)S(1)} %get-tuple-element.85.own_ref, bf16[128,4096]{1,0:T(8,128)(2,1)S(1)} %copy-done, bf16[128,1024]{1,0:T(8,128)(2,1)S(1)} %collective-permute-done.12.refs_0_, bf16[128,4096]{1,0:T(8,128)(2,1)} %finish.8.refs_1_), custom_call_target="tpu_custom_call", output_to_operand_aliasing={{}: (3, {})} | custom-call | tf_op jit(solution)/shard_map/finish/pallas_call | solution.py:517
  62.8 0.8 %finish.10.refs_1_ = bf16[128,4096]{1,0:T(8,128)(2,1)} custom-call(f32[128,768]{1,0:T(8,128)S(1)} %get-tuple-element.84.own_ref, bf16[128,4096]{1,0:T(8,128)(2,1)S(1)} %copy-done, bf16[128,768]{1,0:T(8,128)(2,1)S(1)} %collective-permute-done.11.refs_0_, bf16[128,4096]{1,0:T(8,128)(2,1)} %finish.9.refs_1_), custom_call_target="tpu_custom_call", output_to_operand_aliasing={{}: (3, {})} | custom-call | tf_op jit(solution)/shard_map/finish/pallas_call | solution.py:517
  63.6 0.7 %finish.11 = bf16[128,4096]{1,0:T(8,128)(2,1)} custom-call(f32[128,256]{1,0:T(8,128)S(1)} %get-tuple-element.82.own_ref, bf16[128,4096]{1,0:T(8,128)(2,1)S(1)} %copy-done, bf16[128,256]{1,0:T(8,128)(2,1)S(1)} %collective-permute-done.10.refs_0_, bf16[128,4096]{1,0:T(8,128)(2,1)} %finish.10.refs_1_), custom_call_target="tpu_custom_call", output_to_operand_aliasing={{}: (3, {})} | custom-call | tf_op jit(solution)/shard_map/finish/pallas_call | solution.py:517
  (17 shorter events, 0.2 us)
Async XLA Ops:
  0.0 25.3 %copy-start.1 = (f32[1024]{0:T(1024)S(1)}, f32[1024]{0:T(1024)}, u32[]{:S(2)}) copy-start(f32[1024]{0:T(1024)} %param.11) | copy-start | bytes 12292
  3.8 29.3 %collective-permute-start.9 = (bf16[1024,4096]{1,0:T(8,128)(2,1)}, bf16[1024,4096]{1,0:T(8,128)(2,1)S(1)}, u32[]{:S(2)}, u32[]{:S(2)}) collective-permute-start(bf16[1024,4096]{1,0:T(8,128)(2,1)} %refs_4_.5), channel_id=1, source_target_pairs={{0,1},{1,0},{2,3},{3,2},{4,5},{5,4},{6,7},{7,6},{8,9},{9,8},{10,11... | collective-permute-start | bytes 25165832 | tf_op jit(solution)/shard_map/ppermute | solution.py:556
  4.3 5.4 %collective-permute-start.1 = (bf16[272,128]{1,0:T(8,128)(2,1)S(1)}, bf16[272,128]{1,0:T(8,128)(2,1)S(1)}, u32[]{:S(2)}, u32[]{:S(2)}) collective-permute-start(bf16[272,128]{1,0:T(8,128)(2,1)S(1)} %get-tuple-element.63), channel_id=1, source_target_pairs={{0,8},{4,12},{8,0},{12,4},{16,24},{20,28},{24,16},{28,20},{1,9},{5... | collective-permute-start | bytes 208904 | tf_op jit(solution)/shard_map/ppermute | solution.py:547
  7.0 5.5 %collective-permute-start.2 = (bf16[272,128]{1,0:T(8,128)(2,1)S(1)}, bf16[272,128]{1,0:T(8,128)(2,1)S(1)}, u32[]{:S(2)}, u32[]{:S(2)}) collective-permute-start(bf16[272,128]{1,0:T(8,128)(2,1)S(1)} %get-tuple-element.64), channel_id=1, source_target_pairs={{0,12},{4,8},{8,4},{12,0},{16,28},{20,24},{24,20},{28,16},{1,13},{... | collective-permute-start | bytes 208904 | tf_op jit(solution)/shard_map/ppermute | solution.py:547
  8.3 5.3 %collective-permute-start = (bf16[272,128]{1,0:T(8,128)(2,1)S(1)}, bf16[272,128]{1,0:T(8,128)(2,1)S(1)}, u32[]{:S(2)}, u32[]{:S(2)}) collective-permute-start(bf16[272,128]{1,0:T(8,128)(2,1)S(1)} %get-tuple-element.52.hold_ref), channel_id=1, source_target_pairs={{0,4},{4,0},{8,12},{12,8},{16,20},{20,16},{24,28},{28,24},{1,5},{5... | collective-permute-start | bytes 208904 | tf_op jit(solution)/shard_map/ppermute | solution.py:547
  13.8 6.4 %collective-permute-start.3 = (bf16[272,128]{1,0:T(8,128)(2,1)S(1)}, bf16[272,128]{1,0:T(8,128)(2,1)S(1)}, u32[]{:S(2)}, u32[]{:S(2)}) collective-permute-start(bf16[272,128]{1,0:T(8,128)(2,1)S(1)} %get-tuple-element.65), channel_id=1, source_target_pairs={{0,16},{4,20},{8,24},{12,28},{16,0},{20,4},{24,8},{28,12},{1,17},{... | collective-permute-start | bytes 208904 | tf_op jit(solution)/shard_map/ppermute | solution.py:547
  20.4 4.3 %collective-permute-start.4 = (bf16[256,128]{1,0:T(8,128)(2,1)S(1)}, bf16[256,128]{1,0:T(8,128)(2,1)S(1)}, u32[]{:S(2)}, u32[]{:S(2)}) collective-permute-start(bf16[256,128]{1,0:T(8,128)(2,1)S(1)} %get-tuple-element.70), channel_id=1, source_target_pairs={{0,4},{4,0},{8,12},{12,8},{16,20},{20,16},{24,28},{28,24},{1,5},{5... | collective-permute-start | bytes 196616 | tf_op jit(solution)/shard_map/ppermute | solution.py:547
  21.1 4.3 %collective-permute-start.5 = (bf16[256,128]{1,0:T(8,128)(2,1)S(1)}, bf16[256,128]{1,0:T(8,128)(2,1)S(1)}, u32[]{:S(2)}, u32[]{:S(2)}) collective-permute-start(bf16[256,128]{1,0:T(8,128)(2,1)S(1)} %get-tuple-element.71), channel_id=1, source_target_pairs={{0,8},{4,12},{8,0},{12,4},{16,24},{20,28},{24,16},{28,20},{1,9},{5... | collective-permute-start | bytes 196616 | tf_op jit(solution)/shard_map/ppermute | solution.py:547
  22.0 11.0 %slice-start = ((s8[8388608]{0:T(1024)(128)(4,1)}), s8[4194304]{0:T(1024)(128)(4,1)S(1)}, s32[]{:S(2)}) async-start(s8[8388608]{0:T(1024)(128)(4,1)} %bitcast.5), calls=%async_computation | async-start | bytes 8388608
  25.3 7.7 %slice-start.1 = ((s8[8388608]{0:T(1024)(128)(4,1)}), s8[4194304]{0:T(1024)(128)(4,1)S(1)}, s32[]{:S(2)}) async-start(s8[8388608]{0:T(1024)(128)(4,1)} %bitcast.5), calls=%async_computation.1 | async-start | bytes 8388608
  25.8 7.2 %collective-permute-start.7 = (bf16[256,768]{1,0:T(8,128)(2,1)S(1)}, bf16[256,768]{1,0:T(8,128)(2,1)S(1)}, u32[]{:S(2)}, u32[]{:S(2)}) collective-permute-start(bf16[256,768]{1,0:T(8,128)(2,1)S(1)} %norm_away.2), channel_id=1, source_target_pairs={{0,1},{1,0},{2,3},{3,2},{4,5},{5,4},{6,7},{7,6},{8,9},{9,8},{10,11... | collective-permute-start | bytes 1179656 | tf_op jit(solution)/shard_map/ppermute | solution.py:587
  25.9 5.4 %collective-permute-start.6 = (bf16[256,128]{1,0:T(8,128)(2,1)S(1)}, bf16[256,128]{1,0:T(8,128)(2,1)S(1)}, u32[]{:S(2)}, u32[]{:S(2)}) collective-permute-start(bf16[256,128]{1,0:T(8,128)(2,1)S(1)} %get-tuple-element.74), channel_id=1, source_target_pairs={{0,12},{4,8},{8,4},{12,0},{16,28},{20,24},{24,20},{28,16},{1,13},{... | collective-permute-start | bytes 196616 | tf_op jit(solution)/shard_map/ppermute | solution.py:547
  31.6 1.4 %collective-permute-start.8 = (bf16[256,256]{1,0:T(8,128)(2,1)S(1)}, bf16[256,256]{1,0:T(8,128)(2,1)S(1)}, u32[]{:S(2)}, u32[]{:S(2)}) collective-permute-start(bf16[256,256]{1,0:T(8,128)(2,1)S(1)} %norm_away.3), channel_id=1, source_target_pairs={{0,1},{1,0},{2,3},{3,2},{4,5},{5,4},{6,7},{7,6},{8,9},{9,8},{10,11... | collective-permute-start | bytes 393224 | tf_op jit(solution)/shard_map/ppermute | solution.py:587
  35.8 25.3 %collective-permute-start.13 = (bf16[128,1024]{1,0:T(8,128)(2,1)S(1)}, bf16[128,1024]{1,0:T(8,128)(2,1)S(1)}, u32[]{:S(2)}, u32[]{:S(2)}) collective-permute-start(bf16[128,1024]{1,0:T(8,128)(2,1)S(1)} %get-tuple-element.79.refs_6_), channel_id=1, source_target_pairs={{0,2},{1,3},{2,0},{3,1},{4,6},{5,7},{6,4},{7,5},{8,10},{9,11},{10,... | collective-permute-start | bytes 786440 | tf_op jit(solution)/shard_map/ppermute | solution.py:604
  38.6 23.3 %collective-permute-start.12 = (bf16[128,1024]{1,0:T(8,128)(2,1)S(1)}, bf16[128,1024]{1,0:T(8,128)(2,1)S(1)}, u32[]{:S(2)}, u32[]{:S(2)}) collective-permute-start(bf16[128,1024]{1,0:T(8,128)(2,1)S(1)} %get-tuple-element.80.refs_6_), channel_id=1, source_target_pairs={{0,2},{1,3},{2,0},{3,1},{4,6},{5,7},{6,4},{7,5},{8,10},{9,11},{10,... | collective-permute-start | bytes 786440 | tf_op jit(solution)/shard_map/ppermute | solution.py:604
  40.2 19.0 %copy-start = (bf16[128,4096]{1,0:T(8,128)(2,1)S(1)}, bf16[128,4096]{1,0:T(8,128)(2,1)}, u32[]{:S(2)}) copy-start(bf16[128,4096]{1,0:T(8,128)(2,1)} %residual_ref.11) | copy-start | bytes 3145732
  40.2 22.5 %collective-permute-start.11 = (bf16[128,768]{1,0:T(8,128)(2,1)S(1)}, bf16[128,768]{1,0:T(8,128)(2,1)S(1)}, u32[]{:S(2)}, u32[]{:S(2)}) collective-permute-start(bf16[128,768]{1,0:T(8,128)(2,1)S(1)} %get-tuple-element.81.refs_6_), channel_id=1, source_target_pairs={{0,2},{1,3},{2,0},{3,1},{4,6},{5,7},{6,4},{7,5},{8,10},{9,11},{10,... | collective-permute-start | bytes 589832 | tf_op jit(solution)/shard_map/ppermute | solution.py:604
  41.8 15.8 %collective-permute-start.15 = (bf16[128,512]{1,0:T(8,128)(2,1)S(1)}, bf16[128,512]{1,0:T(8,128)(2,1)S(1)}, u32[]{:S(2)}, u32[]{:S(2)}) collective-permute-start(bf16[128,512]{1,0:T(8,128)(2,1)S(1)} %get-tuple-element.77.refs_6_), channel_id=1, source_target_pairs={{0,2},{1,3},{2,0},{3,1},{4,6},{5,7},{6,4},{7,5},{8,10},{9,11},{10,... | collective-permute-start | bytes 393224 | tf_op jit(solution)/shard_map/ppermute | solution.py:604
  42.3 18.0 %collective-permute-start.14 = (bf16[128,512]{1,0:T(8,128)(2,1)S(1)}, bf16[128,512]{1,0:T(8,128)(2,1)S(1)}, u32[]{:S(2)}, u32[]{:S(2)}) collective-permute-start(bf16[128,512]{1,0:T(8,128)(2,1)S(1)} %get-tuple-element.78.refs_6_), channel_id=1, source_target_pairs={{0,2},{1,3},{2,0},{3,1},{4,6},{5,7},{6,4},{7,5},{8,10},{9,11},{10,... | collective-permute-start | bytes 393224 | tf_op jit(solution)/shard_map/ppermute | solution.py:604
  57.7 5.9 %collective-permute-start.10 = (bf16[128,256]{1,0:T(8,128)(2,1)S(1)}, bf16[128,256]{1,0:T(8,128)(2,1)S(1)}, u32[]{:S(2)}, u32[]{:S(2)}) collective-permute-start(bf16[128,256]{1,0:T(8,128)(2,1)S(1)} %get-tuple-element.83), channel_id=1, source_target_pairs={{0,2},{1,3},{2,0},{3,1},{4,6},{5,7},{6,4},{7,5},{8,10},{9,11},{10,... | collective-permute-start | bytes 196616 | tf_op jit(solution)/shard_map/ppermute | solution.py:604

commit v2 on v1

--- a/solution.py
+++ b/solution.py
@@ -86,16 +86,22 @@
     return (place_ref[0] & (size - 1)) ^ away
 
 
-def put_states(part, count, width, key, value, weight_ref, cum_ref, pay_ref):
+def turned_keys(part, count, width, key, weight_ref):
+    turned = [key[:, j * width : (j + 1) * width].T for j in range(count)]
+    return [
+        turned[j] * weight_ref[pl.ds(part * count + j, 1), :].astype(BF16) for j in range(count)
+    ]
+
+
+def put_states(part, count, width, keyed, value, cum_ref, pay_ref):
     rows = cum_ref.shape[1]
-    turned = [key[:, j * width : (j + 1) * width].T for j in range(count)]
     decays = []
     for j in range(count):
-        head = pl.ds(part * count + j, 1)
-        keyed = turned[j] * weight_ref[head, :].astype(BF16)
-        state = jnp.dot(keyed, value[:, j * width : (j + 1) * width], preferred_element_type=F32)
+        state = jnp.dot(
+            keyed[j], value[:, j * width : (j + 1) * width], preferred_element_type=F32
+        )
         pay_ref[j * width : (j + 1) * width, :] = state.astype(pay_ref.dtype)
-        total = cum_ref[head, :][:, rows - 1 : rows]
+        total = cum_ref[pl.ds(part * count + j, 1), :][:, rows - 1 : rows]
         decays.append(jnp.broadcast_to(jnp.exp(total), (1, width)))
     put_decays(pay_ref, decays, count, width)
 
@@ -113,20 +119,24 @@
 def early_kernel(size, count, width, place_ref, logd_in, key_in, value_in, *refs):
     pay_refs = refs[: size - 1]
     key_ref, value_ref, logd_ref, cum_ref, weight_ref, logd_sem, sems = refs[size - 1 :]
-    copies = [pltpu.make_async_copy(logd_in, logd_ref, logd_sem)]
-    copies += copies_of(key_in, key_ref, sems.at[0]) + copies_of(value_in, value_ref, sems.at[1])
-    for copy in copies:
+    logd = pltpu.make_async_copy(logd_in, logd_ref, logd_sem)
+    keys, values = copies_of(key_in, key_ref, sems.at[0]), copies_of(value_in, value_ref, sems.at[1])
+    for copy in (logd, *keys, *values):
         copy.start()
-    copies[0].wait()
+    logd.wait()
     put_sums(logd_ref, cum_ref, weight_ref)
-    for copy in copies[1:]:
+    for copy in keys:
         copy.wait()
-    for away in range(1, size):
-        here = part_columns(place_ref, size, away, count * width)
-        put_states(
-            part_of(place_ref, size, away), count, width, key_ref[:, here], value_ref[:, here],
-            weight_ref, cum_ref, pay_refs[away - 1],
-        )
+    parts = [part_of(place_ref, size, away) for away in range(1, size)]
+    spans = [part_columns(place_ref, size, away, count * width) for away in range(1, size)]
+    keyed = [
+        turned_keys(part, count, width, key_ref[:, here], weight_ref)
+        for part, here in zip(parts, spans)
+    ]
+    for copy in values:
+        copy.wait()
+    for part, here, turned, pay_ref in zip(parts, spans, keyed, pay_refs):
+        put_states(part, count, width, turned, value_ref[:, here], cum_ref, pay_ref)
 
 
 def early_states(place, logd, key, value, size, count, width):
@@ -154,10 +164,9 @@
     logd.wait()
     put_sums(logd_ref, cum_ref, weight_ref)
     here = part_columns(place_ref, size, 0, count * width)
-    put_states(
-        part_of(place_ref, size, 0), count, width, key_ref[:, here], value_ref[:, here],
-        weight_ref, cum_ref, pay_ref,
-    )
+    part = part_of(place_ref, size, 0)
+    keyed = turned_keys(part, count, width, key_ref[:, here], weight_ref)
+    put_states(part, count, width, keyed, value_ref[:, here], cum_ref, pay_ref)
     for copy in copies:
         copy.wait()
 
@@ -455,23 +464,66 @@
     )(*scalars, gain, *map(near, parts))
 
 
+def summed(size, place_ref, terms, span, total=None):
+    for ref, at, away, weight_ref in terms:
+        cols = weight_ref.shape[0] // size
+        rows = part_columns(place_ref, size, away, cols)
+        part = jnp.dot(
+            ref[:, at * cols : (at + 1) * cols], weight_ref[rows, span], preferred_element_type=F32
+        )
+        total = part if total is None else total + part
+    return total
+
+
+def begin_kernel(size, place_ref, one_ref, two_ref, met_ref, near_ref, far_ref, out_ref):
+    early = range(size - 1)
+    terms = [(one_ref, away, away, near_ref) for away in early]
+    terms += [(met_ref, away, away, far_ref) for away in early]
+    terms += [(two_ref, 0, size - 1, near_ref)]
+    out_ref[...] = summed(size, place_ref, terms, slice(0, out_ref.shape[1]))
+
+
+def begin(place, home, met, first_weight, second_weight, count, size):
+    rows = met.shape[0]
+    return pl.pallas_call(
+        functools.partial(begin_kernel, size),
+        in_specs=[SMEM] + [VMEM] * 5,
+        out_specs=VMEM,
+        out_shape=held((rows, count), F32),
+        compiler_params=PARAMS,
+        name="begin",
+    )(place, *map(near, [*home, met, first_weight, second_weight]))
+
+
+def complete_kernel(block, size, place_ref, begun_ref, two_ref, far_ref, own_ref, away_ref):
+    span = slice(0, own_ref.shape[1])
+    total = summed(size, place_ref, [(two_ref, 0, size - 1, far_ref)], span, begun_ref[...])
+    own_ref[...] = total[:block]
+    away_ref[...] = total[block:].astype(away_ref.dtype)
+
+
+def complete(place, begun, two, second_weight, block, size):
+    rows, count = begun.shape
+    return pl.pallas_call(
+        functools.partial(complete_kernel, block, size),
+        in_specs=[SMEM] + [VMEM] * 3,
+        out_specs=[VMEM, VMEM],
+        out_shape=[held((block, count), F32), held((rows - block, count), BF16)],
+        compiler_params=PARAMS,
+        name="complete",
+    )(place, near(begun), near(two), near(second_weight))
+
+
 def project_kernel(block, first, tile, size, place_ref, *refs):
     own_ref, away_ref = refs[-2:]
-    sides = [(refs[0], refs[1], refs[4]), (refs[2], refs[3], refs[5])]
-    cols = refs[1].shape[1]
+    terms = []
+    for one_ref, two_ref, weight_ref in ((refs[0], refs[1], refs[4]), (refs[2], refs[3], refs[5])):
+        terms += [(one_ref, away, away, weight_ref) for away in range(size - 1)]
+        terms += [(two_ref, 0, size - 1, weight_ref)]
     for i in range(own_ref.shape[1] // tile):
         here = slice(i * tile, (i + 1) * tile)
         span = slice(first + i * tile, first + (i + 1) * tile)
-        total = None
-        for one_ref, two_ref, weight_ref in sides:
-            for away in range(size):
-                last = away == size - 1
-                normed = two_ref[...] if last else one_ref[:, away * cols : (away + 1) * cols]
-                start = pl.multiple_of(part_of(place_ref, size, away) * cols, cols)
-                part = jnp.dot(
-                    normed, weight_ref[pl.ds(start, cols), span], preferred_element_type=F32
-                )
-                total = part if total is None else total + part
+        total = summed(size, place_ref, terms, span)
         own_ref[:, here] = total[:block]
         away_ref[:, here] = total[block:].astype(away_ref.dtype)
 
@@ -592,10 +644,16 @@
         sizes.append(2 * tile)
     rest = total - sum(sizes)
     sizes += [rest - tile // 2, tile // 2] if rest > tile // 2 else [rest]
-    out, at, hold = None, 0, home[1]
+    begun = begin(place, home, other[0], own_weight, far_weight, sizes[0], size)
+    out, at, hold = None, 0, None
     sums = []
-    for span in sizes:
-        own, pieces = project(place, home, other, own_weight, far_weight, hold, block, at, span, tile, size)
+    for index, span in enumerate(sizes):
+        if index:
+            own, pieces = project(
+                place, home, other, own_weight, far_weight, hold, block, at, span, tile, size
+            )
+        else:
+            own, pieces = complete(place, begun, other[1], far_weight, block, size)
         hold = pieces
         got = []
         for d in range(1, chips):

time: 64.4 us -> 64.4 us (level)
    pallas_call x0 -> x2, Pallas kernels: none -> 0.88 us  [the longest x1 0.65 us: begin(): pl.pallas_call(functools.partial(begin_kernel, size), in_specs=[SMEM] + [...]
    pallas_call x6 -> x5, Pallas kernels: 5.44 us -> 4.73 us  [project(): pl.pallas_call(functools.partial(project_kernel, block, first, tile, size...]
  transfers between devices with their start and end apart: 16 -> 16, of which waited for: 10 -> 9; matrix products, arithmetic and copies ran while one was open for 0% -> 0% of each run, Pallas kernels for 18% -> 19%
where the time goes in v2:
time: 64.4 us; the launch traced here: 64.2 us
  waiting for transfers between devices  28 us (43%)
  Pallas kernels  18.8 us (29%)
  starting transfers between devices  17.1 us (27%)
    ppermute x7, waiting for transfers between devices, swap(): return lax.ppermute(x, 'ctx', [(i, i ^ bit) for i in range(blocks)])  14.1 us
    ppermute x6, waiting for transfers between devices, shards(): got.append(lax.ppermute(piece, 'exp', perm))  13.9 us
    ppermute x7, starting transfers between devices, swap(): return lax.ppermute(x, 'ctx', [(i, i ^ bit) for i in range(blocks)])  9.12 us
    ppermute x6, starting transfers between devices, shards(): got.append(lax.ppermute(piece, 'exp', perm))  7.3 us
    pallas_call x5, Pallas kernels, project(): pl.pallas_call(functools.partial(project_kernel, block, first, tile, size...  4.73 us
    pallas_call x6, Pallas kernels, finish(): pl.pallas_call(functools.partial(finish_kernel, first, len(parts)), in_sp...  4.55 us
    pallas_call x4, Pallas kernels, local(): pl.pallas_call(functools.partial(local_kernel, size, count, width, away),...  2.9 us
    pallas_call x1, Pallas kernels, early_states(): pl.pallas_call(functools.partial(early_kernel, size, count, width), in_sp...  2.37 us
  transfers between devices with their start and end apart: 16, of which 9 were waited for; matrix products, arithmetic and copies ran while one was open for 0% of the time, Pallas kernels for 19%

profile of v2, /device:TPU:0, one launch (start us, length us, event | category | flops | bytes accessed | tf_op | source)
XLA Modules:
  0.0 64.2 jit_solution(3924530521948112191)
XLA Ops:
  0.0 2.4 %early_states.1 = (bf16[272,128]{1,0:T(8,128)(2,1)S(1)}, bf16[272,128]{1,0:T(8,128)(2,1)S(1)}, bf16[272,128]{1,0:T(8,128)(2,1)S(1)}, bf16[512,1024]{1,0:T(8,128)(2,1)S(1)}, bf16[512,1024]{1,0:T(8,128)(2,1)S(1)}) custom-call(s32[1]{0:T(128)} %bitcast.place_ref, f32[8,512]{1,0:T(8,128)} %bitcast.11, bf16[512,1024]{1,0:T(8,128)(2,1)} %key_in.1, ...), custom_call_target="tpu_custom_call" | custom-call | tf_op jit(solution)/shard_map/early_states/pallas_call | solution.py:144
  2.4 1.6 %load.1 = (f32[272,128]{1,0:T(8,128)S(1)}, bf16[512,1024]{1,0:T(8,128)(2,1)S(1)}, f32[8,512]{1,0:T(8,128)S(1)}) custom-call(s32[1]{0:T(128)} %bitcast.place_ref, f32[8,512]{1,0:T(8,128)} %bitcast.12, bf16[512,1024]{1,0:T(8,128)(2,1)} %query_in.1, bf16[512,1024]{1,0:T(8,128)(2,1)S(1)} %get-tuple-element.50.key_ref.k_ref, ...), custom_call_target="tpu_custom_call" | custom-call | tf_op jit(solution)/shard_map/load/pallas_call | solution.py:176
  4.0 0.6 collective-permute-start.9
  4.5 2.6 %collective-permute-start.1 = (bf16[272,128]{1,0:T(8,128)(2,1)S(1)}, bf16[272,128]{1,0:T(8,128)(2,1)S(1)}, u32[]{:S(2)}, u32[]{:S(2)}) collective-permute-start(bf16[272,128]{1,0:T(8,128)(2,1)S(1)} %get-tuple-element.63), channel_id=1, source_target_pairs={{0,8},{4,12},{8,0},{12,4},{16,24},{20,28},{24,16},{28,20},{1,9},{5... | collective-permute-start | bytes 208904 | tf_op jit(solution)/shard_map/ppermute | solution.py:599
  7.1 1.4 %collective-permute-start.2 = (bf16[272,128]{1,0:T(8,128)(2,1)S(1)}, bf16[272,128]{1,0:T(8,128)(2,1)S(1)}, u32[]{:S(2)}, u32[]{:S(2)}) collective-permute-start(bf16[272,128]{1,0:T(8,128)(2,1)S(1)} %get-tuple-element.64), channel_id=1, source_target_pairs={{0,12},{4,8},{8,4},{12,0},{16,28},{20,24},{24,20},{28,16},{1,13},{... | collective-permute-start | bytes 208904 | tf_op jit(solution)/shard_map/ppermute | solution.py:599
  8.5 0.2 collective-permute-start
  8.7 1.2 %collective-permute-done.1.refs_2_ = bf16[272,128]{1,0:T(8,128)(2,1)S(1)} collective-permute-done((bf16[272,128]{1,0:T(8,128)(2,1)S(1)}, bf16[272,128]{1,0:T(8,128)(2,1)S(1)}, u32[]{:S(2)}, u32[]{:S(2)}) %collective-permute-start.1) | collective-permute-done | bytes 69664 | tf_op jit(solution)/shard_map/ppermute | solution.py:599
  9.9 2.7 %collective-permute-done.2.refs_3_ = bf16[272,128]{1,0:T(8,128)(2,1)S(1)} collective-permute-done((bf16[272,128]{1,0:T(8,128)(2,1)S(1)}, bf16[272,128]{1,0:T(8,128)(2,1)S(1)}, u32[]{:S(2)}, u32[]{:S(2)}) %collective-permute-start.2) | collective-permute-done | bytes 69664 | tf_op jit(solution)/shard_map/ppermute | solution.py:599
  12.6 1.3 %collective-permute-done.refs_1_ = bf16[272,128]{1,0:T(8,128)(2,1)S(1)} collective-permute-done((bf16[272,128]{1,0:T(8,128)(2,1)S(1)}, bf16[272,128]{1,0:T(8,128)(2,1)S(1)}, u32[]{:S(2)}, u32[]{:S(2)}) %collective-permute-start) | collective-permute-done | bytes 69664 | tf_op jit(solution)/shard_map/ppermute | solution.py:599
  13.9 0.1 gather.1
  14.0 2.7 %collective-permute-start.3 = (bf16[272,128]{1,0:T(8,128)(2,1)S(1)}, bf16[272,128]{1,0:T(8,128)(2,1)S(1)}, u32[]{:S(2)}, u32[]{:S(2)}) collective-permute-start(bf16[272,128]{1,0:T(8,128)(2,1)S(1)} %get-tuple-element.65), channel_id=1, source_target_pairs={{0,16},{4,20},{8,24},{12,28},{16,0},{20,4},{24,8},{28,12},{1,17},{... | collective-permute-start | bytes 208904 | tf_op jit(solution)/shard_map/ppermute | solution.py:599
  16.7 3.8 %collective-permute-done.3.got_ref = bf16[272,128]{1,0:T(8,128)(2,1)S(1)} collective-permute-done((bf16[272,128]{1,0:T(8,128)(2,1)S(1)}, bf16[272,128]{1,0:T(8,128)(2,1)S(1)}, u32[]{:S(2)}, u32[]{:S(2)}) %collective-permute-start.3) | collective-permute-done | bytes 69664 | tf_op jit(solution)/shard_map/ppermute | solution.py:599
  20.4 0.1 enter.1
  20.5 0.7 %collective-permute-start.4 = (bf16[256,128]{1,0:T(8,128)(2,1)S(1)}, bf16[256,128]{1,0:T(8,128)(2,1)S(1)}, u32[]{:S(2)}, u32[]{:S(2)}) collective-permute-start(bf16[256,128]{1,0:T(8,128)(2,1)S(1)} %get-tuple-element.70), channel_id=1, source_target_pairs={{0,4},{4,0},{8,12},{12,8},{16,20},{20,16},{24,28},{28,24},{1,5},{5... | collective-permute-start | bytes 196616 | tf_op jit(solution)/shard_map/ppermute | solution.py:599
  21.2 0.2 collective-permute-start.5
  21.5 0.7 %local.6 = (f32[512,256]{1,0:T(8,128)S(1)}, bf16[512,256]{1,0:T(8,128)(2,1)S(1)}) custom-call(s32[1]{0:T(128)} %bitcast.place_ref, f32[8,512]{1,0:T(8,128)S(1)} %get-tuple-element.53.cum_ref, bf16[512,1024]{1,0:T(8,128)(2,1)S(1)} %get-tuple-element.54.q_ref, bf16[512,1024]{1,0:T(8,128)(2,1)S(1)} %get-tuple-element.50.key_ref.k_ref, ...), custom_call_target="tpu_custom_call" | custom-call | tf_op jit(solution)/shard_map/local/pallas_call | solution.py:401
  22.2 0.7 %local.5 = (f32[512,256]{1,0:T(8,128)S(1)}, bf16[512,256]{1,0:T(8,128)(2,1)S(1)}) custom-call(s32[1]{0:T(128)} %bitcast.place_ref, f32[8,512]{1,0:T(8,128)S(1)} %get-tuple-element.53.cum_ref, bf16[512,1024]{1,0:T(8,128)(2,1)S(1)} %get-tuple-element.54.q_ref, bf16[512,1024]{1,0:T(8,128)(2,1)S(1)} %get-tuple-element.50.key_ref.k_ref, ...), custom_call_target="tpu_custom_call" | custom-call | tf_op jit(solution)/shard_map/local/pallas_call | solution.py:401
  23.0 0.7 %local.4 = (f32[512,256]{1,0:T(8,128)S(1)}, bf16[512,256]{1,0:T(8,128)(2,1)S(1)}) custom-call(s32[1]{0:T(128)} %bitcast.place_ref, f32[8,512]{1,0:T(8,128)S(1)} %get-tuple-element.53.cum_ref, bf16[512,1024]{1,0:T(8,128)(2,1)S(1)} %get-tuple-element.54.q_ref, bf16[512,1024]{1,0:T(8,128)(2,1)S(1)} %get-tuple-element.50.key_ref.k_ref, ...), custom_call_target="tpu_custom_call" | custom-call | tf_op jit(solution)/shard_map/local/pallas_call | solution.py:401
  23.7 1.2 %collective-permute-done.4.refs_7_ = bf16[256,128]{1,0:T(8,128)(2,1)S(1)} collective-permute-done((bf16[256,128]{1,0:T(8,128)(2,1)S(1)}, bf16[256,128]{1,0:T(8,128)(2,1)S(1)}, u32[]{:S(2)}, u32[]{:S(2)}) %collective-permute-start.4) | collective-permute-done | bytes 65568 | tf_op jit(solution)/shard_map/ppermute | solution.py:599
  24.9 0.6 collective-permute-done.5.refs_8_
  25.5 0.4 norm_away.2
  26.0 1.4 %collective-permute-start.6 = (bf16[256,128]{1,0:T(8,128)(2,1)S(1)}, bf16[256,128]{1,0:T(8,128)(2,1)S(1)}, u32[]{:S(2)}, u32[]{:S(2)}) collective-permute-start(bf16[256,128]{1,0:T(8,128)(2,1)S(1)} %get-tuple-element.74), channel_id=1, source_target_pairs={{0,12},{4,8},{8,4},{12,0},{16,28},{20,24},{24,20},{28,16},{1,13},{... | collective-permute-start | bytes 196616 | tf_op jit(solution)/shard_map/ppermute | solution.py:599
  27.4 0.7 %local.7 = (f32[512,256]{1,0:T(8,128)S(1)}, bf16[512,256]{1,0:T(8,128)(2,1)S(1)}) custom-call(s32[1]{0:T(128)} %bitcast.place_ref, f32[8,512]{1,0:T(8,128)S(1)} %get-tuple-element.53.cum_ref, bf16[512,1024]{1,0:T(8,128)(2,1)S(1)} %get-tuple-element.54.q_ref, bf16[512,1024]{1,0:T(8,128)(2,1)S(1)} %get-tuple-element.50.key_ref.k_ref, ...), custom_call_target="tpu_custom_call" | custom-call | tf_op jit(solution)/shard_map/local/pallas_call | solution.py:401
  28.1 3.3 %collective-permute-done.6.refs_2_ = bf16[256,128]{1,0:T(8,128)(2,1)S(1)} collective-permute-done((bf16[256,128]{1,0:T(8,128)(2,1)S(1)}, bf16[256,128]{1,0:T(8,128)(2,1)S(1)}, u32[]{:S(2)}, u32[]{:S(2)}) %collective-permute-start.6) | collective-permute-done | bytes 65568 | tf_op jit(solution)/shard_map/ppermute | solution.py:599
  31.4 0.3 norm_away.3
  31.9 0.3 norm_home.3.two_ref.refs_1_
  32.2 0.5 norm_home.2.one_ref.refs_0_
  32.7 0.6 %begin.1.begun_ref = f32[256,512]{1,0:T(8,128)S(1)} custom-call(s32[1]{0:T(128)} %bitcast.place_ref, bf16[256,768]{1,0:T(8,128)(2,1)S(1)} %norm_home.2.one_ref.refs_0_, bf16[256,256]{1,0:T(8,128)(2,1)S(1)} %norm_home.3.two_ref.refs_1_, bf16[256,768]{1,0:T(8,128)(2,1)S(1)} %collective-permute-done.7.met_ref.refs_2_, bf16[1024,4096]{1,0:T(8,128)(2,1)S(1)} %bitcast.6, ...), custom_call_target="tpu_custom_call" | custom-call | tf_op jit(solution)/shard_map/begin/pallas_call | solution.py:488
  33.4 0.2 complete.1
  33.6 0.7 %project.5 = (f32[128,512]{1,0:T(8,128)S(1)}, bf16[128,512]{1,0:T(8,128)(2,1)S(1)}) custom-call(s32[1]{0:T(128)} %bitcast.place_ref, bf16[256,768]{1,0:T(8,128)(2,1)S(1)} %norm_home.2.one_ref.refs_0_, bf16[256,256]{1,0:T(8,128)(2,1)S(1)} %norm_home.3.two_ref.refs_1_, bf16[256,768]{1,0:T(8,128)(2,1)S(1)} %collective-permute-done.7.met_ref.refs_2_, ...), custom_call_target="tpu_custom_call" | custom-call | tf_op jit(solution)/shard_map/project/pallas_call | solution.py:534
  34.3 1.3 %project.6 = (f32[128,1024]{1,0:T(8,128)S(1)}, bf16[128,1024]{1,0:T(8,128)(2,1)S(1)}) custom-call(s32[1]{0:T(128)} %bitcast.place_ref, bf16[256,768]{1,0:T(8,128)(2,1)S(1)} %norm_home.2.one_ref.refs_0_, bf16[256,256]{1,0:T(8,128)(2,1)S(1)} %norm_home.3.two_ref.refs_1_, bf16[256,768]{1,0:T(8,128)(2,1)S(1)} %collective-permute-done.7.met_ref.refs_2_, ...), custom_call_target="tpu_custom_call" | custom-call | tf_op jit(solution)/shard_map/project/pallas_call | solution.py:534
  35.6 1.6 %collective-permute-start.13 = (bf16[128,1024]{1,0:T(8,128)(2,1)S(1)}, bf16[128,1024]{1,0:T(8,128)(2,1)S(1)}, u32[]{:S(2)}, u32[]{:S(2)}) collective-permute-start(bf16[128,1024]{1,0:T(8,128)(2,1)S(1)} %get-tuple-element.79.refs_6_), channel_id=1, source_target_pairs={{0,2},{1,3},{2,0},{3,1},{4,6},{5,7},{6,4},{7,5},{8,10},{9,11},{10,... | collective-permute-start | bytes 786440 | tf_op jit(solution)/shard_map/ppermute | solution.py:662
  37.2 1.3 %project.7 = (f32[128,1024]{1,0:T(8,128)S(1)}, bf16[128,1024]{1,0:T(8,128)(2,1)S(1)}) custom-call(s32[1]{0:T(128)} %bitcast.place_ref, bf16[256,768]{1,0:T(8,128)(2,1)S(1)} %norm_home.2.one_ref.refs_0_, bf16[256,256]{1,0:T(8,128)(2,1)S(1)} %norm_home.3.two_ref.refs_1_, bf16[256,768]{1,0:T(8,128)(2,1)S(1)} %collective-permute-done.7.met_ref.refs_2_, ...), custom_call_target="tpu_custom_call" | custom-call | tf_op jit(solution)/shard_map/project/pallas_call | solution.py:534
  38.5 0.6 collective-permute-start.12
  39.1 1.0 %project.8 = (f32[128,768]{1,0:T(8,128)S(1)}, bf16[128,768]{1,0:T(8,128)(2,1)S(1)}) custom-call(s32[1]{0:T(128)} %bitcast.place_ref, bf16[256,768]{1,0:T(8,128)(2,1)S(1)} %norm_home.2.one_ref.refs_0_, bf16[256,256]{1,0:T(8,128)(2,1)S(1)} %norm_home.3.two_ref.refs_1_, bf16[256,768]{1,0:T(8,128)(2,1)S(1)} %collective-permute-done.7.met_ref.refs_2_, ...), custom_call_target="tpu_custom_call" | custom-call | tf_op jit(solution)/shard_map/project/pallas_call | solution.py:534
  40.1 1.6 %collective-permute-start.11 = (bf16[128,768]{1,0:T(8,128)(2,1)S(1)}, bf16[128,768]{1,0:T(8,128)(2,1)S(1)}, u32[]{:S(2)}, u32[]{:S(2)}) collective-permute-start(bf16[128,768]{1,0:T(8,128)(2,1)S(1)} %get-tuple-element.81.refs_6_), channel_id=1, source_target_pairs={{0,2},{1,3},{2,0},{3,1},{4,6},{5,7},{6,4},{7,5},{8,10},{9,11},{10,... | collective-permute-start | bytes 589832 | tf_op jit(solution)/shard_map/ppermute | solution.py:662
  41.7 0.5 collective-permute-start.15
  42.2 1.5 %collective-permute-start.14 = (bf16[128,512]{1,0:T(8,128)(2,1)S(1)}, bf16[128,512]{1,0:T(8,128)(2,1)S(1)}, u32[]{:S(2)}, u32[]{:S(2)}) collective-permute-start(bf16[128,512]{1,0:T(8,128)(2,1)S(1)} %get-tuple-element.78.refs_6_), channel_id=1, source_target_pairs={{0,2},{1,3},{2,0},{3,1},{4,6},{5,7},{6,4},{7,5},{8,10},{9,11},{10,... | collective-permute-start | bytes 393224 | tf_op jit(solution)/shard_map/ppermute | solution.py:662
  43.7 0.5 project.9
  44.2 13.3 %collective-permute-done.15.refs_0_ = bf16[128,512]{1,0:T(8,128)(2,1)S(1)} collective-permute-done((bf16[128,512]{1,0:T(8,128)(2,1)S(1)}, bf16[128,512]{1,0:T(8,128)(2,1)S(1)}, u32[]{:S(2)}, u32[]{:S(2)}) %collective-permute-start.15) | collective-permute-done | bytes 131104 | tf_op jit(solution)/shard_map/ppermute | solution.py:662
  57.5 1.5 %collective-permute-start.10 = (bf16[128,256]{1,0:T(8,128)(2,1)S(1)}, bf16[128,256]{1,0:T(8,128)(2,1)S(1)}, u32[]{:S(2)}, u32[]{:S(2)}) collective-permute-start(bf16[128,256]{1,0:T(8,128)(2,1)S(1)} %get-tuple-element.83), channel_id=1, source_target_pairs={{0,2},{1,3},{2,0},{3,1},{4,6},{5,7},{6,4},{7,5},{8,10},{9,11},{10,... | collective-permute-start | bytes 196616 | tf_op jit(solution)/shard_map/ppermute | solution.py:662
  59.0 0.7 %finish.6.refs_1_ = bf16[128,4096]{1,0:T(8,128)(2,1)} custom-call(f32[128,512]{1,0:T(8,128)S(1)} %get-tuple-element.88.own_ref, bf16[128,4096]{1,0:T(8,128)(2,1)S(1)} %copy-done, bf16[128,512]{1,0:T(8,128)(2,1)S(1)} %collective-permute-done.15.refs_0_), custom_call_target="tpu_custom_call" | custom-call | tf_op jit(solution)/shard_map/finish/pallas_call | solution.py:569
  59.8 0.5 collective-permute-done.14.refs_0_
  60.3 0.7 %finish.7.refs_1_ = bf16[128,4096]{1,0:T(8,128)(2,1)} custom-call(f32[128,512]{1,0:T(8,128)S(1)} %get-tuple-element.87.own_ref, bf16[128,4096]{1,0:T(8,128)(2,1)S(1)} %copy-done, bf16[128,512]{1,0:T(8,128)(2,1)S(1)} %collective-permute-done.14.refs_0_, bf16[128,4096]{1,0:T(8,128)(2,1)} %finish.6.refs_1_), custom_call_target="tpu_custom_call", output_to_operand_aliasing={{}: (3, {})} | custom-call | tf_op jit(solution)/shard_map/finish/pallas_call | solution.py:569
  61.1 0.8 %finish.8.refs_1_ = bf16[128,4096]{1,0:T(8,128)(2,1)} custom-call(f32[128,1024]{1,0:T(8,128)S(1)} %get-tuple-element.86.own_ref, bf16[128,4096]{1,0:T(8,128)(2,1)S(1)} %copy-done, bf16[128,1024]{1,0:T(8,128)(2,1)S(1)} %collective-permute-done.13.refs_0_, bf16[128,4096]{1,0:T(8,128)(2,1)} %finish.7.refs_1_), custom_call_target="tpu_custom_call", output_to_operand_aliasing={{}: (3, {})} | custom-call | tf_op jit(solution)/shard_map/finish/pallas_call | solution.py:569
  61.9 0.8 %finish.9.refs_1_ = bf16[128,4096]{1,0:T(8,128)(2,1)} custom-call(f32[128,1024]{1,0:T(8,128)S(1)} %get-tuple-element.85.own_ref, bf16[128,4096]{1,0:T(8,128)(2,1)S(1)} %copy-done, bf16[128,1024]{1,0:T(8,128)(2,1)S(1)} %collective-permute-done.12.refs_0_, bf16[128,4096]{1,0:T(8,128)(2,1)} %finish.8.refs_1_), custom_call_target="tpu_custom_call", output_to_operand_aliasing={{}: (3, {})} | custom-call | tf_op jit(solution)/shard_map/finish/pallas_call | solution.py:569
  62.7 0.8 %finish.10.refs_1_ = bf16[128,4096]{1,0:T(8,128)(2,1)} custom-call(f32[128,768]{1,0:T(8,128)S(1)} %get-tuple-element.84.own_ref, bf16[128,4096]{1,0:T(8,128)(2,1)S(1)} %copy-done, bf16[128,768]{1,0:T(8,128)(2,1)S(1)} %collective-permute-done.11.refs_0_, bf16[128,4096]{1,0:T(8,128)(2,1)} %finish.9.refs_1_), custom_call_target="tpu_custom_call", output_to_operand_aliasing={{}: (3, {})} | custom-call | tf_op jit(solution)/shard_map/finish/pallas_call | solution.py:569
  63.5 0.7 %finish.11 = bf16[128,4096]{1,0:T(8,128)(2,1)} custom-call(f32[128,256]{1,0:T(8,128)S(1)} %get-tuple-element.82.own_ref, bf16[128,4096]{1,0:T(8,128)(2,1)S(1)} %copy-done, bf16[128,256]{1,0:T(8,128)(2,1)S(1)} %collective-permute-done.10.refs_0_, bf16[128,4096]{1,0:T(8,128)(2,1)} %finish.10.refs_1_), custom_call_target="tpu_custom_call", output_to_operand_aliasing={{}: (3, {})} | custom-call | tf_op jit(solution)/shard_map/finish/pallas_call | solution.py:569
  (18 shorter events, 0.2 us)
Async XLA Ops:
  0.0 25.5 %copy-start.1 = (f32[1024]{0:T(1024)S(1)}, f32[1024]{0:T(1024)}, u32[]{:S(2)}) copy-start(f32[1024]{0:T(1024)} %param.11) | copy-start | bytes 12292
  4.0 28.7 %collective-permute-start.9 = (bf16[1024,4096]{1,0:T(8,128)(2,1)}, bf16[1024,4096]{1,0:T(8,128)(2,1)S(1)}, u32[]{:S(2)}, u32[]{:S(2)}) collective-permute-start(bf16[1024,4096]{1,0:T(8,128)(2,1)} %refs_4_.4), channel_id=1, source_target_pairs={{0,1},{1,0},{2,3},{3,2},{4,5},{5,4},{6,7},{7,6},{8,9},{9,8},{10,11... | collective-permute-start | bytes 25165832 | tf_op jit(solution)/shard_map/ppermute | solution.py:608
  4.5 5.4 %collective-permute-start.1 = (bf16[272,128]{1,0:T(8,128)(2,1)S(1)}, bf16[272,128]{1,0:T(8,128)(2,1)S(1)}, u32[]{:S(2)}, u32[]{:S(2)}) collective-permute-start(bf16[272,128]{1,0:T(8,128)(2,1)S(1)} %get-tuple-element.63), channel_id=1, source_target_pairs={{0,8},{4,12},{8,0},{12,4},{16,24},{20,28},{24,16},{28,20},{1,9},{5... | collective-permute-start | bytes 208904 | tf_op jit(solution)/shard_map/ppermute | solution.py:599
  7.1 5.5 %collective-permute-start.2 = (bf16[272,128]{1,0:T(8,128)(2,1)S(1)}, bf16[272,128]{1,0:T(8,128)(2,1)S(1)}, u32[]{:S(2)}, u32[]{:S(2)}) collective-permute-start(bf16[272,128]{1,0:T(8,128)(2,1)S(1)} %get-tuple-element.64), channel_id=1, source_target_pairs={{0,12},{4,8},{8,4},{12,0},{16,28},{20,24},{24,20},{28,16},{1,13},{... | collective-permute-start | bytes 208904 | tf_op jit(solution)/shard_map/ppermute | solution.py:599
  8.5 5.3 %collective-permute-start = (bf16[272,128]{1,0:T(8,128)(2,1)S(1)}, bf16[272,128]{1,0:T(8,128)(2,1)S(1)}, u32[]{:S(2)}, u32[]{:S(2)}) collective-permute-start(bf16[272,128]{1,0:T(8,128)(2,1)S(1)} %get-tuple-element.52.hold_ref), channel_id=1, source_target_pairs={{0,4},{4,0},{8,12},{12,8},{16,20},{20,16},{24,28},{28,24},{1,5},{5... | collective-permute-start | bytes 208904 | tf_op jit(solution)/shard_map/ppermute | solution.py:599
  14.0 6.4 %collective-permute-start.3 = (bf16[272,128]{1,0:T(8,128)(2,1)S(1)}, bf16[272,128]{1,0:T(8,128)(2,1)S(1)}, u32[]{:S(2)}, u32[]{:S(2)}) collective-permute-start(bf16[272,128]{1,0:T(8,128)(2,1)S(1)} %get-tuple-element.65), channel_id=1, source_target_pairs={{0,16},{4,20},{8,24},{12,28},{16,0},{20,4},{24,8},{28,12},{1,17},{... | collective-permute-start | bytes 208904 | tf_op jit(solution)/shard_map/ppermute | solution.py:599
  20.5 4.3 %collective-permute-start.4 = (bf16[256,128]{1,0:T(8,128)(2,1)S(1)}, bf16[256,128]{1,0:T(8,128)(2,1)S(1)}, u32[]{:S(2)}, u32[]{:S(2)}) collective-permute-start(bf16[256,128]{1,0:T(8,128)(2,1)S(1)} %get-tuple-element.70), channel_id=1, source_target_pairs={{0,4},{4,0},{8,12},{12,8},{16,20},{20,16},{24,28},{28,24},{1,5},{5... | collective-permute-start | bytes 196616 | tf_op jit(solution)/shard_map/ppermute | solution.py:599
  21.2 4.3 %collective-permute-start.5 = (bf16[256,128]{1,0:T(8,128)(2,1)S(1)}, bf16[256,128]{1,0:T(8,128)(2,1)S(1)}, u32[]{:S(2)}, u32[]{:S(2)}) collective-permute-start(bf16[256,128]{1,0:T(8,128)(2,1)S(1)} %get-tuple-element.71), channel_id=1, source_target_pairs={{0,8},{4,12},{8,0},{12,4},{16,24},{20,28},{24,16},{28,20},{1,9},{5... | collective-permute-start | bytes 196616 | tf_op jit(solution)/shard_map/ppermute | solution.py:599
  22.2 10.5 %slice-start = ((s8[8388608]{0:T(1024)(128)(4,1)}), s8[4194304]{0:T(1024)(128)(4,1)S(1)}, s32[]{:S(2)}) async-start(s8[8388608]{0:T(1024)(128)(4,1)} %bitcast.5), calls=%async_computation | async-start | bytes 8388608
  25.5 7.2 %slice-start.1 = ((s8[8388608]{0:T(1024)(128)(4,1)}), s8[4194304]{0:T(1024)(128)(4,1)S(1)}, s32[]{:S(2)}) async-start(s8[8388608]{0:T(1024)(128)(4,1)} %bitcast.5), calls=%async_computation.1 | async-start | bytes 8388608
  26.0 6.7 %collective-permute-start.7 = (bf16[256,768]{1,0:T(8,128)(2,1)S(1)}, bf16[256,768]{1,0:T(8,128)(2,1)S(1)}, u32[]{:S(2)}, u32[]{:S(2)}) collective-permute-start(bf16[256,768]{1,0:T(8,128)(2,1)S(1)} %norm_away.2), channel_id=1, source_target_pairs={{0,1},{1,0},{2,3},{3,2},{4,5},{5,4},{6,7},{7,6},{8,9},{9,8},{10,11... | collective-permute-start | bytes 1179656 | tf_op jit(solution)/shard_map/ppermute | solution.py:639
  26.0 5.4 %collective-permute-start.6 = (bf16[256,128]{1,0:T(8,128)(2,1)S(1)}, bf16[256,128]{1,0:T(8,128)(2,1)S(1)}, u32[]{:S(2)}, u32[]{:S(2)}) collective-permute-start(bf16[256,128]{1,0:T(8,128)(2,1)S(1)} %get-tuple-element.74), channel_id=1, source_target_pairs={{0,12},{4,8},{8,4},{12,0},{16,28},{20,24},{24,20},{28,16},{1,13},{... | collective-permute-start | bytes 196616 | tf_op jit(solution)/shard_map/ppermute | solution.py:599
  31.8 1.6 %collective-permute-start.8 = (bf16[256,256]{1,0:T(8,128)(2,1)S(1)}, bf16[256,256]{1,0:T(8,128)(2,1)S(1)}, u32[]{:S(2)}, u32[]{:S(2)}) collective-permute-start(bf16[256,256]{1,0:T(8,128)(2,1)S(1)} %norm_away.3), channel_id=1, source_target_pairs={{0,1},{1,0},{2,3},{3,2},{4,5},{5,4},{6,7},{7,6},{8,9},{9,8},{10,11... | collective-permute-start | bytes 393224 | tf_op jit(solution)/shard_map/ppermute | solution.py:639
  35.6 25.4 %collective-permute-start.13 = (bf16[128,1024]{1,0:T(8,128)(2,1)S(1)}, bf16[128,1024]{1,0:T(8,128)(2,1)S(1)}, u32[]{:S(2)}, u32[]{:S(2)}) collective-permute-start(bf16[128,1024]{1,0:T(8,128)(2,1)S(1)} %get-tuple-element.79.refs_6_), channel_id=1, source_target_pairs={{0,2},{1,3},{2,0},{3,1},{4,6},{5,7},{6,4},{7,5},{8,10},{9,11},{10,... | collective-permute-start | bytes 786440 | tf_op jit(solution)/shard_map/ppermute | solution.py:662
  38.5 23.4 %collective-permute-start.12 = (bf16[128,1024]{1,0:T(8,128)(2,1)S(1)}, bf16[128,1024]{1,0:T(8,128)(2,1)S(1)}, u32[]{:S(2)}, u32[]{:S(2)}) collective-permute-start(bf16[128,1024]{1,0:T(8,128)(2,1)S(1)} %get-tuple-element.80.refs_6_), channel_id=1, source_target_pairs={{0,2},{1,3},{2,0},{3,1},{4,6},{5,7},{6,4},{7,5},{8,10},{9,11},{10,... | collective-permute-start | bytes 786440 | tf_op jit(solution)/shard_map/ppermute | solution.py:662
  40.1 19.0 %copy-start = (bf16[128,4096]{1,0:T(8,128)(2,1)S(1)}, bf16[128,4096]{1,0:T(8,128)(2,1)}, u32[]{:S(2)}) copy-start(bf16[128,4096]{1,0:T(8,128)(2,1)} %residual_ref.11) | copy-start | bytes 3145732
  40.1 22.7 %collective-permute-start.11 = (bf16[128,768]{1,0:T(8,128)(2,1)S(1)}, bf16[128,768]{1,0:T(8,128)(2,1)S(1)}, u32[]{:S(2)}, u32[]{:S(2)}) collective-permute-start(bf16[128,768]{1,0:T(8,128)(2,1)S(1)} %get-tuple-element.81.refs_6_), channel_id=1, source_target_pairs={{0,2},{1,3},{2,0},{3,1},{4,6},{5,7},{6,4},{7,5},{8,10},{9,11},{10,... | collective-permute-start | bytes 589832 | tf_op jit(solution)/shard_map/ppermute | solution.py:662
  41.7 15.8 %collective-permute-start.15 = (bf16[128,512]{1,0:T(8,128)(2,1)S(1)}, bf16[128,512]{1,0:T(8,128)(2,1)S(1)}, u32[]{:S(2)}, u32[]{:S(2)}) collective-permute-start(bf16[128,512]{1,0:T(8,128)(2,1)S(1)} %get-tuple-element.77.refs_6_), channel_id=1, source_target_pairs={{0,2},{1,3},{2,0},{3,1},{4,6},{5,7},{6,4},{7,5},{8,10},{9,11},{10,... | collective-permute-start | bytes 393224 | tf_op jit(solution)/shard_map/ppermute | solution.py:662
  42.2 18.1 %collective-permute-start.14 = (bf16[128,512]{1,0:T(8,128)(2,1)S(1)}, bf16[128,512]{1,0:T(8,128)(2,1)S(1)}, u32[]{:S(2)}, u32[]{:S(2)}) collective-permute-start(bf16[128,512]{1,0:T(8,128)(2,1)S(1)} %get-tuple-element.78.refs_6_), channel_id=1, source_target_pairs={{0,2},{1,3},{2,0},{3,1},{4,6},{5,7},{6,4},{7,5},{8,10},{9,11},{10,... | collective-permute-start | bytes 393224 | tf_op jit(solution)/shard_map/ppermute | solution.py:662
  57.5 6.0 %collective-permute-start.10 = (bf16[128,256]{1,0:T(8,128)(2,1)S(1)}, bf16[128,256]{1,0:T(8,128)(2,1)S(1)}, u32[]{:S(2)}, u32[]{:S(2)}) collective-permute-start(bf16[128,256]{1,0:T(8,128)(2,1)S(1)} %get-tuple-element.83), channel_id=1, source_target_pairs={{0,2},{1,3},{2,0},{3,1},{4,6},{5,7},{6,4},{7,5},{8,10},{9,11},{10,... | collective-permute-start | bytes 196616 | tf_op jit(solution)/shard_map/ppermute | solution.py:662

commit v3 on v2

--- a/solution.py
+++ b/solution.py
@@ -82,6 +82,10 @@
     return held((count * width + 2 * pad_rows(count), width), kind)
 
 
+def order_of(size):
+    return [0, *range(size - 1, 0, -1)]
+
+
 def part_of(place_ref, size, away):
     return (place_ref[0] & (size - 1)) ^ away
 
@@ -125,18 +129,13 @@
         copy.start()
     logd.wait()
     put_sums(logd_ref, cum_ref, weight_ref)
-    for copy in keys:
+    for copy in keys + values:
         copy.wait()
-    parts = [part_of(place_ref, size, away) for away in range(1, size)]
-    spans = [part_columns(place_ref, size, away, count * width) for away in range(1, size)]
-    keyed = [
-        turned_keys(part, count, width, key_ref[:, here], weight_ref)
-        for part, here in zip(parts, spans)
-    ]
-    for copy in values:
-        copy.wait()
-    for part, here, turned, pay_ref in zip(parts, spans, keyed, pay_refs):
-        put_states(part, count, width, turned, value_ref[:, here], cum_ref, pay_ref)
+    for away in range(1, size):
+        part = part_of(place_ref, size, away)
+        here = part_columns(place_ref, size, away, count * width)
+        turned = turned_keys(part, count, width, key_ref[:, here], weight_ref)
+        put_states(part, count, width, turned, value_ref[:, here], cum_ref, pay_refs[away - 1])
 
 
 def early_states(place, logd, key, value, size, count, width):
@@ -476,10 +475,10 @@
 
 
 def begin_kernel(size, place_ref, one_ref, two_ref, met_ref, near_ref, far_ref, out_ref):
-    early = range(size - 1)
-    terms = [(one_ref, away, away, near_ref) for away in early]
-    terms += [(met_ref, away, away, far_ref) for away in early]
-    terms += [(two_ref, 0, size - 1, near_ref)]
+    *early, last = order_of(size)
+    terms = [(one_ref, at, away, near_ref) for at, away in enumerate(early)]
+    terms += [(met_ref, at, away, far_ref) for at, away in enumerate(early)]
+    terms += [(two_ref, 0, last, near_ref)]
     out_ref[...] = summed(size, place_ref, terms, slice(0, out_ref.shape[1]))
 
 
@@ -497,7 +496,7 @@
 
 def complete_kernel(block, size, place_ref, begun_ref, two_ref, far_ref, own_ref, away_ref):
     span = slice(0, own_ref.shape[1])
-    total = summed(size, place_ref, [(two_ref, 0, size - 1, far_ref)], span, begun_ref[...])
+    total = summed(size, place_ref, [(two_ref, 0, order_of(size)[-1], far_ref)], span, begun_ref[...])
     own_ref[...] = total[:block]
     away_ref[...] = total[block:].astype(away_ref.dtype)
 
@@ -518,8 +517,9 @@
     own_ref, away_ref = refs[-2:]
     terms = []
     for one_ref, two_ref, weight_ref in ((refs[0], refs[1], refs[4]), (refs[2], refs[3], refs[5])):
-        terms += [(one_ref, away, away, weight_ref) for away in range(size - 1)]
-        terms += [(two_ref, 0, size - 1, weight_ref)]
+        *early, last = order_of(size)
+        terms += [(one_ref, at, away, weight_ref) for at, away in enumerate(early)]
+        terms += [(two_ref, 0, last, weight_ref)]
     for i in range(own_ref.shape[1] // tile):
         here = slice(i * tile, (i + 1) * tile)
         span = slice(first + i * tile, first + (i + 1) * tile)
@@ -630,7 +630,7 @@
 
     gain = norm_gain.reshape(heads, width)
     home, other = [], []
-    for which in (range(size - 1), range(size - 1, size)):
+    for which in (order_of(size)[:-1], order_of(size)[-1:]):
         args = (
             tuple(which), (place, chip, core), gain, insides, queries, entering,
             size, count, width, chips, block,

time: 64.4 us -> 63.6 us (0.988)
  waiting for transfers between devices: 28 us -> 26.2 us
  starting transfers between devices: 17.1 us -> 18.3 us
    ppermute x7, waiting for transfers between devices: 14.1 us -> 12.3 us  [swap(): return lax.ppermute(x, 'ctx', [(i, i ^ bit) for i in range(blocks)])]
    ppermute x7, starting transfers between devices: 9.12 us -> 10.3 us  [swap(): return lax.ppermute(x, 'ctx', [(i, i ^ bit) for i in range(blocks)])]
  transfers between devices with their start and end apart: 16 -> 16, of which waited for: 9 -> 8; matrix products, arithmetic and copies ran while one was open for 0% -> 0% of each run, Pallas kernels for 19% -> 19%
where the time goes in v3:
time: 63.6 us; the launch traced here: 63.4 us
  waiting for transfers between devices  26.2 us (41%)
  Pallas kernels  18.6 us (29%)
  starting transfers between devices  18.3 us (29%)
    ppermute x6, waiting for transfers between devices, shards(): got.append(lax.ppermute(piece, 'exp', perm))  13.9 us
    ppermute x7, waiting for transfers between devices, swap(): return lax.ppermute(x, 'ctx', [(i, i ^ bit) for i in range(blocks)])  12.3 us
    ppermute x7, starting transfers between devices, swap(): return lax.ppermute(x, 'ctx', [(i, i ^ bit) for i in range(blocks)])  10.3 us
    ppermute x6, starting transfers between devices, shards(): got.append(lax.ppermute(piece, 'exp', perm))  7.26 us
    pallas_call x5, Pallas kernels, project(): pl.pallas_call(functools.partial(project_kernel, block, first, tile, size...  4.72 us
    pallas_call x6, Pallas kernels, finish(): pl.pallas_call(functools.partial(finish_kernel, first, len(parts)), in_sp...  4.55 us
    pallas_call x4, Pallas kernels, local(): pl.pallas_call(functools.partial(local_kernel, size, count, width, away),...  2.9 us
    pallas_call x1, Pallas kernels, early_states(): pl.pallas_call(functools.partial(early_kernel, size, count, width), in_sp...  2.17 us
  transfers between devices with their start and end apart: 16, of which 8 were waited for; matrix products, arithmetic and copies ran while one was open for 0% of the time, Pallas kernels for 19%

profile of v3, /device:TPU:0, one launch (start us, length us, event | category | flops | bytes accessed | tf_op | source)
XLA Modules:
  0.0 63.4 jit_solution(604510854265409750)
XLA Ops:
  0.0 2.2 %early_states.1 = (bf16[272,128]{1,0:T(8,128)(2,1)S(1)}, bf16[272,128]{1,0:T(8,128)(2,1)S(1)}, bf16[272,128]{1,0:T(8,128)(2,1)S(1)}, bf16[512,1024]{1,0:T(8,128)(2,1)S(1)}, bf16[512,1024]{1,0:T(8,128)(2,1)S(1)}) custom-call(s32[1]{0:T(128)} %bitcast.place_ref, f32[8,512]{1,0:T(8,128)} %bitcast.11, bf16[512,1024]{1,0:T(8,128)(2,1)} %key_in.1, ...), custom_call_target="tpu_custom_call" | custom-call | tf_op jit(solution)/shard_map/early_states/pallas_call | solution.py:143
  2.2 1.6 %load.1 = (f32[272,128]{1,0:T(8,128)S(1)}, bf16[512,1024]{1,0:T(8,128)(2,1)S(1)}, f32[8,512]{1,0:T(8,128)S(1)}) custom-call(s32[1]{0:T(128)} %bitcast.place_ref, f32[8,512]{1,0:T(8,128)} %bitcast.12, bf16[512,1024]{1,0:T(8,128)(2,1)} %query_in.1, bf16[512,1024]{1,0:T(8,128)(2,1)S(1)} %get-tuple-element.50.key_ref.k_ref, ...), custom_call_target="tpu_custom_call" | custom-call | tf_op jit(solution)/shard_map/load/pallas_call | solution.py:175
  3.8 0.6 collective-permute-start.9
  4.3 2.7 %collective-permute-start.1 = (bf16[272,128]{1,0:T(8,128)(2,1)S(1)}, bf16[272,128]{1,0:T(8,128)(2,1)S(1)}, u32[]{:S(2)}, u32[]{:S(2)}) collective-permute-start(bf16[272,128]{1,0:T(8,128)(2,1)S(1)} %get-tuple-element.63), channel_id=1, source_target_pairs={{0,8},{4,12},{8,0},{12,4},{16,24},{20,28},{24,16},{28,20},{1,9},{5... | collective-permute-start | bytes 208904 | tf_op jit(solution)/shard_map/ppermute | solution.py:599
  7.0 1.4 %collective-permute-start.2 = (bf16[272,128]{1,0:T(8,128)(2,1)S(1)}, bf16[272,128]{1,0:T(8,128)(2,1)S(1)}, u32[]{:S(2)}, u32[]{:S(2)}) collective-permute-start(bf16[272,128]{1,0:T(8,128)(2,1)S(1)} %get-tuple-element.64), channel_id=1, source_target_pairs={{0,12},{4,8},{8,4},{12,0},{16,28},{20,24},{24,20},{28,16},{1,13},{... | collective-permute-start | bytes 208904 | tf_op jit(solution)/shard_map/ppermute | solution.py:599
  8.3 0.2 collective-permute-start
  8.5 1.2 %collective-permute-done.1.refs_2_ = bf16[272,128]{1,0:T(8,128)(2,1)S(1)} collective-permute-done((bf16[272,128]{1,0:T(8,128)(2,1)S(1)}, bf16[272,128]{1,0:T(8,128)(2,1)S(1)}, u32[]{:S(2)}, u32[]{:S(2)}) %collective-permute-start.1) | collective-permute-done | bytes 69664 | tf_op jit(solution)/shard_map/ppermute | solution.py:599
  9.7 2.7 %collective-permute-done.2.refs_3_ = bf16[272,128]{1,0:T(8,128)(2,1)S(1)} collective-permute-done((bf16[272,128]{1,0:T(8,128)(2,1)S(1)}, bf16[272,128]{1,0:T(8,128)(2,1)S(1)}, u32[]{:S(2)}, u32[]{:S(2)}) %collective-permute-start.2) | collective-permute-done | bytes 69664 | tf_op jit(solution)/shard_map/ppermute | solution.py:599
  12.4 1.3 %collective-permute-done.refs_1_ = bf16[272,128]{1,0:T(8,128)(2,1)S(1)} collective-permute-done((bf16[272,128]{1,0:T(8,128)(2,1)S(1)}, bf16[272,128]{1,0:T(8,128)(2,1)S(1)}, u32[]{:S(2)}, u32[]{:S(2)}) %collective-permute-start) | collective-permute-done | bytes 69664 | tf_op jit(solution)/shard_map/ppermute | solution.py:599
  13.7 0.1 gather.1
  13.8 2.7 %collective-permute-start.3 = (bf16[272,128]{1,0:T(8,128)(2,1)S(1)}, bf16[272,128]{1,0:T(8,128)(2,1)S(1)}, u32[]{:S(2)}, u32[]{:S(2)}) collective-permute-start(bf16[272,128]{1,0:T(8,128)(2,1)S(1)} %get-tuple-element.65), channel_id=1, source_target_pairs={{0,16},{4,20},{8,24},{12,28},{16,0},{20,4},{24,8},{28,12},{1,17},{... | collective-permute-start | bytes 208904 | tf_op jit(solution)/shard_map/ppermute | solution.py:599
  16.5 3.8 %collective-permute-done.3.got_ref = bf16[272,128]{1,0:T(8,128)(2,1)S(1)} collective-permute-done((bf16[272,128]{1,0:T(8,128)(2,1)S(1)}, bf16[272,128]{1,0:T(8,128)(2,1)S(1)}, u32[]{:S(2)}, u32[]{:S(2)}) %collective-permute-start.3) | collective-permute-done | bytes 69664 | tf_op jit(solution)/shard_map/ppermute | solution.py:599
  20.3 0.1 enter.1
  20.4 0.4 collective-permute-start.4
  20.7 1.8 %collective-permute-start.5 = (bf16[256,128]{1,0:T(8,128)(2,1)S(1)}, bf16[256,128]{1,0:T(8,128)(2,1)S(1)}, u32[]{:S(2)}, u32[]{:S(2)}) collective-permute-start(bf16[256,128]{1,0:T(8,128)(2,1)S(1)} %get-tuple-element.71), channel_id=1, source_target_pairs={{0,8},{4,12},{8,0},{12,4},{16,24},{20,28},{24,16},{28,20},{1,9},{5... | collective-permute-start | bytes 196616 | tf_op jit(solution)/shard_map/ppermute | solution.py:599
  22.5 0.7 %local.6 = (f32[512,256]{1,0:T(8,128)S(1)}, bf16[512,256]{1,0:T(8,128)(2,1)S(1)}) custom-call(s32[1]{0:T(128)} %bitcast.place_ref, f32[8,512]{1,0:T(8,128)S(1)} %get-tuple-element.53.cum_ref, bf16[512,1024]{1,0:T(8,128)(2,1)S(1)} %get-tuple-element.54.q_ref, bf16[512,1024]{1,0:T(8,128)(2,1)S(1)} %get-tuple-element.50.key_ref.k_ref, ...), custom_call_target="tpu_custom_call" | custom-call | tf_op jit(solution)/shard_map/local/pallas_call | solution.py:400
  23.3 0.7 %local.5 = (f32[512,256]{1,0:T(8,128)S(1)}, bf16[512,256]{1,0:T(8,128)(2,1)S(1)}) custom-call(s32[1]{0:T(128)} %bitcast.place_ref, f32[8,512]{1,0:T(8,128)S(1)} %get-tuple-element.53.cum_ref, bf16[512,1024]{1,0:T(8,128)(2,1)S(1)} %get-tuple-element.54.q_ref, bf16[512,1024]{1,0:T(8,128)(2,1)S(1)} %get-tuple-element.50.key_ref.k_ref, ...), custom_call_target="tpu_custom_call" | custom-call | tf_op jit(solution)/shard_map/local/pallas_call | solution.py:400
  24.0 0.7 %local.4 = (f32[512,256]{1,0:T(8,128)S(1)}, bf16[512,256]{1,0:T(8,128)(2,1)S(1)}) custom-call(s32[1]{0:T(128)} %bitcast.place_ref, f32[8,512]{1,0:T(8,128)S(1)} %get-tuple-element.53.cum_ref, bf16[512,1024]{1,0:T(8,128)(2,1)S(1)} %get-tuple-element.54.q_ref, bf16[512,1024]{1,0:T(8,128)(2,1)S(1)} %get-tuple-element.50.key_ref.k_ref, ...), custom_call_target="tpu_custom_call" | custom-call | tf_op jit(solution)/shard_map/local/pallas_call | solution.py:400
  24.7 0.9 %collective-permute-done.4.refs_7_ = bf16[256,128]{1,0:T(8,128)(2,1)S(1)} collective-permute-done((bf16[256,128]{1,0:T(8,128)(2,1)S(1)}, bf16[256,128]{1,0:T(8,128)(2,1)S(1)}, u32[]{:S(2)}, u32[]{:S(2)}) %collective-permute-start.4) | collective-permute-done | bytes 65568 | tf_op jit(solution)/shard_map/ppermute | solution.py:599
  25.6 0.5 norm_away.2
  26.1 0.1 collective-permute-start.7
  26.2 1.3 %collective-permute-start.6 = (bf16[256,128]{1,0:T(8,128)(2,1)S(1)}, bf16[256,128]{1,0:T(8,128)(2,1)S(1)}, u32[]{:S(2)}, u32[]{:S(2)}) collective-permute-start(bf16[256,128]{1,0:T(8,128)(2,1)S(1)} %get-tuple-element.74), channel_id=1, source_target_pairs={{0,4},{4,0},{8,12},{12,8},{16,20},{20,16},{24,28},{28,24},{1,5},{5... | collective-permute-start | bytes 196616 | tf_op jit(solution)/shard_map/ppermute | solution.py:599
  27.5 0.7 %local.7 = (f32[512,256]{1,0:T(8,128)S(1)}, bf16[512,256]{1,0:T(8,128)(2,1)S(1)}) custom-call(s32[1]{0:T(128)} %bitcast.place_ref, f32[8,512]{1,0:T(8,128)S(1)} %get-tuple-element.53.cum_ref, bf16[512,1024]{1,0:T(8,128)(2,1)S(1)} %get-tuple-element.54.q_ref, bf16[512,1024]{1,0:T(8,128)(2,1)S(1)} %get-tuple-element.50.key_ref.k_ref, ...), custom_call_target="tpu_custom_call" | custom-call | tf_op jit(solution)/shard_map/local/pallas_call | solution.py:400
  28.2 2.4 %collective-permute-done.6.refs_2_ = bf16[256,128]{1,0:T(8,128)(2,1)S(1)} collective-permute-done((bf16[256,128]{1,0:T(8,128)(2,1)S(1)}, bf16[256,128]{1,0:T(8,128)(2,1)S(1)}, u32[]{:S(2)}, u32[]{:S(2)}) %collective-permute-start.6) | collective-permute-done | bytes 65568 | tf_op jit(solution)/shard_map/ppermute | solution.py:599
  30.7 0.3 norm_away.3
  31.1 0.3 norm_home.3.two_ref.refs_1_
  31.4 0.5 norm_home.2.one_ref.refs_0_
  31.9 0.6 %begin.1.begun_ref = f32[256,512]{1,0:T(8,128)S(1)} custom-call(s32[1]{0:T(128)} %bitcast.place_ref, bf16[256,768]{1,0:T(8,128)(2,1)S(1)} %norm_home.2.one_ref.refs_0_, bf16[256,256]{1,0:T(8,128)(2,1)S(1)} %norm_home.3.two_ref.refs_1_, bf16[256,768]{1,0:T(8,128)(2,1)S(1)} %collective-permute-done.7.met_ref.refs_2_, bf16[1024,4096]{1,0:T(8,128)(2,1)S(1)} %bitcast.6, ...), custom_call_target="tpu_custom_call" | custom-call | tf_op jit(solution)/shard_map/begin/pallas_call | solution.py:487
  32.6 0.2 complete.1
  32.8 0.7 %project.5 = (f32[128,512]{1,0:T(8,128)S(1)}, bf16[128,512]{1,0:T(8,128)(2,1)S(1)}) custom-call(s32[1]{0:T(128)} %bitcast.place_ref, bf16[256,768]{1,0:T(8,128)(2,1)S(1)} %norm_home.2.one_ref.refs_0_, bf16[256,256]{1,0:T(8,128)(2,1)S(1)} %norm_home.3.two_ref.refs_1_, bf16[256,768]{1,0:T(8,128)(2,1)S(1)} %collective-permute-done.7.met_ref.refs_2_, ...), custom_call_target="tpu_custom_call" | custom-call | tf_op jit(solution)/shard_map/project/pallas_call | solution.py:534
  33.6 1.3 %project.6 = (f32[128,1024]{1,0:T(8,128)S(1)}, bf16[128,1024]{1,0:T(8,128)(2,1)S(1)}) custom-call(s32[1]{0:T(128)} %bitcast.place_ref, bf16[256,768]{1,0:T(8,128)(2,1)S(1)} %norm_home.2.one_ref.refs_0_, bf16[256,256]{1,0:T(8,128)(2,1)S(1)} %norm_home.3.two_ref.refs_1_, bf16[256,768]{1,0:T(8,128)(2,1)S(1)} %collective-permute-done.7.met_ref.refs_2_, ...), custom_call_target="tpu_custom_call" | custom-call | tf_op jit(solution)/shard_map/project/pallas_call | solution.py:534
  34.8 1.6 %collective-permute-start.13 = (bf16[128,1024]{1,0:T(8,128)(2,1)S(1)}, bf16[128,1024]{1,0:T(8,128)(2,1)S(1)}, u32[]{:S(2)}, u32[]{:S(2)}) collective-permute-start(bf16[128,1024]{1,0:T(8,128)(2,1)S(1)} %get-tuple-element.79.refs_6_), channel_id=1, source_target_pairs={{0,2},{1,3},{2,0},{3,1},{4,6},{5,7},{6,4},{7,5},{8,10},{9,11},{10,... | collective-permute-start | bytes 786440 | tf_op jit(solution)/shard_map/ppermute | solution.py:662
  36.4 1.3 %project.7 = (f32[128,1024]{1,0:T(8,128)S(1)}, bf16[128,1024]{1,0:T(8,128)(2,1)S(1)}) custom-call(s32[1]{0:T(128)} %bitcast.place_ref, bf16[256,768]{1,0:T(8,128)(2,1)S(1)} %norm_home.2.one_ref.refs_0_, bf16[256,256]{1,0:T(8,128)(2,1)S(1)} %norm_home.3.two_ref.refs_1_, bf16[256,768]{1,0:T(8,128)(2,1)S(1)} %collective-permute-done.7.met_ref.refs_2_, ...), custom_call_target="tpu_custom_call" | custom-call | tf_op jit(solution)/shard_map/project/pallas_call | solution.py:534
  37.7 0.6 collective-permute-start.12
  38.3 1.0 %project.8 = (f32[128,768]{1,0:T(8,128)S(1)}, bf16[128,768]{1,0:T(8,128)(2,1)S(1)}) custom-call(s32[1]{0:T(128)} %bitcast.place_ref, bf16[256,768]{1,0:T(8,128)(2,1)S(1)} %norm_home.2.one_ref.refs_0_, bf16[256,256]{1,0:T(8,128)(2,1)S(1)} %norm_home.3.two_ref.refs_1_, bf16[256,768]{1,0:T(8,128)(2,1)S(1)} %collective-permute-done.7.met_ref.refs_2_, ...), custom_call_target="tpu_custom_call" | custom-call | tf_op jit(solution)/shard_map/project/pallas_call | solution.py:534
  39.3 1.6 %collective-permute-start.11 = (bf16[128,768]{1,0:T(8,128)(2,1)S(1)}, bf16[128,768]{1,0:T(8,128)(2,1)S(1)}, u32[]{:S(2)}, u32[]{:S(2)}) collective-permute-start(bf16[128,768]{1,0:T(8,128)(2,1)S(1)} %get-tuple-element.81.refs_6_), channel_id=1, source_target_pairs={{0,2},{1,3},{2,0},{3,1},{4,6},{5,7},{6,4},{7,5},{8,10},{9,11},{10,... | collective-permute-start | bytes 589832 | tf_op jit(solution)/shard_map/ppermute | solution.py:662
  40.9 0.5 collective-permute-start.15
  41.4 1.5 %collective-permute-start.14 = (bf16[128,512]{1,0:T(8,128)(2,1)S(1)}, bf16[128,512]{1,0:T(8,128)(2,1)S(1)}, u32[]{:S(2)}, u32[]{:S(2)}) collective-permute-start(bf16[128,512]{1,0:T(8,128)(2,1)S(1)} %get-tuple-element.78.refs_6_), channel_id=1, source_target_pairs={{0,2},{1,3},{2,0},{3,1},{4,6},{5,7},{6,4},{7,5},{8,10},{9,11},{10,... | collective-permute-start | bytes 393224 | tf_op jit(solution)/shard_map/ppermute | solution.py:662
  42.9 0.5 project.9
  43.4 13.4 %collective-permute-done.15.refs_0_ = bf16[128,512]{1,0:T(8,128)(2,1)S(1)} collective-permute-done((bf16[128,512]{1,0:T(8,128)(2,1)S(1)}, bf16[128,512]{1,0:T(8,128)(2,1)S(1)}, u32[]{:S(2)}, u32[]{:S(2)}) %collective-permute-start.15) | collective-permute-done | bytes 131104 | tf_op jit(solution)/shard_map/ppermute | solution.py:662
  56.7 1.5 %collective-permute-start.10 = (bf16[128,256]{1,0:T(8,128)(2,1)S(1)}, bf16[128,256]{1,0:T(8,128)(2,1)S(1)}, u32[]{:S(2)}, u32[]{:S(2)}) collective-permute-start(bf16[128,256]{1,0:T(8,128)(2,1)S(1)} %get-tuple-element.83), channel_id=1, source_target_pairs={{0,2},{1,3},{2,0},{3,1},{4,6},{5,7},{6,4},{7,5},{8,10},{9,11},{10,... | collective-permute-start | bytes 196616 | tf_op jit(solution)/shard_map/ppermute | solution.py:662
  58.2 0.7 %finish.6.refs_1_ = bf16[128,4096]{1,0:T(8,128)(2,1)} custom-call(f32[128,512]{1,0:T(8,128)S(1)} %get-tuple-element.88.own_ref, bf16[128,4096]{1,0:T(8,128)(2,1)S(1)} %copy-done, bf16[128,512]{1,0:T(8,128)(2,1)S(1)} %collective-permute-done.15.refs_0_), custom_call_target="tpu_custom_call" | custom-call | tf_op jit(solution)/shard_map/finish/pallas_call | solution.py:569
  59.0 0.6 collective-permute-done.14.refs_0_
  59.5 0.7 %finish.7.refs_1_ = bf16[128,4096]{1,0:T(8,128)(2,1)} custom-call(f32[128,512]{1,0:T(8,128)S(1)} %get-tuple-element.87.own_ref, bf16[128,4096]{1,0:T(8,128)(2,1)S(1)} %copy-done, bf16[128,512]{1,0:T(8,128)(2,1)S(1)} %collective-permute-done.14.refs_0_, bf16[128,4096]{1,0:T(8,128)(2,1)} %finish.6.refs_1_), custom_call_target="tpu_custom_call", output_to_operand_aliasing={{}: (3, {})} | custom-call | tf_op jit(solution)/shard_map/finish/pallas_call | solution.py:569
  60.3 0.8 %finish.8.refs_1_ = bf16[128,4096]{1,0:T(8,128)(2,1)} custom-call(f32[128,1024]{1,0:T(8,128)S(1)} %get-tuple-element.86.own_ref, bf16[128,4096]{1,0:T(8,128)(2,1)S(1)} %copy-done, bf16[128,1024]{1,0:T(8,128)(2,1)S(1)} %collective-permute-done.13.refs_0_, bf16[128,4096]{1,0:T(8,128)(2,1)} %finish.7.refs_1_), custom_call_target="tpu_custom_call", output_to_operand_aliasing={{}: (3, {})} | custom-call | tf_op jit(solution)/shard_map/finish/pallas_call | solution.py:569
  61.1 0.8 %finish.9.refs_1_ = bf16[128,4096]{1,0:T(8,128)(2,1)} custom-call(f32[128,1024]{1,0:T(8,128)S(1)} %get-tuple-element.85.own_ref, bf16[128,4096]{1,0:T(8,128)(2,1)S(1)} %copy-done, bf16[128,1024]{1,0:T(8,128)(2,1)S(1)} %collective-permute-done.12.refs_0_, bf16[128,4096]{1,0:T(8,128)(2,1)} %finish.8.refs_1_), custom_call_target="tpu_custom_call", output_to_operand_aliasing={{}: (3, {})} | custom-call | tf_op jit(solution)/shard_map/finish/pallas_call | solution.py:569
  61.9 0.8 %finish.10.refs_1_ = bf16[128,4096]{1,0:T(8,128)(2,1)} custom-call(f32[128,768]{1,0:T(8,128)S(1)} %get-tuple-element.84.own_ref, bf16[128,4096]{1,0:T(8,128)(2,1)S(1)} %copy-done, bf16[128,768]{1,0:T(8,128)(2,1)S(1)} %collective-permute-done.11.refs_0_, bf16[128,4096]{1,0:T(8,128)(2,1)} %finish.9.refs_1_), custom_call_target="tpu_custom_call", output_to_operand_aliasing={{}: (3, {})} | custom-call | tf_op jit(solution)/shard_map/finish/pallas_call | solution.py:569
  62.7 0.7 %finish.11 = bf16[128,4096]{1,0:T(8,128)(2,1)} custom-call(f32[128,256]{1,0:T(8,128)S(1)} %get-tuple-element.82.own_ref, bf16[128,4096]{1,0:T(8,128)(2,1)S(1)} %copy-done, bf16[128,256]{1,0:T(8,128)(2,1)S(1)} %collective-permute-done.10.refs_0_, bf16[128,4096]{1,0:T(8,128)(2,1)} %finish.10.refs_1_), custom_call_target="tpu_custom_call", output_to_operand_aliasing={{}: (3, {})} | custom-call | tf_op jit(solution)/shard_map/finish/pallas_call | solution.py:569
  (18 shorter events, 0.1 us)
Async XLA Ops:
  0.0 25.6 %copy-start.1 = (f32[1024]{0:T(1024)S(1)}, f32[1024]{0:T(1024)}, u32[]{:S(2)}) copy-start(f32[1024]{0:T(1024)} %param.11) | copy-start | bytes 12292
  3.8 28.1 %collective-permute-start.9 = (bf16[1024,4096]{1,0:T(8,128)(2,1)}, bf16[1024,4096]{1,0:T(8,128)(2,1)S(1)}, u32[]{:S(2)}, u32[]{:S(2)}) collective-permute-start(bf16[1024,4096]{1,0:T(8,128)(2,1)} %refs_4_.4), channel_id=1, source_target_pairs={{0,1},{1,0},{2,3},{3,2},{4,5},{5,4},{6,7},{7,6},{8,9},{9,8},{10,11... | collective-permute-start | bytes 25165832 | tf_op jit(solution)/shard_map/ppermute | solution.py:608
  4.3 5.4 %collective-permute-start.1 = (bf16[272,128]{1,0:T(8,128)(2,1)S(1)}, bf16[272,128]{1,0:T(8,128)(2,1)S(1)}, u32[]{:S(2)}, u32[]{:S(2)}) collective-permute-start(bf16[272,128]{1,0:T(8,128)(2,1)S(1)} %get-tuple-element.63), channel_id=1, source_target_pairs={{0,8},{4,12},{8,0},{12,4},{16,24},{20,28},{24,16},{28,20},{1,9},{5... | collective-permute-start | bytes 208904 | tf_op jit(solution)/shard_map/ppermute | solution.py:599
  7.0 5.4 %collective-permute-start.2 = (bf16[272,128]{1,0:T(8,128)(2,1)S(1)}, bf16[272,128]{1,0:T(8,128)(2,1)S(1)}, u32[]{:S(2)}, u32[]{:S(2)}) collective-permute-start(bf16[272,128]{1,0:T(8,128)(2,1)S(1)} %get-tuple-element.64), channel_id=1, source_target_pairs={{0,12},{4,8},{8,4},{12,0},{16,28},{20,24},{24,20},{28,16},{1,13},{... | collective-permute-start | bytes 208904 | tf_op jit(solution)/shard_map/ppermute | solution.py:599
  8.3 5.4 %collective-permute-start = (bf16[272,128]{1,0:T(8,128)(2,1)S(1)}, bf16[272,128]{1,0:T(8,128)(2,1)S(1)}, u32[]{:S(2)}, u32[]{:S(2)}) collective-permute-start(bf16[272,128]{1,0:T(8,128)(2,1)S(1)} %get-tuple-element.52.hold_ref), channel_id=1, source_target_pairs={{0,4},{4,0},{8,12},{12,8},{16,20},{20,16},{24,28},{28,24},{1,5},{5... | collective-permute-start | bytes 208904 | tf_op jit(solution)/shard_map/ppermute | solution.py:599
  13.8 6.4 %collective-permute-start.3 = (bf16[272,128]{1,0:T(8,128)(2,1)S(1)}, bf16[272,128]{1,0:T(8,128)(2,1)S(1)}, u32[]{:S(2)}, u32[]{:S(2)}) collective-permute-start(bf16[272,128]{1,0:T(8,128)(2,1)S(1)} %get-tuple-element.65), channel_id=1, source_target_pairs={{0,16},{4,20},{8,24},{12,28},{16,0},{20,4},{24,8},{28,12},{1,17},{... | collective-permute-start | bytes 208904 | tf_op jit(solution)/shard_map/ppermute | solution.py:599
  20.4 5.2 %collective-permute-start.4 = (bf16[256,128]{1,0:T(8,128)(2,1)S(1)}, bf16[256,128]{1,0:T(8,128)(2,1)S(1)}, u32[]{:S(2)}, u32[]{:S(2)}) collective-permute-start(bf16[256,128]{1,0:T(8,128)(2,1)S(1)} %get-tuple-element.70), channel_id=1, source_target_pairs={{0,12},{4,8},{8,4},{12,0},{16,28},{20,24},{24,20},{28,16},{1,13},{... | collective-permute-start | bytes 196616 | tf_op jit(solution)/shard_map/ppermute | solution.py:599
  20.7 4.9 %collective-permute-start.5 = (bf16[256,128]{1,0:T(8,128)(2,1)S(1)}, bf16[256,128]{1,0:T(8,128)(2,1)S(1)}, u32[]{:S(2)}, u32[]{:S(2)}) collective-permute-start(bf16[256,128]{1,0:T(8,128)(2,1)S(1)} %get-tuple-element.71), channel_id=1, source_target_pairs={{0,8},{4,12},{8,0},{12,4},{16,24},{20,28},{24,16},{28,20},{1,9},{5... | collective-permute-start | bytes 196616 | tf_op jit(solution)/shard_map/ppermute | solution.py:599
  23.3 8.6 %slice-start = ((s8[8388608]{0:T(1024)(128)(4,1)}), s8[4194304]{0:T(1024)(128)(4,1)S(1)}, s32[]{:S(2)}) async-start(s8[8388608]{0:T(1024)(128)(4,1)} %bitcast.5), calls=%async_computation | async-start | bytes 8388608
  25.6 6.3 %slice-start.1 = ((s8[8388608]{0:T(1024)(128)(4,1)}), s8[4194304]{0:T(1024)(128)(4,1)S(1)}, s32[]{:S(2)}) async-start(s8[8388608]{0:T(1024)(128)(4,1)} %bitcast.5), calls=%async_computation.1 | async-start | bytes 8388608
  26.1 5.8 %collective-permute-start.7 = (bf16[256,768]{1,0:T(8,128)(2,1)S(1)}, bf16[256,768]{1,0:T(8,128)(2,1)S(1)}, u32[]{:S(2)}, u32[]{:S(2)}) collective-permute-start(bf16[256,768]{1,0:T(8,128)(2,1)S(1)} %norm_away.2), channel_id=1, source_target_pairs={{0,1},{1,0},{2,3},{3,2},{4,5},{5,4},{6,7},{7,6},{8,9},{9,8},{10,11... | collective-permute-start | bytes 1179656 | tf_op jit(solution)/shard_map/ppermute | solution.py:639
  26.2 4.5 %collective-permute-start.6 = (bf16[256,128]{1,0:T(8,128)(2,1)S(1)}, bf16[256,128]{1,0:T(8,128)(2,1)S(1)}, u32[]{:S(2)}, u32[]{:S(2)}) collective-permute-start(bf16[256,128]{1,0:T(8,128)(2,1)S(1)} %get-tuple-element.74), channel_id=1, source_target_pairs={{0,4},{4,0},{8,12},{12,8},{16,20},{20,16},{24,28},{28,24},{1,5},{5... | collective-permute-start | bytes 196616 | tf_op jit(solution)/shard_map/ppermute | solution.py:599
  31.0 1.6 %collective-permute-start.8 = (bf16[256,256]{1,0:T(8,128)(2,1)S(1)}, bf16[256,256]{1,0:T(8,128)(2,1)S(1)}, u32[]{:S(2)}, u32[]{:S(2)}) collective-permute-start(bf16[256,256]{1,0:T(8,128)(2,1)S(1)} %norm_away.3), channel_id=1, source_target_pairs={{0,1},{1,0},{2,3},{3,2},{4,5},{5,4},{6,7},{7,6},{8,9},{9,8},{10,11... | collective-permute-start | bytes 393224 | tf_op jit(solution)/shard_map/ppermute | solution.py:639
  34.8 25.4 %collective-permute-start.13 = (bf16[128,1024]{1,0:T(8,128)(2,1)S(1)}, bf16[128,1024]{1,0:T(8,128)(2,1)S(1)}, u32[]{:S(2)}, u32[]{:S(2)}) collective-permute-start(bf16[128,1024]{1,0:T(8,128)(2,1)S(1)} %get-tuple-element.79.refs_6_), channel_id=1, source_target_pairs={{0,2},{1,3},{2,0},{3,1},{4,6},{5,7},{6,4},{7,5},{8,10},{9,11},{10,... | collective-permute-start | bytes 786440 | tf_op jit(solution)/shard_map/ppermute | solution.py:662
  37.7 23.4 %collective-permute-start.12 = (bf16[128,1024]{1,0:T(8,128)(2,1)S(1)}, bf16[128,1024]{1,0:T(8,128)(2,1)S(1)}, u32[]{:S(2)}, u32[]{:S(2)}) collective-permute-start(bf16[128,1024]{1,0:T(8,128)(2,1)S(1)} %get-tuple-element.80.refs_6_), channel_id=1, source_target_pairs={{0,2},{1,3},{2,0},{3,1},{4,6},{5,7},{6,4},{7,5},{8,10},{9,11},{10,... | collective-permute-start | bytes 786440 | tf_op jit(solution)/shard_map/ppermute | solution.py:662
  39.3 19.0 %copy-start = (bf16[128,4096]{1,0:T(8,128)(2,1)S(1)}, bf16[128,4096]{1,0:T(8,128)(2,1)}, u32[]{:S(2)}) copy-start(bf16[128,4096]{1,0:T(8,128)(2,1)} %residual_ref.11) | copy-start | bytes 3145732
  39.3 22.7 %collective-permute-start.11 = (bf16[128,768]{1,0:T(8,128)(2,1)S(1)}, bf16[128,768]{1,0:T(8,128)(2,1)S(1)}, u32[]{:S(2)}, u32[]{:S(2)}) collective-permute-start(bf16[128,768]{1,0:T(8,128)(2,1)S(1)} %get-tuple-element.81.refs_6_), channel_id=1, source_target_pairs={{0,2},{1,3},{2,0},{3,1},{4,6},{5,7},{6,4},{7,5},{8,10},{9,11},{10,... | collective-permute-start | bytes 589832 | tf_op jit(solution)/shard_map/ppermute | solution.py:662
  40.9 15.9 %collective-permute-start.15 = (bf16[128,512]{1,0:T(8,128)(2,1)S(1)}, bf16[128,512]{1,0:T(8,128)(2,1)S(1)}, u32[]{:S(2)}, u32[]{:S(2)}) collective-permute-start(bf16[128,512]{1,0:T(8,128)(2,1)S(1)} %get-tuple-element.77.refs_6_), channel_id=1, source_target_pairs={{0,2},{1,3},{2,0},{3,1},{4,6},{5,7},{6,4},{7,5},{8,10},{9,11},{10,... | collective-permute-start | bytes 393224 | tf_op jit(solution)/shard_map/ppermute | solution.py:662
  41.4 18.1 %collective-permute-start.14 = (bf16[128,512]{1,0:T(8,128)(2,1)S(1)}, bf16[128,512]{1,0:T(8,128)(2,1)S(1)}, u32[]{:S(2)}, u32[]{:S(2)}) collective-permute-start(bf16[128,512]{1,0:T(8,128)(2,1)S(1)} %get-tuple-element.78.refs_6_), channel_id=1, source_target_pairs={{0,2},{1,3},{2,0},{3,1},{4,6},{5,7},{6,4},{7,5},{8,10},{9,11},{10,... | collective-permute-start | bytes 393224 | tf_op jit(solution)/shard_map/ppermute | solution.py:662
  56.7 6.0 %collective-permute-start.10 = (bf16[128,256]{1,0:T(8,128)(2,1)S(1)}, bf16[128,256]{1,0:T(8,128)(2,1)S(1)}, u32[]{:S(2)}, u32[]{:S(2)}) collective-permute-start(bf16[128,256]{1,0:T(8,128)(2,1)S(1)} %get-tuple-element.83), channel_id=1, source_target_pairs={{0,2},{1,3},{2,0},{3,1},{4,6},{5,7},{6,4},{7,5},{8,10},{9,11},{10,... | collective-permute-start | bytes 196616 | tf_op jit(solution)/shard_map/ppermute | solution.py:662

commit v4 on v3

--- a/solution.py
+++ b/solution.py
@@ -153,11 +153,11 @@
     return pays, key, value
 
 
-def load_kernel(size, count, width, place_ref, logd_in, query_in, key_ref, value_ref, hold_ref, *refs):
-    pay_ref, query_ref, cum_ref, logd_ref, weight_ref, logd_sem, sems = refs
+def load_kernel(size, count, width, place_ref, logd_in, query_in, weight_in, key_ref, value_ref, hold_ref, *refs):
+    pay_ref, query_ref, cum_ref, head_ref, logd_ref, weight_ref, logd_sem, sems, head_sems = refs
     logd = pltpu.make_async_copy(logd_in, logd_ref, logd_sem)
     logd.start()
-    copies = copies_of(query_in, query_ref, sems)
+    copies = copies_of(query_in, query_ref, sems) + copies_of(weight_in, head_ref, head_sems)
     for copy in copies:
         copy.start()
     logd.wait()
@@ -170,22 +170,27 @@
         copy.wait()
 
 
-def load(place, logd, key, value, query, hold, size, count, width):
+def load(place, logd, key, value, query, weight, columns, hold, size, count, width):
     heads, rows = logd.shape
     return pl.pallas_call(
         functools.partial(load_kernel, size, count, width),
-        in_specs=[SMEM, ANY, ANY, VMEM, VMEM, ANY],
-        out_specs=[VMEM] * 3,
+        in_specs=[SMEM, ANY, ANY, ANY, VMEM, VMEM, ANY],
+        out_specs=[VMEM] * 4,
         out_shape=[
             pay_shape(count, width, F32),
             held(query.shape, BF16),
             held((heads, rows), F32),
+            held((weight.shape[0], columns), BF16),
         ],
         scratch_shapes=[pltpu.VMEM((heads, rows), F32)] * 2
-        + [pltpu.SemaphoreType.DMA, pltpu.SemaphoreType.DMA((2,))],
+        + [
+            pltpu.SemaphoreType.DMA,
+            pltpu.SemaphoreType.DMA((2,)),
+            pltpu.SemaphoreType.DMA((8,)),
+        ],
         compiler_params=PACKED,
         name="load",
-    )(place, outside(logd), outside(query), near(key), near(value), hold)
+    )(place, outside(logd), outside(query), outside(weight), near(key), near(value), hold)
 
 
 def decay_row(pay, j, count, width):
@@ -603,14 +608,14 @@
         logd = jnp.pad(logd, ((0, pad_rows(heads) - heads), (0, 0)))
     sent, key, value = early_states(place, logd, k_spikes, v_spikes, size, count, width)
     met = [swap(a, i + 1) for i, a in enumerate(sent)]
-    kept, query, cum = load(place, logd, key, value, q_spikes, sent[0], size, count, width)
+    total = out_weight.shape[1]
+    tile = tile_of(total, 512)
+    kept, query, cum, head_weight = load(
+        place, logd, key, value, q_spikes, out_weight, tile, sent[0], size, count, width
+    )
     kept, weight = lax.optimization_barrier((kept, out_weight))
     far_weight = lax.ppermute(outside(weight), "exp", cores)
-    total = out_weight.shape[1]
-    tile = tile_of(total, 512)
-
     pay, past, window = gather(place, kept, met, size, count, width, int(2 * size < blocks))
-    _, own_weight = lax.optimization_barrier((pay, out_weight))
     before, got, level, bit = None, None, 0, size
     while bit < blocks:
         got = swap(pay, bit)
@@ -622,6 +627,7 @@
     own, *theirs = enter(place, got, before, past, size, count, width, bit // 2 if level else 0)
     entering = [own] + [swap(a, i + 1) for i, a in enumerate(theirs)]
 
+    _, own_weight = lax.optimization_barrier((own, out_weight))
     insides, queries = [], []
     for away in range(size):
         inside, decayed = local(place, cum, query, key, value, size, count, width, away)
@@ -644,7 +650,7 @@
         sizes.append(2 * tile)
     rest = total - sum(sizes)
     sizes += [rest - tile // 2, tile // 2] if rest > tile // 2 else [rest]
-    begun = begin(place, home, other[0], own_weight, far_weight, sizes[0], size)
+    begun = begin(place, home, other[0], head_weight, far_weight, sizes[0], size)
     out, at, hold = None, 0, None
     sums = []
     for index, span in enumerate(sizes):

time: 63.6 us -> 64.8 us (1.019)
  Pallas kernels: 18.6 us -> 19.8 us
    pallas_call x1, Pallas kernels: 1.57 us -> 2.72 us  [load(): pl.pallas_call(functools.partial(load_kernel, size, count, width), in_spe...]
  transfers between devices with their start and end apart: 16 -> 16, of which waited for: 8 -> 8; matrix products, arithmetic and copies ran while one was open for 0% -> 0% of each run, Pallas kernels for 19% -> 18%
where the time goes in v4:
time: 64.8 us; the launch traced here: 64.7 us
  waiting for transfers between devices  26.2 us (40%)
  Pallas kernels  19.8 us (31%)
  starting transfers between devices  18.3 us (28%)
    ppermute x6, waiting for transfers between devices, shards(): got.append(lax.ppermute(piece, 'exp', perm))  13.9 us
    ppermute x7, waiting for transfers between devices, swap(): return lax.ppermute(x, 'ctx', [(i, i ^ bit) for i in range(blocks)])  12.3 us
    ppermute x7, starting transfers between devices, swap(): return lax.ppermute(x, 'ctx', [(i, i ^ bit) for i in range(blocks)])  10.3 us
    ppermute x6, starting transfers between devices, shards(): got.append(lax.ppermute(piece, 'exp', perm))  7.3 us
    pallas_call x5, Pallas kernels, project(): pl.pallas_call(functools.partial(project_kernel, block, first, tile, size...  4.64 us
    pallas_call x6, Pallas kernels, finish(): pl.pallas_call(functools.partial(finish_kernel, first, len(parts)), in_sp...  4.56 us
    pallas_call x4, Pallas kernels, local(): pl.pallas_call(functools.partial(local_kernel, size, count, width, away),...  2.9 us
    pallas_call x1, Pallas kernels, load(): pl.pallas_call(functools.partial(load_kernel, size, count, width), in_spe...  2.72 us
  transfers between devices with their start and end apart: 16, of which 8 were waited for; matrix products, arithmetic and copies ran while one was open for 0% of the time, Pallas kernels for 18%

profile of v4, /device:TPU:0, one launch (start us, length us, event | category | flops | bytes accessed | tf_op | source)
XLA Modules:
  0.0 64.7 jit_solution(2938033935807732037)
XLA Ops:
  0.0 2.3 %early_states.1 = (bf16[272,128]{1,0:T(8,128)(2,1)S(1)}, bf16[272,128]{1,0:T(8,128)(2,1)S(1)}, bf16[272,128]{1,0:T(8,128)(2,1)S(1)}, bf16[512,1024]{1,0:T(8,128)(2,1)S(1)}, bf16[512,1024]{1,0:T(8,128)(2,1)S(1)}) custom-call(s32[1]{0:T(128)} %bitcast.place_ref, f32[8,512]{1,0:T(8,128)} %bitcast.9, bf16[512,1024]{1,0:T(8,128)(2,1)} %key_in.1, ...), custom_call_target="tpu_custom_call" | custom-call | tf_op jit(solution)/shard_map/early_states/pallas_call | solution.py:143
  2.3 2.7 %load.1 = (f32[272,128]{1,0:T(8,128)S(1)}, bf16[512,1024]{1,0:T(8,128)(2,1)S(1)}, f32[8,512]{1,0:T(8,128)S(1)}, bf16[1024,512]{1,0:T(8,128)(2,1)S(1)}) custom-call(s32[1]{0:T(128)} %bitcast.place_ref, f32[8,512]{1,0:T(8,128)} %bitcast.10, bf16[512,1024]{1,0:T(8,128)(2,1)} %query_in.1, bf16[1024,4096]{1,0:T(8,128)(2,1)} %refs_4_.4, ...), custom_call_target="tpu_custom_call" | custom-call | tf_op jit(solution)/shard_map/load/pallas_call | solution.py:175
  5.1 0.6 collective-permute-start.9
  5.6 2.6 %collective-permute-start.1 = (bf16[272,128]{1,0:T(8,128)(2,1)S(1)}, bf16[272,128]{1,0:T(8,128)(2,1)S(1)}, u32[]{:S(2)}, u32[]{:S(2)}) collective-permute-start(bf16[272,128]{1,0:T(8,128)(2,1)S(1)} %get-tuple-element.64), channel_id=1, source_target_pairs={{0,8},{4,12},{8,0},{12,4},{16,24},{20,28},{24,16},{28,20},{1,9},{5... | collective-permute-start | bytes 208904 | tf_op jit(solution)/shard_map/ppermute | solution.py:604
  8.3 1.4 %collective-permute-start.2 = (bf16[272,128]{1,0:T(8,128)(2,1)S(1)}, bf16[272,128]{1,0:T(8,128)(2,1)S(1)}, u32[]{:S(2)}, u32[]{:S(2)}) collective-permute-start(bf16[272,128]{1,0:T(8,128)(2,1)S(1)} %get-tuple-element.65), channel_id=1, source_target_pairs={{0,12},{4,8},{8,4},{12,0},{16,28},{20,24},{24,20},{28,16},{1,13},{... | collective-permute-start | bytes 208904 | tf_op jit(solution)/shard_map/ppermute | solution.py:604
  9.7 0.2 collective-permute-start
  9.8 1.2 %collective-permute-done.1.refs_2_ = bf16[272,128]{1,0:T(8,128)(2,1)S(1)} collective-permute-done((bf16[272,128]{1,0:T(8,128)(2,1)S(1)}, bf16[272,128]{1,0:T(8,128)(2,1)S(1)}, u32[]{:S(2)}, u32[]{:S(2)}) %collective-permute-start.1) | collective-permute-done | bytes 69664 | tf_op jit(solution)/shard_map/ppermute | solution.py:604
  11.1 2.7 %collective-permute-done.2.refs_3_ = bf16[272,128]{1,0:T(8,128)(2,1)S(1)} collective-permute-done((bf16[272,128]{1,0:T(8,128)(2,1)S(1)}, bf16[272,128]{1,0:T(8,128)(2,1)S(1)}, u32[]{:S(2)}, u32[]{:S(2)}) %collective-permute-start.2) | collective-permute-done | bytes 69664 | tf_op jit(solution)/shard_map/ppermute | solution.py:604
  13.7 1.3 %collective-permute-done.refs_1_ = bf16[272,128]{1,0:T(8,128)(2,1)S(1)} collective-permute-done((bf16[272,128]{1,0:T(8,128)(2,1)S(1)}, bf16[272,128]{1,0:T(8,128)(2,1)S(1)}, u32[]{:S(2)}, u32[]{:S(2)}) %collective-permute-start) | collective-permute-done | bytes 69664 | tf_op jit(solution)/shard_map/ppermute | solution.py:604
  15.0 0.1 gather.1
  15.1 2.7 %collective-permute-start.3 = (bf16[272,128]{1,0:T(8,128)(2,1)S(1)}, bf16[272,128]{1,0:T(8,128)(2,1)S(1)}, u32[]{:S(2)}, u32[]{:S(2)}) collective-permute-start(bf16[272,128]{1,0:T(8,128)(2,1)S(1)} %get-tuple-element.66), channel_id=1, source_target_pairs={{0,16},{4,20},{8,24},{12,28},{16,0},{20,4},{24,8},{28,12},{1,17},{... | collective-permute-start | bytes 208904 | tf_op jit(solution)/shard_map/ppermute | solution.py:604
  17.8 3.8 %collective-permute-done.3.got_ref = bf16[272,128]{1,0:T(8,128)(2,1)S(1)} collective-permute-done((bf16[272,128]{1,0:T(8,128)(2,1)S(1)}, bf16[272,128]{1,0:T(8,128)(2,1)S(1)}, u32[]{:S(2)}, u32[]{:S(2)}) %collective-permute-start.3) | collective-permute-done | bytes 69664 | tf_op jit(solution)/shard_map/ppermute | solution.py:604
  21.6 0.1 enter.1
  21.7 0.4 collective-permute-start.4
  22.1 1.8 %collective-permute-start.5 = (bf16[256,128]{1,0:T(8,128)(2,1)S(1)}, bf16[256,128]{1,0:T(8,128)(2,1)S(1)}, u32[]{:S(2)}, u32[]{:S(2)}) collective-permute-start(bf16[256,128]{1,0:T(8,128)(2,1)S(1)} %get-tuple-element.72), channel_id=1, source_target_pairs={{0,8},{4,12},{8,0},{12,4},{16,24},{20,28},{24,16},{28,20},{1,9},{5... | collective-permute-start | bytes 196616 | tf_op jit(solution)/shard_map/ppermute | solution.py:604
  23.9 0.7 %local.6 = (f32[512,256]{1,0:T(8,128)S(1)}, bf16[512,256]{1,0:T(8,128)(2,1)S(1)}) custom-call(s32[1]{0:T(128)} %bitcast.place_ref, f32[8,512]{1,0:T(8,128)S(1)} %get-tuple-element.54.cum_ref, bf16[512,1024]{1,0:T(8,128)(2,1)S(1)} %get-tuple-element.55.q_ref, bf16[512,1024]{1,0:T(8,128)(2,1)S(1)} %get-tuple-element.51.key_ref.k_ref, ...), custom_call_target="tpu_custom_call" | custom-call | tf_op jit(solution)/shard_map/local/pallas_call | solution.py:405
  24.6 0.7 %local.5 = (f32[512,256]{1,0:T(8,128)S(1)}, bf16[512,256]{1,0:T(8,128)(2,1)S(1)}) custom-call(s32[1]{0:T(128)} %bitcast.place_ref, f32[8,512]{1,0:T(8,128)S(1)} %get-tuple-element.54.cum_ref, bf16[512,1024]{1,0:T(8,128)(2,1)S(1)} %get-tuple-element.55.q_ref, bf16[512,1024]{1,0:T(8,128)(2,1)S(1)} %get-tuple-element.51.key_ref.k_ref, ...), custom_call_target="tpu_custom_call" | custom-call | tf_op jit(solution)/shard_map/local/pallas_call | solution.py:405
  25.3 0.7 %local.4 = (f32[512,256]{1,0:T(8,128)S(1)}, bf16[512,256]{1,0:T(8,128)(2,1)S(1)}) custom-call(s32[1]{0:T(128)} %bitcast.place_ref, f32[8,512]{1,0:T(8,128)S(1)} %get-tuple-element.54.cum_ref, bf16[512,1024]{1,0:T(8,128)(2,1)S(1)} %get-tuple-element.55.q_ref, bf16[512,1024]{1,0:T(8,128)(2,1)S(1)} %get-tuple-element.51.key_ref.k_ref, ...), custom_call_target="tpu_custom_call" | custom-call | tf_op jit(solution)/shard_map/local/pallas_call | solution.py:405
  26.0 0.9 %collective-permute-done.4.refs_7_ = bf16[256,128]{1,0:T(8,128)(2,1)S(1)} collective-permute-done((bf16[256,128]{1,0:T(8,128)(2,1)S(1)}, bf16[256,128]{1,0:T(8,128)(2,1)S(1)}, u32[]{:S(2)}, u32[]{:S(2)}) %collective-permute-start.4) | collective-permute-done | bytes 65568 | tf_op jit(solution)/shard_map/ppermute | solution.py:604
  26.9 0.5 norm_away.2
  27.4 0.1 collective-permute-start.7
  27.5 1.3 %collective-permute-start.6 = (bf16[256,128]{1,0:T(8,128)(2,1)S(1)}, bf16[256,128]{1,0:T(8,128)(2,1)S(1)}, u32[]{:S(2)}, u32[]{:S(2)}) collective-permute-start(bf16[256,128]{1,0:T(8,128)(2,1)S(1)} %get-tuple-element.75), channel_id=1, source_target_pairs={{0,4},{4,0},{8,12},{12,8},{16,20},{20,16},{24,28},{28,24},{1,5},{5... | collective-permute-start | bytes 196616 | tf_op jit(solution)/shard_map/ppermute | solution.py:604
  28.8 0.7 %local.7 = (f32[512,256]{1,0:T(8,128)S(1)}, bf16[512,256]{1,0:T(8,128)(2,1)S(1)}) custom-call(s32[1]{0:T(128)} %bitcast.place_ref, f32[8,512]{1,0:T(8,128)S(1)} %get-tuple-element.54.cum_ref, bf16[512,1024]{1,0:T(8,128)(2,1)S(1)} %get-tuple-element.55.q_ref, bf16[512,1024]{1,0:T(8,128)(2,1)S(1)} %get-tuple-element.51.key_ref.k_ref, ...), custom_call_target="tpu_custom_call" | custom-call | tf_op jit(solution)/shard_map/local/pallas_call | solution.py:405
  29.5 2.4 %collective-permute-done.6.refs_2_ = bf16[256,128]{1,0:T(8,128)(2,1)S(1)} collective-permute-done((bf16[256,128]{1,0:T(8,128)(2,1)S(1)}, bf16[256,128]{1,0:T(8,128)(2,1)S(1)}, u32[]{:S(2)}, u32[]{:S(2)}) %collective-permute-start.6) | collective-permute-done | bytes 65568 | tf_op jit(solution)/shard_map/ppermute | solution.py:604
  32.0 0.3 norm_away.3
  32.4 0.3 norm_home.3.two_ref.refs_1_
  32.7 0.5 norm_home.2.one_ref.refs_0_
  33.2 0.6 begin.1.begun_ref
  33.9 0.2 complete.1
  34.1 0.7 %project.5 = (f32[128,512]{1,0:T(8,128)S(1)}, bf16[128,512]{1,0:T(8,128)(2,1)S(1)}) custom-call(s32[1]{0:T(128)} %bitcast.place_ref, bf16[256,768]{1,0:T(8,128)(2,1)S(1)} %norm_home.2.one_ref.refs_0_, bf16[256,256]{1,0:T(8,128)(2,1)S(1)} %norm_home.3.two_ref.refs_1_, bf16[256,768]{1,0:T(8,128)(2,1)S(1)} %collective-permute-done.7.met_ref.refs_2_, ...), custom_call_target="tpu_custom_call" | custom-call | tf_op jit(solution)/shard_map/project/pallas_call | solution.py:539
  34.8 1.3 %project.6 = (f32[128,1024]{1,0:T(8,128)S(1)}, bf16[128,1024]{1,0:T(8,128)(2,1)S(1)}) custom-call(s32[1]{0:T(128)} %bitcast.place_ref, bf16[256,768]{1,0:T(8,128)(2,1)S(1)} %norm_home.2.one_ref.refs_0_, bf16[256,256]{1,0:T(8,128)(2,1)S(1)} %norm_home.3.two_ref.refs_1_, bf16[256,768]{1,0:T(8,128)(2,1)S(1)} %collective-permute-done.7.met_ref.refs_2_, ...), custom_call_target="tpu_custom_call" | custom-call | tf_op jit(solution)/shard_map/project/pallas_call | solution.py:539
  36.1 1.6 %collective-permute-start.13 = (bf16[128,1024]{1,0:T(8,128)(2,1)S(1)}, bf16[128,1024]{1,0:T(8,128)(2,1)S(1)}, u32[]{:S(2)}, u32[]{:S(2)}) collective-permute-start(bf16[128,1024]{1,0:T(8,128)(2,1)S(1)} %get-tuple-element.81.refs_6_), channel_id=1, source_target_pairs={{0,2},{1,3},{2,0},{3,1},{4,6},{5,7},{6,4},{7,5},{8,10},{9,11},{10,... | collective-permute-start | bytes 786440 | tf_op jit(solution)/shard_map/ppermute | solution.py:668
  37.7 1.2 %project.7 = (f32[128,1024]{1,0:T(8,128)S(1)}, bf16[128,1024]{1,0:T(8,128)(2,1)S(1)}) custom-call(s32[1]{0:T(128)} %bitcast.place_ref, bf16[256,768]{1,0:T(8,128)(2,1)S(1)} %norm_home.2.one_ref.refs_0_, bf16[256,256]{1,0:T(8,128)(2,1)S(1)} %norm_home.3.two_ref.refs_1_, bf16[256,768]{1,0:T(8,128)(2,1)S(1)} %collective-permute-done.7.met_ref.refs_2_, ...), custom_call_target="tpu_custom_call" | custom-call | tf_op jit(solution)/shard_map/project/pallas_call | solution.py:539
  38.9 0.6 collective-permute-start.12
  39.5 1.0 %project.8 = (f32[128,768]{1,0:T(8,128)S(1)}, bf16[128,768]{1,0:T(8,128)(2,1)S(1)}) custom-call(s32[1]{0:T(128)} %bitcast.place_ref, bf16[256,768]{1,0:T(8,128)(2,1)S(1)} %norm_home.2.one_ref.refs_0_, bf16[256,256]{1,0:T(8,128)(2,1)S(1)} %norm_home.3.two_ref.refs_1_, bf16[256,768]{1,0:T(8,128)(2,1)S(1)} %collective-permute-done.7.met_ref.refs_2_, ...), custom_call_target="tpu_custom_call" | custom-call | tf_op jit(solution)/shard_map/project/pallas_call | solution.py:539
  40.5 1.6 %collective-permute-start.11 = (bf16[128,768]{1,0:T(8,128)(2,1)S(1)}, bf16[128,768]{1,0:T(8,128)(2,1)S(1)}, u32[]{:S(2)}, u32[]{:S(2)}) collective-permute-start(bf16[128,768]{1,0:T(8,128)(2,1)S(1)} %get-tuple-element.83.refs_6_), channel_id=1, source_target_pairs={{0,2},{1,3},{2,0},{3,1},{4,6},{5,7},{6,4},{7,5},{8,10},{9,11},{10,... | collective-permute-start | bytes 589832 | tf_op jit(solution)/shard_map/ppermute | solution.py:668
  42.1 0.5 collective-permute-start.15
  42.6 1.5 %collective-permute-start.14 = (bf16[128,512]{1,0:T(8,128)(2,1)S(1)}, bf16[128,512]{1,0:T(8,128)(2,1)S(1)}, u32[]{:S(2)}, u32[]{:S(2)}) collective-permute-start(bf16[128,512]{1,0:T(8,128)(2,1)S(1)} %get-tuple-element.80.refs_6_), channel_id=1, source_target_pairs={{0,2},{1,3},{2,0},{3,1},{4,6},{5,7},{6,4},{7,5},{8,10},{9,11},{10,... | collective-permute-start | bytes 393224 | tf_op jit(solution)/shard_map/ppermute | solution.py:668
  44.1 0.5 project.9
  44.6 13.4 %collective-permute-done.15.refs_0_ = bf16[128,512]{1,0:T(8,128)(2,1)S(1)} collective-permute-done((bf16[128,512]{1,0:T(8,128)(2,1)S(1)}, bf16[128,512]{1,0:T(8,128)(2,1)S(1)}, u32[]{:S(2)}, u32[]{:S(2)}) %collective-permute-start.15) | collective-permute-done | bytes 131104 | tf_op jit(solution)/shard_map/ppermute | solution.py:668
  57.9 1.5 %collective-permute-start.10 = (bf16[128,256]{1,0:T(8,128)(2,1)S(1)}, bf16[128,256]{1,0:T(8,128)(2,1)S(1)}, u32[]{:S(2)}, u32[]{:S(2)}) collective-permute-start(bf16[128,256]{1,0:T(8,128)(2,1)S(1)} %get-tuple-element.85), channel_id=1, source_target_pairs={{0,2},{1,3},{2,0},{3,1},{4,6},{5,7},{6,4},{7,5},{8,10},{9,11},{10,... | collective-permute-start | bytes 196616 | tf_op jit(solution)/shard_map/ppermute | solution.py:668
  59.5 0.7 %finish.6.refs_1_ = bf16[128,4096]{1,0:T(8,128)(2,1)} custom-call(f32[128,512]{1,0:T(8,128)S(1)} %get-tuple-element.90.own_ref, bf16[128,4096]{1,0:T(8,128)(2,1)S(1)} %copy-done.1, bf16[128,512]{1,0:T(8,128)(2,1)S(1)} %collective-permute-done.15.refs_0_), custom_call_target="tpu_custom_call" | custom-call | tf_op jit(solution)/shard_map/finish/pallas_call | solution.py:574
  60.2 0.5 collective-permute-done.14.refs_0_
  60.8 0.7 %finish.7.refs_1_ = bf16[128,4096]{1,0:T(8,128)(2,1)} custom-call(f32[128,512]{1,0:T(8,128)S(1)} %get-tuple-element.89.own_ref, bf16[128,4096]{1,0:T(8,128)(2,1)S(1)} %copy-done.1, bf16[128,512]{1,0:T(8,128)(2,1)S(1)} %collective-permute-done.14.refs_0_, bf16[128,4096]{1,0:T(8,128)(2,1)} %finish.6.refs_1_), custom_call_target="tpu_custom_call", output_to_operand_aliasing={{}: (3, {})} | custom-call | tf_op jit(solution)/shard_map/finish/pallas_call | solution.py:574
  61.5 0.8 %finish.8.refs_1_ = bf16[128,4096]{1,0:T(8,128)(2,1)} custom-call(f32[128,1024]{1,0:T(8,128)S(1)} %get-tuple-element.88.own_ref, bf16[128,4096]{1,0:T(8,128)(2,1)S(1)} %copy-done.1, bf16[128,1024]{1,0:T(8,128)(2,1)S(1)} %collective-permute-done.13.refs_0_, bf16[128,4096]{1,0:T(8,128)(2,1)} %finish.7.refs_1_), custom_call_target="tpu_custom_call", output_to_operand_aliasing={{}: (3, {})} | custom-call | tf_op jit(solution)/shard_map/finish/pallas_call | solution.py:574
  62.4 0.8 %finish.9.refs_1_ = bf16[128,4096]{1,0:T(8,128)(2,1)} custom-call(f32[128,1024]{1,0:T(8,128)S(1)} %get-tuple-element.87.own_ref, bf16[128,4096]{1,0:T(8,128)(2,1)S(1)} %copy-done.1, bf16[128,1024]{1,0:T(8,128)(2,1)S(1)} %collective-permute-done.12.refs_0_, bf16[128,4096]{1,0:T(8,128)(2,1)} %finish.8.refs_1_), custom_call_target="tpu_custom_call", output_to_operand_aliasing={{}: (3, {})} | custom-call | tf_op jit(solution)/shard_map/finish/pallas_call | solution.py:574
  63.2 0.8 %finish.10.refs_1_ = bf16[128,4096]{1,0:T(8,128)(2,1)} custom-call(f32[128,768]{1,0:T(8,128)S(1)} %get-tuple-element.86.own_ref, bf16[128,4096]{1,0:T(8,128)(2,1)S(1)} %copy-done.1, bf16[128,768]{1,0:T(8,128)(2,1)S(1)} %collective-permute-done.11.refs_0_, bf16[128,4096]{1,0:T(8,128)(2,1)} %finish.9.refs_1_), custom_call_target="tpu_custom_call", output_to_operand_aliasing={{}: (3, {})} | custom-call | tf_op jit(solution)/shard_map/finish/pallas_call | solution.py:574
  64.0 0.7 %finish.11 = bf16[128,4096]{1,0:T(8,128)(2,1)} custom-call(f32[128,256]{1,0:T(8,128)S(1)} %get-tuple-element.84.own_ref, bf16[128,4096]{1,0:T(8,128)(2,1)S(1)} %copy-done.1, bf16[128,256]{1,0:T(8,128)(2,1)S(1)} %collective-permute-done.10.refs_0_, bf16[128,4096]{1,0:T(8,128)(2,1)} %finish.10.refs_1_), custom_call_target="tpu_custom_call", output_to_operand_aliasing={{}: (3, {})} | custom-call | tf_op jit(solution)/shard_map/finish/pallas_call | solution.py:574
  (15 shorter events, 0.1 us)
Async XLA Ops:
  0.0 5.1 %copy-start = (bf16[1024,4096]{1,0:T(8,128)(2,1)S(1)}, bf16[1024,4096]{1,0:T(8,128)(2,1)}, u32[]{:S(2)}) copy-start(bf16[1024,4096]{1,0:T(8,128)(2,1)} %refs_4_.4) | copy-start | bytes 25165828
  2.3 24.6 %copy-start.2 = (f32[1024]{0:T(1024)S(1)}, f32[1024]{0:T(1024)}, u32[]{:S(2)}) copy-start(f32[1024]{0:T(1024)} %param.11) | copy-start | bytes 12292
  5.1 28.1 %collective-permute-start.9 = (bf16[1024,4096]{1,0:T(8,128)(2,1)S(1)}, bf16[1024,4096]{1,0:T(8,128)(2,1)S(1)}, u32[]{:S(2)}, u32[]{:S(2)}) collective-permute-start(bf16[1024,4096]{1,0:T(8,128)(2,1)S(1)} %copy-done), channel_id=1, source_target_pairs={{0,1},{1,0},{2,3},{3,2},{4,5},{5,4},{6,7},{7,6},{8,9},{9,8},{10,11... | collective-permute-start | bytes 25165832 | tf_op jit(solution)/shard_map/ppermute | solution.py:617
  5.6 5.4 %collective-permute-start.1 = (bf16[272,128]{1,0:T(8,128)(2,1)S(1)}, bf16[272,128]{1,0:T(8,128)(2,1)S(1)}, u32[]{:S(2)}, u32[]{:S(2)}) collective-permute-start(bf16[272,128]{1,0:T(8,128)(2,1)S(1)} %get-tuple-element.64), channel_id=1, source_target_pairs={{0,8},{4,12},{8,0},{12,4},{16,24},{20,28},{24,16},{28,20},{1,9},{5... | collective-permute-start | bytes 208904 | tf_op jit(solution)/shard_map/ppermute | solution.py:604
  8.3 5.5 %collective-permute-start.2 = (bf16[272,128]{1,0:T(8,128)(2,1)S(1)}, bf16[272,128]{1,0:T(8,128)(2,1)S(1)}, u32[]{:S(2)}, u32[]{:S(2)}) collective-permute-start(bf16[272,128]{1,0:T(8,128)(2,1)S(1)} %get-tuple-element.65), channel_id=1, source_target_pairs={{0,12},{4,8},{8,4},{12,0},{16,28},{20,24},{24,20},{28,16},{1,13},{... | collective-permute-start | bytes 208904 | tf_op jit(solution)/shard_map/ppermute | solution.py:604
  9.7 5.3 %collective-permute-start = (bf16[272,128]{1,0:T(8,128)(2,1)S(1)}, bf16[272,128]{1,0:T(8,128)(2,1)S(1)}, u32[]{:S(2)}, u32[]{:S(2)}) collective-permute-start(bf16[272,128]{1,0:T(8,128)(2,1)S(1)} %get-tuple-element.53.hold_ref), channel_id=1, source_target_pairs={{0,4},{4,0},{8,12},{12,8},{16,20},{20,16},{24,28},{28,24},{1,5},{5... | collective-permute-start | bytes 208904 | tf_op jit(solution)/shard_map/ppermute | solution.py:604
  15.1 6.4 %collective-permute-start.3 = (bf16[272,128]{1,0:T(8,128)(2,1)S(1)}, bf16[272,128]{1,0:T(8,128)(2,1)S(1)}, u32[]{:S(2)}, u32[]{:S(2)}) collective-permute-start(bf16[272,128]{1,0:T(8,128)(2,1)S(1)} %get-tuple-element.66), channel_id=1, source_target_pairs={{0,16},{4,20},{8,24},{12,28},{16,0},{20,4},{24,8},{28,12},{1,17},{... | collective-permute-start | bytes 208904 | tf_op jit(solution)/shard_map/ppermute | solution.py:604
  21.7 5.2 %collective-permute-start.4 = (bf16[256,128]{1,0:T(8,128)(2,1)S(1)}, bf16[256,128]{1,0:T(8,128)(2,1)S(1)}, u32[]{:S(2)}, u32[]{:S(2)}) collective-permute-start(bf16[256,128]{1,0:T(8,128)(2,1)S(1)} %get-tuple-element.71), channel_id=1, source_target_pairs={{0,12},{4,8},{8,4},{12,0},{16,28},{20,24},{24,20},{28,16},{1,13},{... | collective-permute-start | bytes 196616 | tf_op jit(solution)/shard_map/ppermute | solution.py:604
  22.1 4.9 %collective-permute-start.5 = (bf16[256,128]{1,0:T(8,128)(2,1)S(1)}, bf16[256,128]{1,0:T(8,128)(2,1)S(1)}, u32[]{:S(2)}, u32[]{:S(2)}) collective-permute-start(bf16[256,128]{1,0:T(8,128)(2,1)S(1)} %get-tuple-element.72), channel_id=1, source_target_pairs={{0,8},{4,12},{8,0},{12,4},{16,24},{20,28},{24,16},{28,20},{1,9},{5... | collective-permute-start | bytes 196616 | tf_op jit(solution)/shard_map/ppermute | solution.py:604
  27.4 5.8 %collective-permute-start.7 = (bf16[256,768]{1,0:T(8,128)(2,1)S(1)}, bf16[256,768]{1,0:T(8,128)(2,1)S(1)}, u32[]{:S(2)}, u32[]{:S(2)}) collective-permute-start(bf16[256,768]{1,0:T(8,128)(2,1)S(1)} %norm_away.2), channel_id=1, source_target_pairs={{0,1},{1,0},{2,3},{3,2},{4,5},{5,4},{6,7},{7,6},{8,9},{9,8},{10,11... | collective-permute-start | bytes 1179656 | tf_op jit(solution)/shard_map/ppermute | solution.py:645
  27.5 4.5 %collective-permute-start.6 = (bf16[256,128]{1,0:T(8,128)(2,1)S(1)}, bf16[256,128]{1,0:T(8,128)(2,1)S(1)}, u32[]{:S(2)}, u32[]{:S(2)}) collective-permute-start(bf16[256,128]{1,0:T(8,128)(2,1)S(1)} %get-tuple-element.75), channel_id=1, source_target_pairs={{0,4},{4,0},{8,12},{12,8},{16,20},{20,16},{24,28},{28,24},{1,5},{5... | collective-permute-start | bytes 196616 | tf_op jit(solution)/shard_map/ppermute | solution.py:604
  32.3 1.5 %collective-permute-start.8 = (bf16[256,256]{1,0:T(8,128)(2,1)S(1)}, bf16[256,256]{1,0:T(8,128)(2,1)S(1)}, u32[]{:S(2)}, u32[]{:S(2)}) collective-permute-start(bf16[256,256]{1,0:T(8,128)(2,1)S(1)} %norm_away.3), channel_id=1, source_target_pairs={{0,1},{1,0},{2,3},{3,2},{4,5},{5,4},{6,7},{7,6},{8,9},{9,8},{10,11... | collective-permute-start | bytes 393224 | tf_op jit(solution)/shard_map/ppermute | solution.py:645
  36.1 25.4 %collective-permute-start.13 = (bf16[128,1024]{1,0:T(8,128)(2,1)S(1)}, bf16[128,1024]{1,0:T(8,128)(2,1)S(1)}, u32[]{:S(2)}, u32[]{:S(2)}) collective-permute-start(bf16[128,1024]{1,0:T(8,128)(2,1)S(1)} %get-tuple-element.81.refs_6_), channel_id=1, source_target_pairs={{0,2},{1,3},{2,0},{3,1},{4,6},{5,7},{6,4},{7,5},{8,10},{9,11},{10,... | collective-permute-start | bytes 786440 | tf_op jit(solution)/shard_map/ppermute | solution.py:668
  38.9 23.4 %collective-permute-start.12 = (bf16[128,1024]{1,0:T(8,128)(2,1)S(1)}, bf16[128,1024]{1,0:T(8,128)(2,1)S(1)}, u32[]{:S(2)}, u32[]{:S(2)}) collective-permute-start(bf16[128,1024]{1,0:T(8,128)(2,1)S(1)} %get-tuple-element.82.refs_6_), channel_id=1, source_target_pairs={{0,2},{1,3},{2,0},{3,1},{4,6},{5,7},{6,4},{7,5},{8,10},{9,11},{10,... | collective-permute-start | bytes 786440 | tf_op jit(solution)/shard_map/ppermute | solution.py:668
  40.5 19.0 %copy-start.1 = (bf16[128,4096]{1,0:T(8,128)(2,1)S(1)}, bf16[128,4096]{1,0:T(8,128)(2,1)}, u32[]{:S(2)}) copy-start(bf16[128,4096]{1,0:T(8,128)(2,1)} %residual_ref.11) | copy-start | bytes 3145732
  40.5 22.7 %collective-permute-start.11 = (bf16[128,768]{1,0:T(8,128)(2,1)S(1)}, bf16[128,768]{1,0:T(8,128)(2,1)S(1)}, u32[]{:S(2)}, u32[]{:S(2)}) collective-permute-start(bf16[128,768]{1,0:T(8,128)(2,1)S(1)} %get-tuple-element.83.refs_6_), channel_id=1, source_target_pairs={{0,2},{1,3},{2,0},{3,1},{4,6},{5,7},{6,4},{7,5},{8,10},{9,11},{10,... | collective-permute-start | bytes 589832 | tf_op jit(solution)/shard_map/ppermute | solution.py:668
  42.1 15.9 %collective-permute-start.15 = (bf16[128,512]{1,0:T(8,128)(2,1)S(1)}, bf16[128,512]{1,0:T(8,128)(2,1)S(1)}, u32[]{:S(2)}, u32[]{:S(2)}) collective-permute-start(bf16[128,512]{1,0:T(8,128)(2,1)S(1)} %get-tuple-element.79.refs_6_), channel_id=1, source_target_pairs={{0,2},{1,3},{2,0},{3,1},{4,6},{5,7},{6,4},{7,5},{8,10},{9,11},{10,... | collective-permute-start | bytes 393224 | tf_op jit(solution)/shard_map/ppermute | solution.py:668
  42.6 18.2 %collective-permute-start.14 = (bf16[128,512]{1,0:T(8,128)(2,1)S(1)}, bf16[128,512]{1,0:T(8,128)(2,1)S(1)}, u32[]{:S(2)}, u32[]{:S(2)}) collective-permute-start(bf16[128,512]{1,0:T(8,128)(2,1)S(1)} %get-tuple-element.80.refs_6_), channel_id=1, source_target_pairs={{0,2},{1,3},{2,0},{3,1},{4,6},{5,7},{6,4},{7,5},{8,10},{9,11},{10,... | collective-permute-start | bytes 393224 | tf_op jit(solution)/shard_map/ppermute | solution.py:668
  57.9 6.0 %collective-permute-start.10 = (bf16[128,256]{1,0:T(8,128)(2,1)S(1)}, bf16[128,256]{1,0:T(8,128)(2,1)S(1)}, u32[]{:S(2)}, u32[]{:S(2)}) collective-permute-start(bf16[128,256]{1,0:T(8,128)(2,1)S(1)} %get-tuple-element.85), channel_id=1, source_target_pairs={{0,2},{1,3},{2,0},{3,1},{4,6},{5,7},{6,4},{7,5},{8,10},{9,11},{10,... | collective-permute-start | bytes 196616 | tf_op jit(solution)/shard_map/ppermute | solution.py:668

commit v5 on v3

--- a/solution.py
+++ b/solution.py
@@ -146,7 +146,7 @@
         out_specs=[VMEM] * (size + 1),
         out_shape=[pay_shape(count, width, BF16)] * (size - 1) + [held(key.shape, BF16)] * 2,
         scratch_shapes=[pltpu.VMEM((heads, rows), F32)] * 3
-        + [pltpu.SemaphoreType.DMA, pltpu.SemaphoreType.DMA((2, 2))],
+        + [pltpu.SemaphoreType.DMA, pltpu.SemaphoreType.DMA((2, 1))],
         compiler_params=PACKED,
         name="early_states",
     )(place, outside(logd), outside(key), outside(value))
@@ -474,11 +474,10 @@
     return total
 
 
-def begin_kernel(size, place_ref, one_ref, two_ref, met_ref, near_ref, far_ref, out_ref):
-    *early, last = order_of(size)
-    terms = [(one_ref, at, away, near_ref) for at, away in enumerate(early)]
-    terms += [(met_ref, at, away, far_ref) for at, away in enumerate(early)]
-    terms += [(two_ref, 0, last, near_ref)]
+def begin_kernel(size, place_ref, home_ref, met_ref, near_ref, far_ref, out_ref):
+    order = order_of(size)
+    terms = [(met_ref, at, away, far_ref) for at, away in enumerate(order[:-1])]
+    terms += [(home_ref, at, away, near_ref) for at, away in enumerate(order)]
     out_ref[...] = summed(size, place_ref, terms, slice(0, out_ref.shape[1]))
 
 
@@ -486,12 +485,12 @@
     rows = met.shape[0]
     return pl.pallas_call(
         functools.partial(begin_kernel, size),
-        in_specs=[SMEM] + [VMEM] * 5,
+        in_specs=[SMEM] + [VMEM] * 4,
         out_specs=VMEM,
         out_shape=held((rows, count), F32),
         compiler_params=PARAMS,
         name="begin",
-    )(place, *map(near, [*home, met, first_weight, second_weight]))
+    )(place, *map(near, [home, met, first_weight, second_weight]))
 
 
 def complete_kernel(block, size, place_ref, begun_ref, two_ref, far_ref, own_ref, away_ref):
@@ -515,11 +514,11 @@
 
 def project_kernel(block, first, tile, size, place_ref, *refs):
     own_ref, away_ref = refs[-2:]
-    terms = []
-    for one_ref, two_ref, weight_ref in ((refs[0], refs[1], refs[4]), (refs[2], refs[3], refs[5])):
-        *early, last = order_of(size)
-        terms += [(one_ref, at, away, weight_ref) for at, away in enumerate(early)]
-        terms += [(two_ref, 0, last, weight_ref)]
+    home_ref, one_ref, two_ref, near_ref, far_ref = refs[:5]
+    order = order_of(size)
+    terms = [(home_ref, at, away, near_ref) for at, away in enumerate(order)]
+    terms += [(one_ref, at, away, far_ref) for at, away in enumerate(order[:-1])]
+    terms += [(two_ref, 0, order[-1], far_ref)]
     for i in range(own_ref.shape[1] // tile):
         here = slice(i * tile, (i + 1) * tile)
         span = slice(first + i * tile, first + (i + 1) * tile)
@@ -529,16 +528,16 @@
 
 
 def project(place, home, other, first_weight, second_weight, hold, block, first, count, tile, size):
-    rows = home[0].shape[0]
+    rows = home.shape[0]
     tile = tile_of(count, tile)
     return pl.pallas_call(
         functools.partial(project_kernel, block, first, tile, size),
-        in_specs=[SMEM] + [VMEM] * 6 + [ANY],
+        in_specs=[SMEM] + [VMEM] * 5 + [ANY],
         out_specs=[VMEM, VMEM],
         out_shape=[held((block, count), F32), held((rows - block, count), BF16)],
         compiler_params=PARAMS,
         name="project",
-    )(place, *map(near, [*home, *other, first_weight, second_weight]), hold)
+    )(place, *map(near, [home, *other, first_weight, second_weight]), hold)
 
 
 def finish_kernel(first, pieces, own_ref, residual_ref, *refs):
@@ -573,7 +572,7 @@
         out_shape=pltpu.HBM((block, total), BF16),
         scratch_shapes=[
             pltpu.VMEM((block, own.shape[1]), BF16),
-            pltpu.SemaphoreType.DMA((tile_of(block // 16, 4),)),
+            pltpu.SemaphoreType.DMA((1,)),
         ],
         input_output_aliases={2 + len(parts): 0} if earlier else {},
         compiler_params=PARAMS,
@@ -629,15 +628,19 @@
         queries.append(decayed)
 
     gain = norm_gain.reshape(heads, width)
-    home, other = [], []
-    for which in (order_of(size)[:-1], order_of(size)[-1:]):
-        args = (
+    order = order_of(size)
+    other = []
+
+    def normed(which, away):
+        return norm(
             tuple(which), (place, chip, core), gain, insides, queries, entering,
-            size, count, width, chips, block,
+            size, count, width, chips, block, away,
         )
-        away = norm(*args, True)
+
+    for which in (order[:-1], order[-1:]):
+        away = normed(which, True)
         other.append(lax.ppermute(away, "exp", cores))
-        home.append(norm(*args, False))
+    home = normed(order, False)
 
     sizes = [tile, tile]
     while total - sum(sizes) > 2 * tile:

time: 63.6 us -> 63.3 us (level)
    pallas_call x4 -> x3, Pallas kernels: 1.56 us -> 1.32 us  [norm(): pl.pallas_call(functools.partial(norm_kernel, size, count, width, chips,...]
  transfers between devices with their start and end apart: 16 -> 16, of which waited for: 8 -> 9; matrix products, arithmetic and copies ran while one was open for 0% -> 0% of each run, Pallas kernels for 19% -> 19%
where the time goes in v5:
time: 63.3 us; the launch traced here: 63.1 us
  waiting for transfers between devices  26.3 us (42%)
  starting transfers between devices  18.3 us (29%)
  Pallas kernels  18.2 us (29%)
    ppermute x6, waiting for transfers between devices, shards(): got.append(lax.ppermute(piece, 'exp', perm))  13.9 us
    ppermute x7, waiting for transfers between devices, swap(): return lax.ppermute(x, 'ctx', [(i, i ^ bit) for i in range(blocks)])  12.3 us
    ppermute x7, starting transfers between devices, swap(): return lax.ppermute(x, 'ctx', [(i, i ^ bit) for i in range(blocks)])  10.3 us
    ppermute x6, starting transfers between devices, shards(): got.append(lax.ppermute(piece, 'exp', perm))  7.29 us
    pallas_call x5, Pallas kernels, project(): pl.pallas_call(functools.partial(project_kernel, block, first, tile, size...  4.72 us
    pallas_call x6, Pallas kernels, finish(): pl.pallas_call(functools.partial(finish_kernel, first, len(parts)), in_sp...  4.49 us
    pallas_call x4, Pallas kernels, local(): pl.pallas_call(functools.partial(local_kernel, size, count, width, away),...  2.91 us
    pallas_call x1, Pallas kernels, early_states(): pl.pallas_call(functools.partial(early_kernel, size, count, width), in_sp...  2.08 us
  transfers between devices with their start and end apart: 16, of which 9 were waited for; matrix products, arithmetic and copies ran while one was open for 0% of the time, Pallas kernels for 19%

profile of v5, /device:TPU:0, one launch (start us, length us, event | category | flops | bytes accessed | tf_op | source)
XLA Modules:
  0.0 63.1 jit_solution(1198415732348350743)
XLA Ops:
  0.0 2.1 %early_states.1 = (bf16[272,128]{1,0:T(8,128)(2,1)S(1)}, bf16[272,128]{1,0:T(8,128)(2,1)S(1)}, bf16[272,128]{1,0:T(8,128)(2,1)S(1)}, bf16[512,1024]{1,0:T(8,128)(2,1)S(1)}, bf16[512,1024]{1,0:T(8,128)(2,1)S(1)}) custom-call(s32[1]{0:T(128)} %bitcast.place_ref, f32[8,512]{1,0:T(8,128)} %bitcast.10, bf16[512,1024]{1,0:T(8,128)(2,1)} %key_in.1, ...), custom_call_target="tpu_custom_call" | custom-call | tf_op jit(solution)/shard_map/early_states/pallas_call | solution.py:143
  2.1 1.6 %load.1 = (f32[272,128]{1,0:T(8,128)S(1)}, bf16[512,1024]{1,0:T(8,128)(2,1)S(1)}, f32[8,512]{1,0:T(8,128)S(1)}) custom-call(s32[1]{0:T(128)} %bitcast.place_ref, f32[8,512]{1,0:T(8,128)} %bitcast.11, bf16[512,1024]{1,0:T(8,128)(2,1)} %query_in.1, bf16[512,1024]{1,0:T(8,128)(2,1)S(1)} %get-tuple-element.50.key_ref.k_ref, ...), custom_call_target="tpu_custom_call" | custom-call | tf_op jit(solution)/shard_map/load/pallas_call | solution.py:175
  3.7 0.6 collective-permute-start.9
  4.2 2.7 %collective-permute-start.1 = (bf16[272,128]{1,0:T(8,128)(2,1)S(1)}, bf16[272,128]{1,0:T(8,128)(2,1)S(1)}, u32[]{:S(2)}, u32[]{:S(2)}) collective-permute-start(bf16[272,128]{1,0:T(8,128)(2,1)S(1)} %get-tuple-element.65), channel_id=1, source_target_pairs={{0,8},{4,12},{8,0},{12,4},{16,24},{20,28},{24,16},{28,20},{1,9},{5... | collective-permute-start | bytes 208904 | tf_op jit(solution)/shard_map/ppermute | solution.py:598
  6.9 1.4 %collective-permute-start.2 = (bf16[272,128]{1,0:T(8,128)(2,1)S(1)}, bf16[272,128]{1,0:T(8,128)(2,1)S(1)}, u32[]{:S(2)}, u32[]{:S(2)}) collective-permute-start(bf16[272,128]{1,0:T(8,128)(2,1)S(1)} %get-tuple-element.66), channel_id=1, source_target_pairs={{0,12},{4,8},{8,4},{12,0},{16,28},{20,24},{24,20},{28,16},{1,13},{... | collective-permute-start | bytes 208904 | tf_op jit(solution)/shard_map/ppermute | solution.py:598
  8.2 0.2 collective-permute-start
  8.4 1.2 %collective-permute-done.1.refs_2_ = bf16[272,128]{1,0:T(8,128)(2,1)S(1)} collective-permute-done((bf16[272,128]{1,0:T(8,128)(2,1)S(1)}, bf16[272,128]{1,0:T(8,128)(2,1)S(1)}, u32[]{:S(2)}, u32[]{:S(2)}) %collective-permute-start.1) | collective-permute-done | bytes 69664 | tf_op jit(solution)/shard_map/ppermute | solution.py:598
  9.7 2.7 %collective-permute-done.2.refs_3_ = bf16[272,128]{1,0:T(8,128)(2,1)S(1)} collective-permute-done((bf16[272,128]{1,0:T(8,128)(2,1)S(1)}, bf16[272,128]{1,0:T(8,128)(2,1)S(1)}, u32[]{:S(2)}, u32[]{:S(2)}) %collective-permute-start.2) | collective-permute-done | bytes 69664 | tf_op jit(solution)/shard_map/ppermute | solution.py:598
  12.3 1.3 %collective-permute-done.refs_1_ = bf16[272,128]{1,0:T(8,128)(2,1)S(1)} collective-permute-done((bf16[272,128]{1,0:T(8,128)(2,1)S(1)}, bf16[272,128]{1,0:T(8,128)(2,1)S(1)}, u32[]{:S(2)}, u32[]{:S(2)}) %collective-permute-start) | collective-permute-done | bytes 69664 | tf_op jit(solution)/shard_map/ppermute | solution.py:598
  13.6 0.1 gather.1
  13.7 2.7 %collective-permute-start.3 = (bf16[272,128]{1,0:T(8,128)(2,1)S(1)}, bf16[272,128]{1,0:T(8,128)(2,1)S(1)}, u32[]{:S(2)}, u32[]{:S(2)}) collective-permute-start(bf16[272,128]{1,0:T(8,128)(2,1)S(1)} %get-tuple-element.67), channel_id=1, source_target_pairs={{0,16},{4,20},{8,24},{12,28},{16,0},{20,4},{24,8},{28,12},{1,17},{... | collective-permute-start | bytes 208904 | tf_op jit(solution)/shard_map/ppermute | solution.py:598
  16.4 3.8 %collective-permute-done.3.got_ref = bf16[272,128]{1,0:T(8,128)(2,1)S(1)} collective-permute-done((bf16[272,128]{1,0:T(8,128)(2,1)S(1)}, bf16[272,128]{1,0:T(8,128)(2,1)S(1)}, u32[]{:S(2)}, u32[]{:S(2)}) %collective-permute-start.3) | collective-permute-done | bytes 69664 | tf_op jit(solution)/shard_map/ppermute | solution.py:598
  20.2 0.1 enter.1
  20.3 0.4 collective-permute-start.4
  20.7 1.8 %collective-permute-start.5 = (bf16[256,128]{1,0:T(8,128)(2,1)S(1)}, bf16[256,128]{1,0:T(8,128)(2,1)S(1)}, u32[]{:S(2)}, u32[]{:S(2)}) collective-permute-start(bf16[256,128]{1,0:T(8,128)(2,1)S(1)} %get-tuple-element.73), channel_id=1, source_target_pairs={{0,8},{4,12},{8,0},{12,4},{16,24},{20,28},{24,16},{28,20},{1,9},{5... | collective-permute-start | bytes 196616 | tf_op jit(solution)/shard_map/ppermute | solution.py:598
  22.4 0.7 %local.6 = (f32[512,256]{1,0:T(8,128)S(1)}, bf16[512,256]{1,0:T(8,128)(2,1)S(1)}) custom-call(s32[1]{0:T(128)} %bitcast.place_ref, f32[8,512]{1,0:T(8,128)S(1)} %get-tuple-element.53.cum_ref, bf16[512,1024]{1,0:T(8,128)(2,1)S(1)} %get-tuple-element.54.q_ref, bf16[512,1024]{1,0:T(8,128)(2,1)S(1)} %get-tuple-element.50.key_ref.k_ref, ...), custom_call_target="tpu_custom_call" | custom-call | tf_op jit(solution)/shard_map/local/pallas_call | solution.py:400
  23.2 0.7 %local.5 = (f32[512,256]{1,0:T(8,128)S(1)}, bf16[512,256]{1,0:T(8,128)(2,1)S(1)}) custom-call(s32[1]{0:T(128)} %bitcast.place_ref, f32[8,512]{1,0:T(8,128)S(1)} %get-tuple-element.53.cum_ref, bf16[512,1024]{1,0:T(8,128)(2,1)S(1)} %get-tuple-element.54.q_ref, bf16[512,1024]{1,0:T(8,128)(2,1)S(1)} %get-tuple-element.50.key_ref.k_ref, ...), custom_call_target="tpu_custom_call" | custom-call | tf_op jit(solution)/shard_map/local/pallas_call | solution.py:400
  23.9 0.7 %local.4 = (f32[512,256]{1,0:T(8,128)S(1)}, bf16[512,256]{1,0:T(8,128)(2,1)S(1)}) custom-call(s32[1]{0:T(128)} %bitcast.place_ref, f32[8,512]{1,0:T(8,128)S(1)} %get-tuple-element.53.cum_ref, bf16[512,1024]{1,0:T(8,128)(2,1)S(1)} %get-tuple-element.54.q_ref, bf16[512,1024]{1,0:T(8,128)(2,1)S(1)} %get-tuple-element.50.key_ref.k_ref, ...), custom_call_target="tpu_custom_call" | custom-call | tf_op jit(solution)/shard_map/local/pallas_call | solution.py:400
  24.7 0.9 %collective-permute-done.4.refs_9_.refs_7_ = bf16[256,128]{1,0:T(8,128)(2,1)S(1)} collective-permute-done((bf16[256,128]{1,0:T(8,128)(2,1)S(1)}, bf16[256,128]{1,0:T(8,128)(2,1)S(1)}, u32[]{:S(2)}, u32[]{:S(2)}) %collective-permute-start.4) | collective-permute-done | bytes 65568 | tf_op jit(solution)/shard_map/ppermute | solution.py:598
  25.5 0.5 norm_away.2
  26.0 0.1 collective-permute-start.7
  26.1 1.3 %collective-permute-start.6 = (bf16[256,128]{1,0:T(8,128)(2,1)S(1)}, bf16[256,128]{1,0:T(8,128)(2,1)S(1)}, u32[]{:S(2)}, u32[]{:S(2)}) collective-permute-start(bf16[256,128]{1,0:T(8,128)(2,1)S(1)} %get-tuple-element.74), channel_id=1, source_target_pairs={{0,4},{4,0},{8,12},{12,8},{16,20},{20,16},{24,28},{28,24},{1,5},{5... | collective-permute-start | bytes 196616 | tf_op jit(solution)/shard_map/ppermute | solution.py:598
  27.4 0.7 %local.7 = (f32[512,256]{1,0:T(8,128)S(1)}, bf16[512,256]{1,0:T(8,128)(2,1)S(1)}) custom-call(s32[1]{0:T(128)} %bitcast.place_ref, f32[8,512]{1,0:T(8,128)S(1)} %get-tuple-element.53.cum_ref, bf16[512,1024]{1,0:T(8,128)(2,1)S(1)} %get-tuple-element.54.q_ref, bf16[512,1024]{1,0:T(8,128)(2,1)S(1)} %get-tuple-element.50.key_ref.k_ref, ...), custom_call_target="tpu_custom_call" | custom-call | tf_op jit(solution)/shard_map/local/pallas_call | solution.py:400
  28.1 2.4 %collective-permute-done.6.refs_11_.refs_2_ = bf16[256,128]{1,0:T(8,128)(2,1)S(1)} collective-permute-done((bf16[256,128]{1,0:T(8,128)(2,1)S(1)}, bf16[256,128]{1,0:T(8,128)(2,1)S(1)}, u32[]{:S(2)}, u32[]{:S(2)}) %collective-permute-start.6) | collective-permute-done | bytes 65568 | tf_op jit(solution)/shard_map/ppermute | solution.py:598
  30.6 0.3 norm_away.3
  31.0 0.5 norm_home.1.home_ref.refs_0_
  31.6 0.7 %begin.1.begun_ref = f32[256,512]{1,0:T(8,128)S(1)} custom-call(s32[1]{0:T(128)} %bitcast.place_ref, bf16[256,1024]{1,0:T(8,128)(2,1)S(1)} %norm_home.1.home_ref.refs_0_, bf16[256,768]{1,0:T(8,128)(2,1)S(1)} %collective-permute-done.7.met_ref.refs_1_, bf16[1024,4096]{1,0:T(8,128)(2,1)S(1)} %bitcast.6, ...), custom_call_target="tpu_custom_call" | custom-call | tf_op jit(solution)/shard_map/begin/pallas_call | solution.py:486
  32.2 0.1 collective-permute-done.8.two_ref.refs_2_
  32.3 0.2 complete.1
  32.6 0.7 %project.5 = (f32[128,512]{1,0:T(8,128)S(1)}, bf16[128,512]{1,0:T(8,128)(2,1)S(1)}) custom-call(s32[1]{0:T(128)} %bitcast.place_ref, bf16[256,1024]{1,0:T(8,128)(2,1)S(1)} %norm_home.1.home_ref.refs_0_, bf16[256,768]{1,0:T(8,128)(2,1)S(1)} %collective-permute-done.7.met_ref.refs_1_, bf16[256,256]{1,0:T(8,128)(2,1)S(1)} %collective-permute-done.8.two_ref.refs_2_, ...), custom_call_target="tpu_custom_call" | custom-call | tf_op jit(solution)/shard_map/project/pallas_call | solution.py:533
  33.3 1.3 %project.6 = (f32[128,1024]{1,0:T(8,128)S(1)}, bf16[128,1024]{1,0:T(8,128)(2,1)S(1)}) custom-call(s32[1]{0:T(128)} %bitcast.place_ref, bf16[256,1024]{1,0:T(8,128)(2,1)S(1)} %norm_home.1.home_ref.refs_0_, bf16[256,768]{1,0:T(8,128)(2,1)S(1)} %collective-permute-done.7.met_ref.refs_1_, bf16[256,256]{1,0:T(8,128)(2,1)S(1)} %collective-permute-done.8.two_ref.refs_2_, ...), custom_call_target="tpu_custom_call" | custom-call | tf_op jit(solution)/shard_map/project/pallas_call | solution.py:533
  34.6 1.6 %collective-permute-start.13 = (bf16[128,1024]{1,0:T(8,128)(2,1)S(1)}, bf16[128,1024]{1,0:T(8,128)(2,1)S(1)}, u32[]{:S(2)}, u32[]{:S(2)}) collective-permute-start(bf16[128,1024]{1,0:T(8,128)(2,1)S(1)} %get-tuple-element.79.refs_5_), channel_id=1, source_target_pairs={{0,2},{1,3},{2,0},{3,1},{4,6},{5,7},{6,4},{7,5},{8,10},{9,11},{10,... | collective-permute-start | bytes 786440 | tf_op jit(solution)/shard_map/ppermute | solution.py:665
  36.1 1.3 %project.7 = (f32[128,1024]{1,0:T(8,128)S(1)}, bf16[128,1024]{1,0:T(8,128)(2,1)S(1)}) custom-call(s32[1]{0:T(128)} %bitcast.place_ref, bf16[256,1024]{1,0:T(8,128)(2,1)S(1)} %norm_home.1.home_ref.refs_0_, bf16[256,768]{1,0:T(8,128)(2,1)S(1)} %collective-permute-done.7.met_ref.refs_1_, bf16[256,256]{1,0:T(8,128)(2,1)S(1)} %collective-permute-done.8.two_ref.refs_2_, ...), custom_call_target="tpu_custom_call" | custom-call | tf_op jit(solution)/shard_map/project/pallas_call | solution.py:533
  37.4 0.6 collective-permute-start.12
  38.0 1.0 %project.8 = (f32[128,768]{1,0:T(8,128)S(1)}, bf16[128,768]{1,0:T(8,128)(2,1)S(1)}) custom-call(s32[1]{0:T(128)} %bitcast.place_ref, bf16[256,1024]{1,0:T(8,128)(2,1)S(1)} %norm_home.1.home_ref.refs_0_, bf16[256,768]{1,0:T(8,128)(2,1)S(1)} %collective-permute-done.7.met_ref.refs_1_, bf16[256,256]{1,0:T(8,128)(2,1)S(1)} %collective-permute-done.8.two_ref.refs_2_, ...), custom_call_target="tpu_custom_call" | custom-call | tf_op jit(solution)/shard_map/project/pallas_call | solution.py:533
  39.0 1.6 %collective-permute-start.11 = (bf16[128,768]{1,0:T(8,128)(2,1)S(1)}, bf16[128,768]{1,0:T(8,128)(2,1)S(1)}, u32[]{:S(2)}, u32[]{:S(2)}) collective-permute-start(bf16[128,768]{1,0:T(8,128)(2,1)S(1)} %get-tuple-element.81.refs_5_), channel_id=1, source_target_pairs={{0,2},{1,3},{2,0},{3,1},{4,6},{5,7},{6,4},{7,5},{8,10},{9,11},{10,... | collective-permute-start | bytes 589832 | tf_op jit(solution)/shard_map/ppermute | solution.py:665
  40.6 0.5 collective-permute-start.15
  41.1 1.5 %collective-permute-start.14 = (bf16[128,512]{1,0:T(8,128)(2,1)S(1)}, bf16[128,512]{1,0:T(8,128)(2,1)S(1)}, u32[]{:S(2)}, u32[]{:S(2)}) collective-permute-start(bf16[128,512]{1,0:T(8,128)(2,1)S(1)} %get-tuple-element.78.refs_5_), channel_id=1, source_target_pairs={{0,2},{1,3},{2,0},{3,1},{4,6},{5,7},{6,4},{7,5},{8,10},{9,11},{10,... | collective-permute-start | bytes 393224 | tf_op jit(solution)/shard_map/ppermute | solution.py:665
  42.6 0.5 project.9
  43.1 13.3 %collective-permute-done.15.refs_0_ = bf16[128,512]{1,0:T(8,128)(2,1)S(1)} collective-permute-done((bf16[128,512]{1,0:T(8,128)(2,1)S(1)}, bf16[128,512]{1,0:T(8,128)(2,1)S(1)}, u32[]{:S(2)}, u32[]{:S(2)}) %collective-permute-start.15) | collective-permute-done | bytes 131104 | tf_op jit(solution)/shard_map/ppermute | solution.py:665
  56.4 1.5 %collective-permute-start.10 = (bf16[128,256]{1,0:T(8,128)(2,1)S(1)}, bf16[128,256]{1,0:T(8,128)(2,1)S(1)}, u32[]{:S(2)}, u32[]{:S(2)}) collective-permute-start(bf16[128,256]{1,0:T(8,128)(2,1)S(1)} %get-tuple-element.83), channel_id=1, source_target_pairs={{0,2},{1,3},{2,0},{3,1},{4,6},{5,7},{6,4},{7,5},{8,10},{9,11},{10,... | collective-permute-start | bytes 196616 | tf_op jit(solution)/shard_map/ppermute | solution.py:665
  58.0 0.7 %finish.6.refs_1_ = bf16[128,4096]{1,0:T(8,128)(2,1)} custom-call(f32[128,512]{1,0:T(8,128)S(1)} %get-tuple-element.88.own_ref, bf16[128,4096]{1,0:T(8,128)(2,1)S(1)} %copy-done, bf16[128,512]{1,0:T(8,128)(2,1)S(1)} %collective-permute-done.15.refs_0_), custom_call_target="tpu_custom_call" | custom-call | tf_op jit(solution)/shard_map/finish/pallas_call | solution.py:568
  58.7 0.6 collective-permute-done.14.refs_0_
  59.2 0.7 %finish.7.refs_1_ = bf16[128,4096]{1,0:T(8,128)(2,1)} custom-call(f32[128,512]{1,0:T(8,128)S(1)} %get-tuple-element.87.own_ref, bf16[128,4096]{1,0:T(8,128)(2,1)S(1)} %copy-done, bf16[128,512]{1,0:T(8,128)(2,1)S(1)} %collective-permute-done.14.refs_0_, bf16[128,4096]{1,0:T(8,128)(2,1)} %finish.6.refs_1_), custom_call_target="tpu_custom_call", output_to_operand_aliasing={{}: (3, {})} | custom-call | tf_op jit(solution)/shard_map/finish/pallas_call | solution.py:568
  60.0 0.8 %finish.8.refs_1_ = bf16[128,4096]{1,0:T(8,128)(2,1)} custom-call(f32[128,1024]{1,0:T(8,128)S(1)} %get-tuple-element.86.own_ref, bf16[128,4096]{1,0:T(8,128)(2,1)S(1)} %copy-done, bf16[128,1024]{1,0:T(8,128)(2,1)S(1)} %collective-permute-done.13.refs_0_, bf16[128,4096]{1,0:T(8,128)(2,1)} %finish.7.refs_1_), custom_call_target="tpu_custom_call", output_to_operand_aliasing={{}: (3, {})} | custom-call | tf_op jit(solution)/shard_map/finish/pallas_call | solution.py:568
  60.8 0.8 %finish.9.refs_1_ = bf16[128,4096]{1,0:T(8,128)(2,1)} custom-call(f32[128,1024]{1,0:T(8,128)S(1)} %get-tuple-element.85.own_ref, bf16[128,4096]{1,0:T(8,128)(2,1)S(1)} %copy-done, bf16[128,1024]{1,0:T(8,128)(2,1)S(1)} %collective-permute-done.12.refs_0_, bf16[128,4096]{1,0:T(8,128)(2,1)} %finish.8.refs_1_), custom_call_target="tpu_custom_call", output_to_operand_aliasing={{}: (3, {})} | custom-call | tf_op jit(solution)/shard_map/finish/pallas_call | solution.py:568
  61.6 0.8 %finish.10.refs_1_ = bf16[128,4096]{1,0:T(8,128)(2,1)} custom-call(f32[128,768]{1,0:T(8,128)S(1)} %get-tuple-element.84.own_ref, bf16[128,4096]{1,0:T(8,128)(2,1)S(1)} %copy-done, bf16[128,768]{1,0:T(8,128)(2,1)S(1)} %collective-permute-done.11.refs_0_, bf16[128,4096]{1,0:T(8,128)(2,1)} %finish.9.refs_1_), custom_call_target="tpu_custom_call", output_to_operand_aliasing={{}: (3, {})} | custom-call | tf_op jit(solution)/shard_map/finish/pallas_call | solution.py:568
  62.4 0.7 %finish.11 = bf16[128,4096]{1,0:T(8,128)(2,1)} custom-call(f32[128,256]{1,0:T(8,128)S(1)} %get-tuple-element.82.own_ref, bf16[128,4096]{1,0:T(8,128)(2,1)S(1)} %copy-done, bf16[128,256]{1,0:T(8,128)(2,1)S(1)} %collective-permute-done.10.refs_0_, bf16[128,4096]{1,0:T(8,128)(2,1)} %finish.10.refs_1_), custom_call_target="tpu_custom_call", output_to_operand_aliasing={{}: (3, {})} | custom-call | tf_op jit(solution)/shard_map/finish/pallas_call | solution.py:568
  (17 shorter events, 0.1 us)
Async XLA Ops:
  0.0 25.5 %copy-start.1 = (f32[1024]{0:T(1024)S(1)}, f32[1024]{0:T(1024)}, u32[]{:S(2)}) copy-start(f32[1024]{0:T(1024)} %param.11) | copy-start | bytes 12292
  3.7 27.9 %collective-permute-start.9 = (bf16[1024,4096]{1,0:T(8,128)(2,1)}, bf16[1024,4096]{1,0:T(8,128)(2,1)S(1)}, u32[]{:S(2)}, u32[]{:S(2)}) collective-permute-start(bf16[1024,4096]{1,0:T(8,128)(2,1)} %refs_3_.4), channel_id=1, source_target_pairs={{0,1},{1,0},{2,3},{3,2},{4,5},{5,4},{6,7},{7,6},{8,9},{9,8},{10,11... | collective-permute-start | bytes 25165832 | tf_op jit(solution)/shard_map/ppermute | solution.py:607
  4.2 5.4 %collective-permute-start.1 = (bf16[272,128]{1,0:T(8,128)(2,1)S(1)}, bf16[272,128]{1,0:T(8,128)(2,1)S(1)}, u32[]{:S(2)}, u32[]{:S(2)}) collective-permute-start(bf16[272,128]{1,0:T(8,128)(2,1)S(1)} %get-tuple-element.65), channel_id=1, source_target_pairs={{0,8},{4,12},{8,0},{12,4},{16,24},{20,28},{24,16},{28,20},{1,9},{5... | collective-permute-start | bytes 208904 | tf_op jit(solution)/shard_map/ppermute | solution.py:598
  6.9 5.4 %collective-permute-start.2 = (bf16[272,128]{1,0:T(8,128)(2,1)S(1)}, bf16[272,128]{1,0:T(8,128)(2,1)S(1)}, u32[]{:S(2)}, u32[]{:S(2)}) collective-permute-start(bf16[272,128]{1,0:T(8,128)(2,1)S(1)} %get-tuple-element.66), channel_id=1, source_target_pairs={{0,12},{4,8},{8,4},{12,0},{16,28},{20,24},{24,20},{28,16},{1,13},{... | collective-permute-start | bytes 208904 | tf_op jit(solution)/shard_map/ppermute | solution.py:598
  8.2 5.4 %collective-permute-start = (bf16[272,128]{1,0:T(8,128)(2,1)S(1)}, bf16[272,128]{1,0:T(8,128)(2,1)S(1)}, u32[]{:S(2)}, u32[]{:S(2)}) collective-permute-start(bf16[272,128]{1,0:T(8,128)(2,1)S(1)} %get-tuple-element.52.hold_ref), channel_id=1, source_target_pairs={{0,4},{4,0},{8,12},{12,8},{16,20},{20,16},{24,28},{28,24},{1,5},{5... | collective-permute-start | bytes 208904 | tf_op jit(solution)/shard_map/ppermute | solution.py:598
  13.7 6.4 %collective-permute-start.3 = (bf16[272,128]{1,0:T(8,128)(2,1)S(1)}, bf16[272,128]{1,0:T(8,128)(2,1)S(1)}, u32[]{:S(2)}, u32[]{:S(2)}) collective-permute-start(bf16[272,128]{1,0:T(8,128)(2,1)S(1)} %get-tuple-element.67), channel_id=1, source_target_pairs={{0,16},{4,20},{8,24},{12,28},{16,0},{20,4},{24,8},{28,12},{1,17},{... | collective-permute-start | bytes 208904 | tf_op jit(solution)/shard_map/ppermute | solution.py:598
  20.3 5.2 %collective-permute-start.4 = (bf16[256,128]{1,0:T(8,128)(2,1)S(1)}, bf16[256,128]{1,0:T(8,128)(2,1)S(1)}, u32[]{:S(2)}, u32[]{:S(2)}) collective-permute-start(bf16[256,128]{1,0:T(8,128)(2,1)S(1)} %get-tuple-element.72), channel_id=1, source_target_pairs={{0,12},{4,8},{8,4},{12,0},{16,28},{20,24},{24,20},{28,16},{1,13},{... | collective-permute-start | bytes 196616 | tf_op jit(solution)/shard_map/ppermute | solution.py:598
  20.7 4.9 %collective-permute-start.5 = (bf16[256,128]{1,0:T(8,128)(2,1)S(1)}, bf16[256,128]{1,0:T(8,128)(2,1)S(1)}, u32[]{:S(2)}, u32[]{:S(2)}) collective-permute-start(bf16[256,128]{1,0:T(8,128)(2,1)S(1)} %get-tuple-element.73), channel_id=1, source_target_pairs={{0,8},{4,12},{8,0},{12,4},{16,24},{20,28},{24,16},{28,20},{1,9},{5... | collective-permute-start | bytes 196616 | tf_op jit(solution)/shard_map/ppermute | solution.py:598
  23.2 8.4 %slice-start = ((s8[8388608]{0:T(1024)(128)(4,1)}), s8[4194304]{0:T(1024)(128)(4,1)S(1)}, s32[]{:S(2)}) async-start(s8[8388608]{0:T(1024)(128)(4,1)} %bitcast.5), calls=%async_computation | async-start | bytes 8388608
  25.5 6.0 %slice-start.1 = ((s8[8388608]{0:T(1024)(128)(4,1)}), s8[4194304]{0:T(1024)(128)(4,1)S(1)}, s32[]{:S(2)}) async-start(s8[8388608]{0:T(1024)(128)(4,1)} %bitcast.5), calls=%async_computation.1 | async-start | bytes 8388608
  26.0 5.5 %collective-permute-start.7 = (bf16[256,768]{1,0:T(8,128)(2,1)S(1)}, bf16[256,768]{1,0:T(8,128)(2,1)S(1)}, u32[]{:S(2)}, u32[]{:S(2)}) collective-permute-start(bf16[256,768]{1,0:T(8,128)(2,1)S(1)} %norm_away.2), channel_id=1, source_target_pairs={{0,1},{1,0},{2,3},{3,2},{4,5},{5,4},{6,7},{7,6},{8,9},{9,8},{10,11... | collective-permute-start | bytes 1179656 | tf_op jit(solution)/shard_map/ppermute | solution.py:642
  26.1 4.5 %collective-permute-start.6 = (bf16[256,128]{1,0:T(8,128)(2,1)S(1)}, bf16[256,128]{1,0:T(8,128)(2,1)S(1)}, u32[]{:S(2)}, u32[]{:S(2)}) collective-permute-start(bf16[256,128]{1,0:T(8,128)(2,1)S(1)} %get-tuple-element.74), channel_id=1, source_target_pairs={{0,4},{4,0},{8,12},{12,8},{16,20},{20,16},{24,28},{28,24},{1,5},{5... | collective-permute-start | bytes 196616 | tf_op jit(solution)/shard_map/ppermute | solution.py:598
  30.9 1.4 %collective-permute-start.8 = (bf16[256,256]{1,0:T(8,128)(2,1)S(1)}, bf16[256,256]{1,0:T(8,128)(2,1)S(1)}, u32[]{:S(2)}, u32[]{:S(2)}) collective-permute-start(bf16[256,256]{1,0:T(8,128)(2,1)S(1)} %norm_away.3), channel_id=1, source_target_pairs={{0,1},{1,0},{2,3},{3,2},{4,5},{5,4},{6,7},{7,6},{8,9},{9,8},{10,11... | collective-permute-start | bytes 393224 | tf_op jit(solution)/shard_map/ppermute | solution.py:642
  34.6 25.4 %collective-permute-start.13 = (bf16[128,1024]{1,0:T(8,128)(2,1)S(1)}, bf16[128,1024]{1,0:T(8,128)(2,1)S(1)}, u32[]{:S(2)}, u32[]{:S(2)}) collective-permute-start(bf16[128,1024]{1,0:T(8,128)(2,1)S(1)} %get-tuple-element.79.refs_5_), channel_id=1, source_target_pairs={{0,2},{1,3},{2,0},{3,1},{4,6},{5,7},{6,4},{7,5},{8,10},{9,11},{10,... | collective-permute-start | bytes 786440 | tf_op jit(solution)/shard_map/ppermute | solution.py:665
  37.4 23.4 %collective-permute-start.12 = (bf16[128,1024]{1,0:T(8,128)(2,1)S(1)}, bf16[128,1024]{1,0:T(8,128)(2,1)S(1)}, u32[]{:S(2)}, u32[]{:S(2)}) collective-permute-start(bf16[128,1024]{1,0:T(8,128)(2,1)S(1)} %get-tuple-element.80.refs_5_), channel_id=1, source_target_pairs={{0,2},{1,3},{2,0},{3,1},{4,6},{5,7},{6,4},{7,5},{8,10},{9,11},{10,... | collective-permute-start | bytes 786440 | tf_op jit(solution)/shard_map/ppermute | solution.py:665
  39.0 19.0 %copy-start = (bf16[128,4096]{1,0:T(8,128)(2,1)S(1)}, bf16[128,4096]{1,0:T(8,128)(2,1)}, u32[]{:S(2)}) copy-start(bf16[128,4096]{1,0:T(8,128)(2,1)} %residual_ref.11) | copy-start | bytes 3145732
  39.0 22.6 %collective-permute-start.11 = (bf16[128,768]{1,0:T(8,128)(2,1)S(1)}, bf16[128,768]{1,0:T(8,128)(2,1)S(1)}, u32[]{:S(2)}, u32[]{:S(2)}) collective-permute-start(bf16[128,768]{1,0:T(8,128)(2,1)S(1)} %get-tuple-element.81.refs_5_), channel_id=1, source_target_pairs={{0,2},{1,3},{2,0},{3,1},{4,6},{5,7},{6,4},{7,5},{8,10},{9,11},{10,... | collective-permute-start | bytes 589832 | tf_op jit(solution)/shard_map/ppermute | solution.py:665
  40.6 15.8 %collective-permute-start.15 = (bf16[128,512]{1,0:T(8,128)(2,1)S(1)}, bf16[128,512]{1,0:T(8,128)(2,1)S(1)}, u32[]{:S(2)}, u32[]{:S(2)}) collective-permute-start(bf16[128,512]{1,0:T(8,128)(2,1)S(1)} %get-tuple-element.77.refs_5_), channel_id=1, source_target_pairs={{0,2},{1,3},{2,0},{3,1},{4,6},{5,7},{6,4},{7,5},{8,10},{9,11},{10,... | collective-permute-start | bytes 393224 | tf_op jit(solution)/shard_map/ppermute | solution.py:665
  41.1 18.1 %collective-permute-start.14 = (bf16[128,512]{1,0:T(8,128)(2,1)S(1)}, bf16[128,512]{1,0:T(8,128)(2,1)S(1)}, u32[]{:S(2)}, u32[]{:S(2)}) collective-permute-start(bf16[128,512]{1,0:T(8,128)(2,1)S(1)} %get-tuple-element.78.refs_5_), channel_id=1, source_target_pairs={{0,2},{1,3},{2,0},{3,1},{4,6},{5,7},{6,4},{7,5},{8,10},{9,11},{10,... | collective-permute-start | bytes 393224 | tf_op jit(solution)/shard_map/ppermute | solution.py:665
  56.4 6.0 %collective-permute-start.10 = (bf16[128,256]{1,0:T(8,128)(2,1)S(1)}, bf16[128,256]{1,0:T(8,128)(2,1)S(1)}, u32[]{:S(2)}, u32[]{:S(2)}) collective-permute-start(bf16[128,256]{1,0:T(8,128)(2,1)S(1)} %get-tuple-element.83), channel_id=1, source_target_pairs={{0,2},{1,3},{2,0},{3,1},{4,6},{5,7},{6,4},{7,5},{8,10},{9,11},{10,... | collective-permute-start | bytes 196616 | tf_op jit(solution)/shard_map/ppermute | solution.py:665
